TPU v7x, 512 devices: a whole 4x4x16 slice. The times are simulated.
512 devices in a mesh: grp: 8 (over y, core), tile: 64 (over x, z).
Axes of the slice: x: 4, y: 4, z: 16, core: 2. Of those that a mesh axis runs over, the one named last changes fastest.
Arguments:
- level_set: float32 [2560, 40960], P('grp', 'tile'), may hold values from -8 to 8
- fuel: int32 [2560, 40960], P('grp', 'tile'), may hold values from 0 to 12
- wind: float32 [2, 128, 2048], P(None, 'grp', 'tile'), may hold values from -6 to 6
- owner: int32 [8, 64], P('grp'), may hold values from 0 to 63, each once within a row
- active: int32 [4, 8, 64], P(None, 'grp', 'tile'), may hold values 0 or 1
- fuel_rate: float32 [13], replicated, may hold values from 0.05 to 0.3
- fuel_wind: float32 [13], replicated, may hold values from 0.01 to 0.05
- fuel_heat: float32 [13], replicated, may hold values from 0.5 to 4
Outputs:
- level_out: float32 [2560, 40960], P('grp', 'tile')
- wind_out: float32 [2, 128, 2048], P(None, 'grp', 'tile')
Inputs may be any that keep to these rules, and one draw needn't show every extreme that they name: Each row of owner is a permutation of the 64 tiles of a group.
All inputs are finite; a program needn't handle non-finite values. No bound on the sum of `active` on one device may be relied on, other than what follows from the above.
Results may differ from a plain program's by a relative error of at most 0.0003.
Values sent between devices are 32-bit elements; how exact they have to be, the bound alone decides.
No kernel may reach another device: no remote copies, remote signals or barrier semaphores. Data moves between devices by JAX's collectives and lax.ppermute only.
A program may use at most 64 MiB of HBM per device.

v0:
```python
import jax
import jax.numpy as jnp
from jax import lax
from jax.sharding import PartitionSpec as P

STEPS = 2
SUBSTEPS = 2


def extended(shard, sides, width):
    for axis, dim in sides:
        size, length = (lax.axis_size(axis), shard.shape[dim])
        up = [(i, (i + 1) % size) for i in range(size - 1)]
        down = [(j, i) for i, j in up]
        last = lax.slice_in_dim(shard, length - width, length, axis=dim)
        first = lax.slice_in_dim(shard, 0, width, axis=dim)
        before = lax.ppermute(last, axis, up)
        after = lax.ppermute(first, axis, down)
        shard = jnp.concatenate([before, shard, after], axis=dim)
    return shard


def lookup(fuel, table):
    total = jnp.zeros(fuel.shape, jnp.float32)
    for category in range(table.shape[0]):
        total = total + jnp.where(fuel == category, table[category], jnp.float32(0.0))
    return total


def burnt(level):
    return 0.5 * (1.0 - jnp.tanh(level))


def expander(fine_count, coarse_count):
    fine_index = lax.broadcasted_iota(jnp.int32, (fine_count, coarse_count), 0)
    coarse_index = lax.broadcasted_iota(jnp.int32, (fine_count, coarse_count), 1)
    refine = fine_count // coarse_count
    return (fine_index // refine == coarse_index).astype(jnp.float32)


def product(left, right):
    return jnp.dot(left, right, preferred_element_type=jnp.float32, precision=lax.Precision.HIGHEST)


def neighbours(level):
    padded = extended(level, (("grp", 0), ("tile", 1)), 1)
    first_row = lax.axis_index("grp") == 0
    last_row = lax.axis_index("grp") == lax.axis_size("grp") - 1
    first_col = lax.axis_index("tile") == 0
    last_col = lax.axis_index("tile") == lax.axis_size("tile") - 1
    top_edge = jnp.where(first_row, level[0], padded[0, 1:-1])
    bottom_edge = jnp.where(last_row, level[-1], padded[-1, 1:-1])
    left_edge = jnp.where(first_col, level[:, 0], padded[1:-1, 0])
    right_edge = jnp.where(last_col, level[:, -1], padded[1:-1, -1])
    south = jnp.concatenate([top_edge[None, :], level[:-1]], axis=0)
    north_cell = jnp.concatenate([level[1:], bottom_edge[None, :]], axis=0)
    west = jnp.concatenate([left_edge[:, None], level[:, :-1]], axis=1)
    east_cell = jnp.concatenate([level[:, 1:], right_edge[:, None]], axis=1)
    return (south, north_cell, west, east_cell)


def wind_update(block, owned):
    padq = jnp.pad(owned, 1, mode="edge")
    grad_x = (padq[1:-1, 2:] - padq[1:-1, :-2]) * 0.5
    grad_y = (padq[2:, 1:-1] - padq[:-2, 1:-1]) * 0.5
    return jnp.stack([0.9 * block[0] + 40.0 * grad_x, 0.9 * block[1] + 40.0 * grad_y])


def shards(level_set, fuel, wind, owner, active, fuel_rate, fuel_wind, fuel_heat):
    cell_rows, cell_cols = level_set.shape
    atm_rows, atm_cols = (wind.shape[1], wind.shape[2])
    rows_expand = expander(cell_rows, atm_rows)
    cols_expand = expander(cell_cols, atm_cols).T
    rate = lookup(fuel, fuel_rate)
    drift = lookup(fuel, fuel_wind)
    heat = lookup(fuel, fuel_heat)
    owner_row = owner[0]
    myself = lax.axis_index("tile")
    tiles = lax.axis_size("tile")
    slots = jnp.arange(tiles, dtype=jnp.int32)
    readers_of_mine = (owner_row == myself).astype(jnp.float32)
    my_owner = (slots == owner_row[myself]).astype(jnp.float32)
    level = level_set
    counter = 0
    held = wind
    for atmos_step in range(STEPS):
        flat_wind = held.reshape(2 * atm_rows * atm_cols)
        read_everyone = lax.all_gather(flat_wind[None, :], "tile", axis=0, tiled=True)
        got = jnp.sum(my_owner[:, None] * read_everyone, axis=0)
        read_wind = got.reshape(2, atm_rows, atm_cols)
        east = product(product(rows_expand, read_wind[0]), cols_expand)
        north = product(product(rows_expand, read_wind[1]), cols_expand)
        fine_flux = jnp.zeros(level.shape, jnp.float32)
        for substep in range(SUBSTEPS):
            south, north_cell, west, east_cell = neighbours(level)
            back_x = level - west
            ahead_x = east_cell - level
            back_y = level - south
            ahead_y = north_cell - level
            slope = jnp.sqrt(
                jnp.maximum(back_x, 0.0) ** 2
                + jnp.minimum(ahead_x, 0.0) ** 2
                + jnp.maximum(back_y, 0.0) ** 2
                + jnp.minimum(ahead_y, 0.0) ** 2
                + 1e-12
            )
            carry = (
                jnp.maximum(east, 0.0) * back_x
                + jnp.minimum(east, 0.0) * ahead_x
                + jnp.maximum(north, 0.0) * back_y
                + jnp.minimum(north, 0.0) * ahead_y
            )
            candidate = level - rate * slope - drift * carry
            newer = jnp.where(active[counter, 0, 0] > 0, candidate, level)
            fine_flux = fine_flux + heat * (burnt(newer) - burnt(level))
            level = newer
            counter += 1
        refine = cell_rows // atm_rows
        coarse = product(product(rows_expand.T, fine_flux), cols_expand.T) / float(refine * refine)
        flat_flux = coarse.reshape(atm_rows * atm_cols)
        everyone = lax.all_gather(flat_flux[None, :], "tile", axis=0, tiled=True)
        owned = jnp.sum(readers_of_mine[:, None] * everyone, axis=0)
        held = wind_update(held, owned.reshape(atm_rows, atm_cols))
    return (level, held)


def solution(mesh):
    in_specs = (
        P("grp", "tile"),
        P("grp", "tile"),
        P(None, "grp", "tile"),
        P("grp", None),
        P(None, "grp", "tile"),
        P(),
        P(),
        P(),
    )
    out_specs = (P("grp", "tile"), P(None, "grp", "tile"))
    return jax.shard_map(shards, mesh=mesh, in_specs=in_specs, out_specs=out_specs, check_vma=False)
```

profile of v0, /device:TPU:16, one launch (start us, length us, event | category | flops | bytes accessed | tf_op | source)
XLA Modules:
  0.0 505.4 jit_solution(1527925878186152022)
XLA Ops:
  0.6 0.8 fusion.110
  1.4 1.9 collective-permute-start
  3.3 3.6 collective-permute-start.1
  7.0 2.9 fusion.109
  10.0 1.3 fusion.111
  12.6 0.7 fusion.118
  13.3 0.7 fusion.117
  14.0 0.7 fusion.119
  14.7 88.7 %all-gather = f32[64,1,1024]{2,1,0:T(1,128)S(1)} all-gather(f32[1,1,1024]{2,1,0:T(1,128)S(1)} %reshape.88), channel_id=1, replica_groups=mesh['grp'=8,'tile'=64] {'tile'}, dimensions={0}, use_global_device_ids=true | all-gather | bytes 266240 | tf_op jit(solution)/shard_map/all_gather | solution.py:88
  103.6 1.0 fusion.46
  105.0 0.7 fusion.29
  105.8 11.5 %select_add_fusion = (f32[320,640]{1,0:T(8,128)S(1)}, pred[320,640]{1,0:T(32,128)(4,1)S(1)}, pred[320,640]{1,0:T(32,128)(4,1)}, pred[320,640]{1,0:T(32,128)(4,1)...) fusion(f32[]{:T(128)} %bitcast.45, f32[]{:T(128)} %bitcast.44, ...), kind=kLoop, calls=%fused_computation.43 | loop fusion | flops 7782400 | bytes 4300852 | tf_op jit(solution)/shard_map/add | solution.py:26
  120.8 3.1 collective-permute-start.2
  123.9 1.3 collective-permute-start.3
  125.2 1.5 collective-permute-done.2
  126.7 4.4 collective-permute-done.3
  131.3 23.2 %subtract_select_fusion.3 = (f32[320,640]{1,0:T(8,128)S(1)}, f32[320,640]{1,0:T(8,128)S(1)}, f32[320,640]{1,0:T(8,128)S(1)}, f32[320,640]{1,0:T(8,128)S(1)}) fusion(f32[320,640]{1,0:T(8,128)S(1)} %copy-done, f32[1,640]{1,0:T(1,128)S(1)} %get-tuple-element.62, f32[319,640]{1,0:T(8,128)} %get-tuple-element.66, f32[319,640]{1,0:T(8,128)} %get-tuple-element.65, ...), kind=kOutput, calls=%fused_computation.45 | convolution fusion | flops 96296960 | bytes 10901225 | tf_op jit(solution)/shard_map/dot_general | solution.py:42
  154.6 1.9 collective-permute-start.4
  156.5 3.6 collective-permute-start.5
  160.5 1.0 collective-permute-done.5
  161.6 1.9 collective-permute-start.6
  163.5 1.5 collective-permute-start.7
  165.0 2.9 collective-permute-done.6
  167.9 4.6 collective-permute-done.7
  172.6 1.2 subtract_select_fusion.2
  173.8 0.9 fusion.3
  175.3 102.7 %all-gather.1 = f32[64,1,512]{2,1,0:T(1,128)S(1)} all-gather(f32[1,1,512]{2,1,0:T(1,128)S(1)} %reshape.90), channel_id=1, replica_groups=mesh['grp'=8,'tile'=64] {'tile'}, dimensions={0}, use_global_device_ids=true | all-gather | bytes 133120 | tf_op jit(solution)/shard_map/all_gather | solution.py:121
  278.2 1.4 fusion.103
  279.6 1.3 fusion.105
  280.9 1.9 collective-permute-start.8
  282.8 3.6 collective-permute-start.9
  286.7 79.1 %all-gather.2 = f32[64,1,1024]{2,1,0:T(1,128)S(1)} all-gather(f32[1,1,1024]{2,1,0:T(1,128)S(1)} %reshape.92), channel_id=1, replica_groups=mesh['grp'=8,'tile'=64] {'tile'}, dimensions={0}, use_global_device_ids=true | all-gather | bytes 266240 | tf_op jit(solution)/shard_map/all_gather | solution.py:88
  366.5 0.7 fusion.27
  367.8 3.6 collective-permute-start.10
  371.4 1.3 collective-permute-start.11
  372.7 1.5 collective-permute-done.10
  374.3 4.4 collective-permute-done.11
  378.8 2.9 subtract_select_fusion.1
  381.8 1.9 collective-permute-start.12
  383.8 3.6 collective-permute-start.13
  387.7 1.0 collective-permute-done.13
  388.8 1.9 collective-permute-start.14
  390.8 1.3 collective-permute-start.15
  392.1 2.2 collective-permute-done.14
  394.3 4.1 collective-permute-done.15
  398.5 1.2 subtract_select_fusion
  399.8 0.9 fusion
  401.2 103.1 %all-gather.3 = f32[64,1,512]{2,1,0:T(1,128)S(1)} all-gather(f32[1,1,512]{2,1,0:T(1,128)S(1)} %reshape.94), channel_id=1, replica_groups=mesh['grp'=8,'tile'=64] {'tile'}, dimensions={0}, use_global_device_ids=true | all-gather | bytes 133120 | tf_op jit(solution)/shard_map/all_gather | solution.py:121
  (107 shorter events, 8.1 us)
Async XLA Ops:
  1.4 119.2 %collective-permute-start = (f32[1,640]{1,0:T(1,128)S(1)}, f32[1,640]{1,0:T(1,128)S(1)}, u32[]{:S(2)}, u32[]{:S(2)}) collective-permute-start(f32[1,640]{1,0:T(1,128)S(1)} %get-tuple-element.63), channel_id=1, source_target_pairs={{0,64},{64,128},{128,192},{192,256},{256,320},{320,384},{384,448},... | collective-permute-start | bytes 7688 | tf_op jit(solution)/shard_map/ppermute | solution.py:17
  3.3 117.3 %collective-permute-start.1 = (f32[1,640]{1,0:T(1,128)S(1)}, f32[1,640]{1,0:T(1,128)S(1)}, u32[]{:S(2)}, u32[]{:S(2)}) collective-permute-start(f32[1,640]{1,0:T(1,128)S(1)} %get-tuple-element.64), channel_id=1, source_target_pairs={{64,0},{128,64},{192,128},{256,192},{320,256},{384,320},{448,384},... | collective-permute-start | bytes 7688 | tf_op jit(solution)/shard_map/ppermute | solution.py:18
  7.0 2.9 copy-start
  10.0 1.3 copy-start.20
  10.0 2.7 copy-start.16
  10.0 3.3 copy-start.17
  10.0 4.0 copy-start.18
  11.3 1.3 copy-start.15
  103.4 2.4 copy-start.11
  105.8 25.4 %copy-start.3 = (f32[320,640]{1,0:T(8,128)}, f32[320,640]{1,0:T(8,128)S(1)}, u32[]{:S(2)}) copy-start(f32[320,640]{1,0:T(8,128)S(1)} %fusion.29) | copy-start | bytes 2457604
  105.8 11.5 %copy-start.19 = (s32[4,1,1]{0,2,1:T(1,128)S(1)}, s32[4,1,1]{0,2,1:T(1,128)}, u32[]{:S(2)}) copy-start(s32[4,1,1]{0,2,1:T(1,128)} %param.12) | copy-start | bytes 52
  120.6 10.6 %copy-start.7 = (f32[320,639]{1,0:T(8,128)S(1)}, f32[320,639]{1,0:T(8,128)}, u32[]{:S(2)}) copy-start(f32[320,639]{1,0:T(8,128)} %get-tuple-element.60) | copy-start | bytes 2453764
  120.6 10.6 %copy-start.13 = (pred[320,640]{1,0:T(32,128)(4,1)S(1)}, pred[320,640]{1,0:T(32,128)(4,1)}, u32[]{:S(2)}) copy-start(pred[320,640]{1,0:T(32,128)(4,1)} %get-tuple-element.5) | copy-start | bytes 614404
  120.6 10.6 %copy-start.14 = (pred[320,640]{1,0:T(32,128)(4,1)S(1)}, pred[320,640]{1,0:T(32,128)(4,1)}, u32[]{:S(2)}) copy-start(pred[320,640]{1,0:T(32,128)(4,1)} %get-tuple-element.6) | copy-start | bytes 614404
  120.8 10.5 %copy-start.6 = (f32[320,639]{1,0:T(8,128)S(1)}, f32[320,639]{1,0:T(8,128)}, u32[]{:S(2)}) copy-start(f32[320,639]{1,0:T(8,128)} %get-tuple-element.59) | copy-start | bytes 2453764
  120.8 5.9 %collective-permute-start.2 = (f32[322,1]{1,0:T(8,128)S(1)}, f32[322,1]{1,0:T(8,128)S(1)}, u32[]{:S(2)}, u32[]{:S(2)}) collective-permute-start(f32[322,1]{1,0:T(8,128)S(1)} %get-tuple-element.25), channel_id=1, source_target_pairs={{0,1},{1,2},{2,3},{3,4},{4,5},{5,6},{6,7},{7,8},{8,9},{9,10},{10,1... | collective-permute-start | bytes 3872 | tf_op jit(solution)/shard_map/ppermute | solution.py:17
  123.9 7.3 %collective-permute-start.3 = (f32[322,1]{1,0:T(8,128)S(1)}, f32[322,1]{1,0:T(8,128)S(1)}, u32[]{:S(2)}, u32[]{:S(2)}) collective-permute-start(f32[322,1]{1,0:T(8,128)S(1)} %get-tuple-element.26), channel_id=1, source_target_pairs={{1,0},{2,1},{3,2},{4,3},{5,4},{6,5},{7,6},{8,7},{9,8},{10,9},{11,1... | collective-permute-start | bytes 3872 | tf_op jit(solution)/shard_map/ppermute | solution.py:18
  125.2 6.1 %copy-start.12 = (pred[320,640]{1,0:T(32,128)(4,1)S(1)}, pred[320,640]{1,0:T(32,128)(4,1)}, u32[]{:S(2)}) copy-start(pred[320,640]{1,0:T(32,128)(4,1)} %get-tuple-element.4) | copy-start | bytes 614404
  154.5 18.1 %copy-start.1 = (f32[320,640]{1,0:T(8,128)}, f32[320,640]{1,0:T(8,128)S(1)}, u32[]{:S(2)}) copy-start(f32[320,640]{1,0:T(8,128)S(1)} %get-tuple-element.18) | copy-start | bytes 2457604
  154.6 5.9 %collective-permute-start.4 = (f32[1,640]{1,0:T(1,128)S(1)}, f32[1,640]{1,0:T(1,128)S(1)}, u32[]{:S(2)}, u32[]{:S(2)}) collective-permute-start(f32[1,640]{1,0:T(1,128)S(1)} %get-tuple-element.53), channel_id=1, source_target_pairs={{0,64},{64,128},{128,192},{192,256},{256,320},{320,384},{384,448},... | collective-permute-start | bytes 7688 | tf_op jit(solution)/shard_map/ppermute | solution.py:17
  156.5 4.9 collective-permute-start.5
  160.5 12.1 %copy-start.4 = (f32[320,640]{1,0:T(8,128)S(1)}, f32[320,640]{1,0:T(8,128)}, u32[]{:S(2)}) copy-start(f32[320,640]{1,0:T(8,128)} %copy-done.3) | copy-start | bytes 2457604
  161.6 6.3 %collective-permute-start.6 = (f32[322,1]{1,0:T(8,128)S(1)}, f32[322,1]{1,0:T(8,128)S(1)}, u32[]{:S(2)}, u32[]{:S(2)}) collective-permute-start(f32[322,1]{1,0:T(8,128)S(1)} %get-tuple-element.23), channel_id=1, source_target_pairs={{0,1},{1,2},{2,3},{3,4},{4,5},{5,6},{6,7},{7,8},{8,9},{9,10},{10,1... | collective-permute-start | bytes 3872 | tf_op jit(solution)/shard_map/ppermute | solution.py:17
  163.5 8.9 %collective-permute-start.7 = (f32[322,1]{1,0:T(8,128)S(1)}, f32[322,1]{1,0:T(8,128)S(1)}, u32[]{:S(2)}, u32[]{:S(2)}) collective-permute-start(f32[322,1]{1,0:T(8,128)S(1)} %get-tuple-element.24), channel_id=1, source_target_pairs={{1,0},{2,1},{3,2},{4,3},{5,4},{6,5},{7,6},{8,7},{9,8},{10,9},{11,1... | collective-permute-start | bytes 3872 | tf_op jit(solution)/shard_map/ppermute | solution.py:18
  280.9 86.7 %collective-permute-start.8 = (f32[1,640]{1,0:T(1,128)S(1)}, f32[1,640]{1,0:T(1,128)S(1)}, u32[]{:S(2)}, u32[]{:S(2)}) collective-permute-start(f32[1,640]{1,0:T(1,128)S(1)} %get-tuple-element.43), channel_id=1, source_target_pairs={{0,64},{64,128},{128,192},{192,256},{256,320},{320,384},{384,448},... | collective-permute-start | bytes 7688 | tf_op jit(solution)/shard_map/ppermute | solution.py:17
  282.8 84.8 %collective-permute-start.9 = (f32[1,640]{1,0:T(1,128)S(1)}, f32[1,640]{1,0:T(1,128)S(1)}, u32[]{:S(2)}, u32[]{:S(2)}) collective-permute-start(f32[1,640]{1,0:T(1,128)S(1)} %get-tuple-element.44), channel_id=1, source_target_pairs={{64,0},{128,64},{192,128},{256,192},{320,256},{384,320},{448,384},... | collective-permute-start | bytes 7688 | tf_op jit(solution)/shard_map/ppermute | solution.py:18
  366.5 12.3 %copy-start.9 = (f32[320,639]{1,0:T(8,128)S(1)}, f32[320,639]{1,0:T(8,128)}, u32[]{:S(2)}) copy-start(f32[320,639]{1,0:T(8,128)} %get-tuple-element.40) | copy-start | bytes 2453764
  366.5 12.3 %copy-start.10 = (f32[319,640]{1,0:T(8,128)S(1)}, f32[319,640]{1,0:T(8,128)}, u32[]{:S(2)}) copy-start(f32[319,640]{1,0:T(8,128)} %get-tuple-element.45) | copy-start | bytes 2449924
  367.6 11.2 %copy-start.2 = (f32[320,640]{1,0:T(8,128)S(1)}, f32[320,640]{1,0:T(8,128)}, u32[]{:S(2)}) copy-start(f32[320,640]{1,0:T(8,128)} %copy-done.1) | copy-start | bytes 2457604
  367.6 11.2 %copy-start.8 = (f32[320,639]{1,0:T(8,128)S(1)}, f32[320,639]{1,0:T(8,128)}, u32[]{:S(2)}) copy-start(f32[320,639]{1,0:T(8,128)} %get-tuple-element.39) | copy-start | bytes 2453764
  367.8 6.5 %collective-permute-start.10 = (f32[322,1]{1,0:T(8,128)S(1)}, f32[322,1]{1,0:T(8,128)S(1)}, u32[]{:S(2)}, u32[]{:S(2)}) collective-permute-start(f32[322,1]{1,0:T(8,128)S(1)} %get-tuple-element.21), channel_id=1, source_target_pairs={{0,1},{1,2},{2,3},{3,4},{4,5},{5,6},{6,7},{7,8},{8,9},{9,10},{10,1... | collective-permute-start | bytes 3872 | tf_op jit(solution)/shard_map/ppermute | solution.py:17
  371.4 7.3 %collective-permute-start.11 = (f32[322,1]{1,0:T(8,128)S(1)}, f32[322,1]{1,0:T(8,128)S(1)}, u32[]{:S(2)}, u32[]{:S(2)}) collective-permute-start(f32[322,1]{1,0:T(8,128)S(1)} %get-tuple-element.22), channel_id=1, source_target_pairs={{1,0},{2,1},{3,2},{4,3},{5,4},{6,5},{7,6},{8,7},{9,8},{10,9},{11,1... | collective-permute-start | bytes 3872 | tf_op jit(solution)/shard_map/ppermute | solution.py:18
  381.8 5.9 %collective-permute-start.12 = (f32[1,640]{1,0:T(1,128)S(1)}, f32[1,640]{1,0:T(1,128)S(1)}, u32[]{:S(2)}, u32[]{:S(2)}) collective-permute-start(f32[1,640]{1,0:T(1,128)S(1)} %get-tuple-element.33), channel_id=1, source_target_pairs={{0,64},{64,128},{128,192},{192,256},{256,320},{320,384},{384,448},... | collective-permute-start | bytes 7688 | tf_op jit(solution)/shard_map/ppermute | solution.py:17
  383.8 4.9 collective-permute-start.13
  388.8 5.5 %collective-permute-start.14 = (f32[322,1]{1,0:T(8,128)S(1)}, f32[322,1]{1,0:T(8,128)S(1)}, u32[]{:S(2)}, u32[]{:S(2)}) collective-permute-start(f32[322,1]{1,0:T(8,128)S(1)} %get-tuple-element.19), channel_id=1, source_target_pairs={{0,1},{1,2},{2,3},{3,4},{4,5},{5,6},{6,7},{7,8},{8,9},{9,10},{10,1... | collective-permute-start | bytes 3872 | tf_op jit(solution)/shard_map/ppermute | solution.py:17
  390.8 7.7 %collective-permute-start.15 = (f32[322,1]{1,0:T(8,128)S(1)}, f32[322,1]{1,0:T(8,128)S(1)}, u32[]{:S(2)}, u32[]{:S(2)}) collective-permute-start(f32[322,1]{1,0:T(8,128)S(1)} %get-tuple-element.20), channel_id=1, source_target_pairs={{1,0},{2,1},{3,2},{4,3},{5,4},{6,5},{7,6},{8,7},{9,8},{10,9},{11,1... | collective-permute-start | bytes 3872 | tf_op jit(solution)/shard_map/ppermute | solution.py:18
  399.7 0.9 copy-start.5
where the time goes:
time: 507 us; the launch traced here: 505 us
  blocking collectives  374 us (74%)
  starting transfers between devices  38.1 us (8%)
  matrix products  32.4 us (6%)
  waiting for transfers between devices  27.7 us (5%)
  other arithmetic  16.8 us (3%)
  local copies, waits for them, and re-layouts  12.9 us (3%)
    all_gather x2, blocking collectives, shards(): everyone = lax.all_gather(flat_flux[None, :], 'tile', axis=0, tiled=True)  206 us
    all_gather x2, blocking collectives, shards(): lax.all_gather(flat_wind[None, :], 'tile', axis=0, tiled=True)  168 us
    dot_general x12, matrix products, product(): jnp.dot(left, right, preferred_element_type=jnp.float32, precision=lax.Pr...  32.4 us
    ppermute x8, starting transfers between devices, extended(): after = lax.ppermute(first, axis, down)  19.9 us
    ppermute x8, waiting for transfers between devices, extended(): after = lax.ppermute(first, axis, down)  19.5 us
    ppermute x8, starting transfers between devices, extended(): before = lax.ppermute(last, axis, up)  18.2 us
    add x1, other arithmetic, lookup(): total + jnp.where(fuel == category, table[category], jnp.float32(0.0))  11.5 us
  transfers between devices with their start and end apart: 16, of which 10 were waited for; matrix products, arithmetic and copies ran while one was open for 5% of the time, Pallas kernels for 0%

commit v1 on v0

v1 whole, which is shorter than its diff:
```python
import jax
import jax.numpy as jnp
from jax import lax
from jax.experimental import pallas as pl
from jax.experimental.pallas import tpu as pltpu
from jax.sharding import PartitionSpec as P

R = 20
AY = 16
AX = 32
FY = 320
FX = 640
STEPS = 2
SUBSTEPS = 2
NZ = 16
NX = 4
HALO = 48
HALF = 64
PAD = 8
TOP = PAD + HALO
ROWS = TOP + FY + HALO + PAD
COLS = FX + 2 * HALF
NL = COLS // 128
RIGHT = 40
LEFT = 51
CR = 24

VM = pl.BlockSpec(memory_space=pltpu.VMEM)
SM = pl.BlockSpec(memory_space=pltpu.SMEM)
PARAMS = pltpu.CompilerParams(vmem_limit_bytes=40 * 1024 * 1024)


def lanes(shape):
    return lax.broadcasted_iota(jnp.int32, shape, 1)


def f32(*shape):
    return jax.ShapeDtypeStruct(shape, jnp.float32)


def thirds(x):
    high = x.astype(jnp.bfloat16)
    rest = x - high.astype(jnp.float32)
    middle = rest.astype(jnp.bfloat16)
    low = (rest - middle.astype(jnp.float32)).astype(jnp.bfloat16)
    return jnp.concatenate([high, middle, low], axis=0)


def exact_dot(x, onehot):
    n = x.shape[0]
    out = jnp.dot(thirds(x), onehot, preferred_element_type=jnp.float32)
    return out[:n] + out[n : 2 * n] + out[2 * n :]


def coarse_lane(fine):
    own = fine // R
    right = RIGHT + (fine - FX) // R
    left = LEFT - (COLS - 1 - fine) // R
    edge = jnp.where(fine < FX + 3 * R, right, jnp.where(fine >= COLS - 3 * R, left, -1))
    return jnp.where(fine < FX, own, edge)


def pack_kernel(level0, level4, fuel0, fuel4, wind, active, to_left, to_right, slots):
    lane = lanes((FY, 128))
    fuel_first = pltpu.roll(fuel0[...].astype(jnp.float32), HALF, 1)
    fuel_last = pltpu.roll(fuel4[...].astype(jnp.float32), HALF, 1)
    to_left[0:FY, :] = jnp.where(lane < HALF, level0[...], fuel_first)
    to_right[0:FY, :] = jnp.where(lane >= HALF, level4[...], fuel_last)
    for k in range(8):
        flag = (active[min(k, 3), 0, 0] > 0).astype(jnp.float32)
        row = jnp.full((1, 128), flag, jnp.float32)
        to_left[FY + k : FY + k + 1, :] = row
        to_right[FY + k : FY + k + 1, :] = row
    parts = [wind[0, 0:8, :], wind[0, 8:16, :], wind[1, 0:8, :], wind[1, 8:16, :]]
    block = jnp.concatenate(parts, axis=1)
    for k in range(NX):
        slots[k] = block


def pack(level, fuel, wind, active):
    edge0 = pl.BlockSpec((FY, 128), lambda i: (0, 0))
    edge4 = pl.BlockSpec((FY, 128), lambda i: (0, FX // 128 - 1))
    whole = lambda *s: pl.BlockSpec(s, lambda i: (0,) * len(s))
    return pl.pallas_call(
        pack_kernel,
        grid=(1,),
        in_specs=[edge0, edge4, edge0, edge4, whole(2, AY, AX), SM],
        out_specs=[whole(FY + 8, 128), whole(FY + 8, 128), whole(NX, 8, 128)],
        out_shape=[f32(FY + 8, 128), f32(FY + 8, 128), f32(NX, 8, 128)],
        name="pack",
    )(level, level, fuel, fuel, wind, active)


def route_kernel(owner, blocks, slots):
    tile = lax.axis_index("tile")
    first = (tile // NZ) * NZ
    inside = lanes((8, 128)) % AX
    for k in range(NZ):
        reader = first + k
        main = blocks[owner[0, reader] // NZ]
        left = blocks[owner[0, jnp.maximum(reader - 1, 0)] // NZ]
        right = blocks[owner[0, jnp.minimum(reader + 1, NX * NZ - 1)] // NZ]
        edges = jnp.where(inside >= AX - 3, left, jnp.where(inside < 3, right, 0.0))
        edges = pltpu.roll(edges, 3, 1)
        small = edges[0:2]
        for b in range(1, 4):
            small = small + pltpu.roll(edges[2 * b : 2 * b + 2], 8 * b, 1)
        for b in range(4):
            slots[5 * k + b] = main[2 * b : 2 * b + 2]
        slots[5 * k + 4] = small


def route(owner, blocks):
    return pl.pallas_call(
        route_kernel, in_specs=[SM, VM], out_specs=VM, out_shape=f32(5 * NZ, 2, 128), name="route"
    )(owner, blocks)


def rows_kernel(level_top, level_bottom, fuel_top, fuel_bottom, from_left, from_right, active, to_up, to_down):
    lane = lanes((HALO, 128))
    for out, level, fuel, start, cut in (
        (to_up, level_top, fuel_top, 0, 0),
        (to_down, level_bottom, fuel_bottom, FY - HALO, 80 - HALO),
    ):
        out[0:HALO, 0:FX] = level[cut : cut + HALO, :]
        out[HALO : 2 * HALO, 0:FX] = fuel[cut : cut + HALO, :].astype(jnp.float32)
        one = from_left[start : start + HALO, :]
        two = from_right[start : start + HALO, :]
        out[0:HALO, FX:COLS] = jnp.where(lane < HALF, two, one)
        out[HALO : 2 * HALO, FX:COLS] = pltpu.roll(jnp.where(lane < HALF, one, two), HALF, 1)
        for k in range(8):
            flag = (active[min(k, 3), 0, 0] > 0).astype(jnp.float32)
            out[2 * HALO + k : 2 * HALO + k + 1, 0:FX] = jnp.full((1, FX), flag, jnp.float32)
        out[2 * HALO : 2 * HALO + 8, FX:COLS] = jnp.where(
            lane[0:8] < HALF, from_right[FY : FY + 8, :], from_left[FY : FY + 8, :]
        )


def rows(level, fuel, from_left, from_right, active):
    top = pl.BlockSpec((80, FX), lambda i: (0, 0))
    bottom = pl.BlockSpec((80, FX), lambda i: (FY // 80 - 1, 0))
    whole = lambda *s: pl.BlockSpec(s, lambda i: (0,) * len(s))
    shape = (2 * HALO + 8, COLS)
    return pl.pallas_call(
        rows_kernel,
        grid=(1,),
        in_specs=[top, bottom, top, bottom, whole(FY + 8, 128), whole(FY + 8, 128), SM],
        out_specs=[whole(*shape), whole(*shape)],
        out_shape=[f32(*shape), f32(*shape)],
        name="rows",
    )(level, level, fuel, fuel, from_left, from_right, active)


def readers_kernel(owner, received, held, to_up, to_down):
    tile = lax.axis_index("tile")
    lane = lanes((8, 128))
    main_at = 5 * (owner[0, tile] % NZ)
    left_at = 5 * (owner[0, jnp.maximum(tile - 1, 0)] % NZ) + 4
    right_at = 5 * (owner[0, jnp.minimum(tile + 1, NX * NZ - 1)] % NZ) + 4
    main = jnp.concatenate([received[main_at + b] for b in range(4)], axis=0)
    left = received[left_at]
    right = received[right_at]
    left = jnp.concatenate([pltpu.roll(left, (128 - 8 * b) % 128, 1) for b in range(4)], axis=0)
    right = jnp.concatenate([pltpu.roll(right, (128 - 8 * b) % 128, 1) for b in range(4)], axis=0)
    for q in range(4):
        own = pltpu.roll(main, (128 - 32 * q) % 128, 1)
        one = pltpu.roll(left, (LEFT - 2 - 32 * (q + 1)) % 128, 1)
        two = pltpu.roll(right, (RIGHT - 3 - 32 * q) % 128, 1)
        is_left = jnp.logical_and(lane >= LEFT - 2, lane <= LEFT)
        is_right = jnp.logical_and(lane >= RIGHT, lane <= RIGHT + 2)
        held[8 * q : 8 * q + 8, :] = jnp.where(
            lane < AX, own, jnp.where(is_left, one, jnp.where(is_right, two, 0.0))
        )
    for out, start in ((to_up, 0), (to_down, AY - 3)):
        out[0:3, :] = held[start : start + 3, :]
        out[3:6, :] = held[AY + start : AY + start + 3, :]
        out[6:8, :] = jnp.zeros((2, 128), jnp.float32)


def readers(owner, received):
    return pl.pallas_call(
        readers_kernel,
        in_specs=[SM, VM],
        out_specs=[VM, VM, VM],
        out_shape=[f32(2 * AY, 128), f32(8, 128), f32(8, 128)],
        name="readers",
    )(owner, received)


def slab_kernel(
    level, fuel, from_left, from_right, from_up, from_down, held, wind_up, wind_down,
    active, fuel_rate, fuel_wind, fuel_heat,
    level_out, slots,
    phi_a, phi_b, phi_c, rate, drift, heat, east, north, winds, gates, sums, spread, gather,
):
    group = lax.axis_index("grp")
    tile = lax.axis_index("tile")
    first_row = group == 0
    last_row = group == lax.axis_size("grp") - 1
    first_col = tile == 0
    last_col = tile == lax.axis_size("tile") - 1
    lane8 = lanes((8, 128))
    sub8 = lax.broadcasted_iota(jnp.int32, (8, COLS), 0)

    def table(values):
        row = jnp.zeros((8, 128), jnp.float32)
        for c in range(values.shape[0]):
            row = jnp.where(lane8 == c, values[c], row)
        return row

    tables = [(table(fuel_rate), rate), (table(fuel_wind), drift), (table(fuel_heat), heat)]

    def look(kinds, at, col):
        for row, out in tables:
            out[pl.ds(at, 8), col : col + 128] = jnp.take_along_axis(
                row, kinds, axis=1, mode="promise_in_bounds"
            )

    zero = jnp.zeros((PAD, COLS), jnp.float32)
    for buf in (phi_a, phi_b, phi_c, rate, drift, heat):
        buf[0:PAD, :] = zero
        buf[ROWS - PAD : ROWS, :] = zero
    phi_a[TOP - HALO : TOP, :] = from_up[0:HALO, :]
    phi_a[TOP + FY : TOP + FY + HALO, :] = from_down[0:HALO, :]

    def own_rows(i, _):
        at = pl.multiple_of(i * 8, 8)
        to = pl.multiple_of(i * 8 + TOP, 8)
        phi_a[pl.ds(to, 8), 0:FX] = level[pl.ds(at, 8), :]
        one = from_left[pl.ds(at, 8), :]
        two = from_right[pl.ds(at, 8), :]
        phi_a[pl.ds(to, 8), FX:COLS] = jnp.where(lane8 < HALF, two, one)
        beside = pltpu.roll(jnp.where(lane8 < HALF, one, two), HALF, 1).astype(jnp.int32)
        for c in range(FX // 128):
            look(fuel[pl.ds(at, 8), 128 * c : 128 * c + 128], to, 128 * c)
        look(beside, to, FX)
        return 0

    lax.fori_loop(0, FY // 8, own_rows, 0)

    def halo_rows(i, _):
        at = pl.multiple_of(i * 8 + HALO, 8)
        for source, start in ((from_up, TOP - HALO), (from_down, TOP + FY)):
            to = pl.multiple_of(i * 8 + start, 8)
            for c in range(NL):
                look(source[pl.ds(at, 8), 128 * c : 128 * c + 128].astype(jnp.int32), to, 128 * c)
        return 0

    lax.fori_loop(0, HALO // 8, halo_rows, 0)

    gates[0:8, :] = from_up[2 * HALO : 2 * HALO + 8, :]
    gates[16:24, :] = from_down[2 * HALO : 2 * HALO + 8, :]
    for k in range(STEPS * SUBSTEPS):
        flag = (active[k, 0, 0] > 0).astype(jnp.float32)
        gates[8 + k : 9 + k, 0:FX] = jnp.full((1, FX), flag, jnp.float32)
    gates[8:16, FX:COLS] = jnp.where(
        lane8 < HALF, from_right[FY : FY + 8, :], from_left[FY : FY + 8, :]
    )

    for comp in range(2):
        base = comp * CR
        winds[base : base + 3, :] = wind_up[3 * comp : 3 * comp + 3, :]
        winds[base + 3 : base + 3 + AY, :] = held[AY * comp : AY * comp + AY, :]
        winds[base + 3 + AY : base + 6 + AY, :] = wind_down[3 * comp : 3 * comp + 3, :]
        winds[base + 6 + AY : base + CR, :] = jnp.zeros((CR - 6 - AY, 128), jnp.float32)

    spread[...] = (
        coarse_lane(lanes((128, COLS))) == lax.broadcasted_iota(jnp.int32, (128, COLS), 0)
    ).astype(jnp.bfloat16)
    gather[...] = (
        coarse_lane(lax.broadcasted_iota(jnp.int32, (COLS, 128), 0)) == lanes((COLS, 128))
    ).astype(jnp.bfloat16)

    def expand():
        wide = exact_dot(winds[...], spread[...])
        east[...] = wide[0:CR]
        north[...] = wide[CR : 2 * CR]

    def edges(phi):
        @pl.when(first_row)
        def _():
            phi[TOP - 1 : TOP, :] = phi[TOP : TOP + 1, :]

        @pl.when(last_row)
        def _():
            phi[TOP + FY : TOP + FY + 1, :] = phi[TOP + FY - 1 : TOP + FY, :]

        @pl.when(first_col)
        def _():
            old = phi[:, COLS - 128 : COLS]
            new = jnp.broadcast_to(phi[:, 0:1], (ROWS, 128))
            phi[:, COLS - 128 : COLS] = jnp.where(lanes((ROWS, 128)) == 127, new, old)

        @pl.when(last_col)
        def _():
            old = phi[:, FX : FX + 128]
            new = jnp.broadcast_to(phi[:, FX - 1 : FX], (ROWS, 128))
            phi[:, FX : FX + 128] = jnp.where(lanes((ROWS, 128)) == 0, new, old)

    def update(phi, at, e, n, gate):
        before = phi[pl.ds(pl.multiple_of(at - 8, 8), 8), :]
        now = phi[pl.ds(at, 8), :]
        after = phi[pl.ds(pl.multiple_of(at + 8, 8), 8), :]
        south = jnp.where(sub8 == 0, pltpu.roll(before, 1, 0), pltpu.roll(now, 1, 0))
        above = jnp.where(sub8 == 7, pltpu.roll(after, 7, 0), pltpu.roll(now, 7, 0))
        west = pltpu.roll(now, 1, 1)
        east_cell = pltpu.roll(now, COLS - 1, 1)
        back_x = now - west
        ahead_x = east_cell - now
        back_y = now - south
        ahead_y = above - now
        bx = jnp.maximum(back_x, 0.0)
        ax = jnp.minimum(ahead_x, 0.0)
        by = jnp.maximum(back_y, 0.0)
        ay = jnp.minimum(ahead_y, 0.0)
        slope = jnp.sqrt(bx * bx + ax * ax + by * by + ay * ay + 1e-12)
        carry = e[0] * back_x + e[1] * ahead_x + n[0] * back_y + n[1] * ahead_y
        change = rate[pl.ds(at, 8), :] * slope + drift[pl.ds(at, 8), :] * carry
        return now - gate * change

    def signed(row):
        return (jnp.maximum(row, 0.0), jnp.minimum(row, 0.0))

    def wind_row(ref, row):
        return jnp.broadcast_to(ref[pl.ds(row, 1), :], (8, COLS))

    def band(phi, m, k, which, finish):
        at = pl.multiple_of(2 * PAD + 40 * m, 8)
        region = (m > 0).astype(jnp.int32) + (m > 8).astype(jnp.int32)
        gate = jnp.broadcast_to(gates[pl.ds(region * 8 + k, 1), :], (8, COLS))
        row = 2 * m + 1
        low = (wind_row(east, row), wind_row(north, row))
        high = (wind_row(east, row + 1), wind_row(north, row + 1))
        mixed = tuple(jnp.where(sub8 < 4, a, b) for a, b in zip(low, high))
        for t in which:
            e, n = (low, low, mixed, high, high)[t]
            here = pl.multiple_of(at + 8 * t, 8)
            finish(t, here, update(phi, here, signed(e), signed(n), gate))

    def tile_rows(phi, at, row, region, k):
        gate = jnp.broadcast_to(gates[region * 8 + k : region * 8 + k + 1, :], (8, COLS))
        return update(phi, at, signed(wind_row(east, row)), signed(wind_row(north, row)), gate)

    def store_to(out):
        def finish(t, here, new):
            out[pl.ds(here, 8), :] = new

        return finish

    def flux_bands(before, phi, out, k, first, last):
        def body(m, _):
            parts = []

            def finish(t, here, new):
                if out is not None:
                    out[pl.ds(here, 8), :] = new
                else:
                    level_out[pl.ds(pl.multiple_of(here - TOP, 8), 8), :] = new[:, 0:FX]
                old = before[pl.ds(here, 8), :]
                parts.append(heat[pl.ds(here, 8), :] * (jnp.tanh(old) - jnp.tanh(new)))

            band(phi, m, k, range(5), finish)
            low = parts[0] + parts[1] + jnp.where(sub8 < 4, parts[2], 0.0)
            high = parts[3] + parts[4] + jnp.where(sub8 >= 4, parts[2], 0.0)
            sums[pl.ds(2 * m + 1, 1), :] = jnp.sum(low, axis=0, keepdims=True)
            sums[pl.ds(2 * m + 2, 1), :] = jnp.sum(high, axis=0, keepdims=True)
            return 0

        lax.fori_loop(first, last, body, 0)

    def pooled():
        return exact_dot(sums[...], gather[...]) * (0.5 / (R * R))

    lane_c = lanes((CR, 128))
    row_c = lax.broadcasted_iota(jnp.int32, (CR, 128), 0)
    sums[...] = jnp.zeros((CR, COLS), jnp.float32)

    expand()
    edges(phi_a)
    phi_b[PAD : PAD + 8, :] = tile_rows(phi_a, PAD, 0, 0, 0)
    phi_b[ROWS - 2 * PAD : ROWS - PAD, :] = tile_rows(phi_a, ROWS - 2 * PAD, AY + 5, 2, 0)

    def first_substep(m, _):
        band(phi_a, m, 0, range(5), store_to(phi_b))
        return 0

    lax.fori_loop(0, 10, first_substep, 0)
    edges(phi_b)
    flux_bands(phi_a, phi_b, phi_c, 1, 0, 10)
    edges(phi_c)

    flux0 = pooled()
    ahead = jnp.where(jnp.logical_or(lane_c == AX - 1, lane_c == LEFT), flux0, pltpu.roll(flux0, 127, 1))
    back = jnp.where(jnp.logical_or(lane_c == 0, lane_c == RIGHT), flux0, pltpu.roll(flux0, 1, 1))
    last_rows = jnp.logical_or(row_c == 2, row_c == AY + 2)
    first_rows = jnp.logical_or(row_c == 3, row_c == AY + 3)
    below = jnp.where(last_rows, flux0, pltpu.roll(flux0, CR - 1, 0))
    upper = jnp.where(first_rows, flux0, pltpu.roll(flux0, 1, 0))
    winds[0:CR, :] = 0.9 * winds[0:CR, :] + 20.0 * (ahead - back)
    winds[CR : 2 * CR, :] = 0.9 * winds[CR : 2 * CR, :] + 20.0 * (below - upper)
    expand()

    top = TOP - 8
    bottom = TOP + FY
    phi_b[top : top + 8, :] = tile_rows(phi_c, top, 2, 0, 2)
    phi_b[bottom : bottom + 8, :] = tile_rows(phi_c, bottom, AY + 3, 2, 2)

    def third_substep(m, _):
        band(phi_c, m, 2, range(5), store_to(phi_b))
        return 0

    lax.fori_loop(1, 9, third_substep, 0)
    edges(phi_b)
    flux_bands(phi_c, phi_b, None, 3, 1, 9)
    total = 0.9 * flux0 + pooled()

    packed = jnp.zeros((4, 128), jnp.float32)
    lane4 = lanes((4, 128))
    for q in range(4):
        moved = pltpu.roll(total, 32 * q, 1)[3 + 4 * q : 7 + 4 * q]
        packed = jnp.where(lane4 // AX == q, moved, packed)
    for k in range(NX * NZ):
        slots[k] = packed


def slab(*args):
    big = pltpu.VMEM((ROWS, COLS), jnp.float32)
    return pl.pallas_call(
        slab_kernel,
        in_specs=[VM] * 9 + [SM] * 4,
        out_specs=[VM, VM],
        out_shape=[f32(FY, FX), f32(NX * NZ, 4, 128)],
        scratch_shapes=[big] * 6
        + [
            pltpu.VMEM((CR, COLS), jnp.float32),
            pltpu.VMEM((CR, COLS), jnp.float32),
            pltpu.VMEM((2 * CR, 128), jnp.float32),
            pltpu.VMEM((CR, COLS), jnp.float32),
            pltpu.VMEM((CR, COLS), jnp.float32),
            pltpu.VMEM((128, COLS), jnp.bfloat16),
            pltpu.VMEM((COLS, 128), jnp.bfloat16),
        ],
        compiler_params=PARAMS,
        name="slab",
    )(*args)


def final_kernel(owner, received, wind, wind_out):
    tile = lax.axis_index("tile")
    source = jnp.int32(0)
    for t in range(NX * NZ):
        source = jnp.where(owner[0, t] == tile, t, source)
    block = received[source]
    flux = jnp.concatenate([pltpu.roll(block, (128 - 32 * q) % 128, 1) for q in range(4)], axis=0)
    lane = lanes((AY, 128))
    row = lax.broadcasted_iota(jnp.int32, (AY, 128), 0)
    ahead = jnp.where(lane == AX - 1, flux, pltpu.roll(flux, 127, 1))
    back = jnp.where(lane == 0, flux, pltpu.roll(flux, 1, 1))
    below = jnp.where(row == AY - 1, flux, pltpu.roll(flux, AY - 1, 0))
    upper = jnp.where(row == 0, flux, pltpu.roll(flux, 1, 0))
    wind_out[0] = 0.81 * wind[0] + 20.0 * (ahead - back)[:, 0:AX]
    wind_out[1] = 0.81 * wind[1] + 20.0 * (below - upper)[:, 0:AX]


def final(owner, received, wind):
    return pl.pallas_call(
        final_kernel, in_specs=[SM, VM, VM], out_specs=VM, out_shape=f32(2, AY, AX), name="final"
    )(owner, received, wind)


def shift(value, axis, step):
    size = lax.axis_size(axis)
    pairs = [(i, i + step) for i in range(size) if 0 <= i + step < size]
    return lax.ppermute(value, axis, pairs)


def shards(level, fuel, wind, owner, active, fuel_rate, fuel_wind, fuel_heat):
    along_x = [[x * NZ + z for x in range(NX)] for z in range(NZ)]
    along_z = [[x * NZ + z for z in range(NZ)] for x in range(NX)]
    to_left, to_right, blocks = pack(level, fuel, wind, active)
    from_right = shift(to_left, "tile", -1)
    from_left = shift(to_right, "tile", 1)
    blocks = lax.all_to_all(blocks, "tile", 0, 0, tiled=True, axis_index_groups=along_x)
    slots = route(owner, blocks)
    to_up, to_down = rows(level, fuel, from_left, from_right, active)
    from_down = shift(to_up, "grp", -1)
    from_up = shift(to_down, "grp", 1)
    received = lax.all_to_all(slots, "tile", 0, 0, tiled=True, axis_index_groups=along_z)
    held, wind_to_up, wind_to_down = readers(owner, received)
    wind_down = shift(wind_to_up, "grp", -1)
    wind_up = shift(wind_to_down, "grp", 1)
    level_out, flux = slab(
        level, fuel, from_left, from_right, from_up, from_down, held, wind_up, wind_down,
        active, fuel_rate, fuel_wind, fuel_heat,
    )
    flux = lax.all_to_all(flux, "tile", 0, 0, tiled=True)
    return (level_out, final(owner, flux, wind))


def solution(mesh):
    in_specs = (
        P("grp", "tile"),
        P("grp", "tile"),
        P(None, "grp", "tile"),
        P("grp", None),
        P(None, "grp", "tile"),
        P(),
        P(),
        P(),
    )
    out_specs = (P("grp", "tile"), P(None, "grp", "tile"))
    return jax.shard_map(shards, mesh=mesh, in_specs=in_specs, out_specs=out_specs, check_vma=False)
```

time: 507 us -> 111 us (0.22)
  the two profiles are of different devices: /device:TPU:16 before, /device:TPU:1 now
where the time goes in v1:
time: 111 us; the launch traced here: 110 us
  blocking collectives  42.2 us (38%)
  starting transfers between devices  31.4 us (28%)
  Pallas kernels  28.7 us (26%)
  local copies, waits for them, and re-layouts  4.01 us (4%)
  waiting for transfers between devices  3.21 us (3%)
    all_to_all x1, blocking collectives, shards(): flux = lax.all_to_all(flux, 'tile', 0, 0, tiled=True)  21.4 us
    all_to_all x1, blocking collectives, shards(): lax.all_to_all(slots, 'tile', 0, 0, tiled=True, axis_index_groups=along_z)  20.8 us
    ppermute x6, starting transfers between devices, shift(): return lax.ppermute(value, axis, pairs)  19.2 us
    pallas_call x1, Pallas kernels, slab(): pl.pallas_call(slab_kernel, in_specs=[VM] * 9 + [SM] * 4, out_specs=[VM,...  19.2 us
    all_to_all x1, starting transfers between devices, shards(): lax.all_to_all(blocks, 'tile', 0, 0, tiled=True, axis_index_groups=along_x)  12.2 us
    unnamed x25, local copies, waits for them, and re-layouts  4.01 us
    ppermute x6, waiting for transfers between devices, shift(): return lax.ppermute(value, axis, pairs)  3.21 us
    pallas_call x1, Pallas kernels, rows(): pl.pallas_call(rows_kernel, grid=(1,), in_specs=[top, bottom, top, bottom...  2.35 us
  transfers between devices with their start and end apart: 7, of which 1 were waited for; matrix products, arithmetic and copies ran while one was open for 0% of the time, Pallas kernels for 5%

profile of v1, /device:TPU:1, one launch (start us, length us, event | category | flops | bytes accessed | tf_op | source)
XLA Modules:
  0.0 110.4 jit_solution(12245620185810135721)
XLA Ops:
  0.6 1.3 %copy.10.active = s32[4,1,1]{2,1,0:T(1,128)} copy(s32[4,1,1]{0,2,1:T(1,128)} %param.12) | data formatting | bytes 32 | tf_op args[4]
  2.0 2.0 %pack.1 = (f32[328,128]{1,0:T(8,128)}, f32[328,128]{1,0:T(8,128)}, f32[4,8,128]{2,1,0:T(8,128)}) custom-call(f32[320,640]{1,0:T(8,128)} %level.1, f32[320,640]{1,0:T(8,128)} %level.1, s32[320,640]{1,0:T(8,128)} %fuel.1, s32[320,640]{1,0:T(8,128)} %fuel.1, f32[2,16,32]{2,1,0:T(8,128)} %wind.3, s32[4,1,1]{2,1,0:T(1,128)} %copy.10.active), custom_call_target="tpu_custom_call" | custom-call | tf_op jit(solution)/shard_map/pack/pallas_call | solution.py:84
  4.0 4.4 %collective-permute-start = (f32[328,128]{1,0:T(8,128)}, f32[328,128]{1,0:T(8,128)S(1)}, u32[]{:S(2)}, u32[]{:S(2)}) collective-permute-start(f32[328,128]{1,0:T(8,128)} %get-tuple-element.12), channel_id=1, source_target_pairs={{0,1},{1,2},{2,3},{3,4},{4,5},{5,6},{6,7},{7,8},{8,9},{9,10},{10,1... | collective-permute-start | bytes 503816 | tf_op jit(solution)/shard_map/ppermute | solution.py:474
  8.3 1.3 %collective-permute-start.1 = (f32[328,128]{1,0:T(8,128)}, f32[328,128]{1,0:T(8,128)S(1)}, u32[]{:S(2)}, u32[]{:S(2)}) collective-permute-start(f32[328,128]{1,0:T(8,128)} %get-tuple-element.13), channel_id=1, source_target_pairs={{1,0},{2,1},{3,2},{4,3},{5,4},{6,5},{7,6},{8,7},{9,8},{10,9},{11,1... | collective-permute-start | bytes 503816 | tf_op jit(solution)/shard_map/ppermute | solution.py:474
  9.6 12.2 %all-to-all-start = ((f32[4,8,128]{2,1,0:T(8,128)}), f32[4,8,128]{2,1,0:T(8,128)S(1)}, u32[]{:S(2)}, u32[]{:S(2)}) async-start(f32[4,8,128]{2,1,0:T(8,128)} %get-tuple-element.16), calls=%async_computation | async-start | bytes 32768 | tf_op jit(solution)/shard_map/all_to_all | solution.py:483
  21.9 0.0 collective-permute-done.from_left
  21.9 0.0 copy-start.2
  21.9 0.0 collective-permute-done.1.from_right
  21.9 0.7 copy-done.2
  22.5 0.0 copy-start.4
  22.5 0.7 copy-done.4
  23.2 0.0 copy-start
  23.2 0.0 copy-start.1
  23.2 2.4 %rows.1 = (f32[104,768]{1,0:T(8,128)}, f32[104,768]{1,0:T(8,128)}) custom-call(f32[320,640]{1,0:T(8,128)} %level.1, f32[320,640]{1,0:T(8,128)} %level.1, s32[320,640]{1,0:T(8,128)} %fuel.1, s32[320,640]{1,0:T(8,128)} %fuel.1, f32[328,128]{1,0:T(8,128)} %copy-done.2, f32[328,128]{1,0:T(8,128)} %copy-done.4, s32[4,1,1]{2,1,0:T(1,128)} %copy.10.active), custom_call_target="tpu_custom_call" | custom-call | tf_op jit(solution)/shard_map/rows/pallas_call | solution.py:144
  25.6 4.3 %collective-permute-start.2 = (f32[104,768]{1,0:T(8,128)}, f32[104,768]{1,0:T(8,128)S(1)}, u32[]{:S(2)}, u32[]{:S(2)}) collective-permute-start(f32[104,768]{1,0:T(8,128)} %get-tuple-element.14), channel_id=1, source_target_pairs={{0,64},{64,128},{128,192},{192,256},{256,320},{320,384},{384,448},... | collective-permute-start | bytes 958472 | tf_op jit(solution)/shard_map/ppermute | solution.py:474
  29.9 0.0 copy-start.3
  29.9 0.0 copy-start.5
  29.9 2.1 %collective-permute-start.3 = (f32[104,768]{1,0:T(8,128)}, f32[104,768]{1,0:T(8,128)S(1)}, u32[]{:S(2)}, u32[]{:S(2)}) collective-permute-start(f32[104,768]{1,0:T(8,128)} %get-tuple-element.15), channel_id=1, source_target_pairs={{64,0},{128,64},{192,128},{256,192},{320,256},{384,320},{448,384},... | collective-permute-start | bytes 958472 | tf_op jit(solution)/shard_map/ppermute | solution.py:474
  32.0 0.0 all-to-all-done.blocks
  32.0 0.0 copy-start.11
  32.0 0.6 copy-done.11
  32.6 1.8 %route.1 = f32[80,2,128]{2,1,0:T(2,128)} custom-call(s32[1,64]{1,0:T(1,128)} %owner.5, f32[4,8,128]{2,1,0:T(8,128)} %copy-done.11), custom_call_target="tpu_custom_call" | custom-call | tf_op jit(solution)/shard_map/route/pallas_call | solution.py:114
  34.4 20.8 %all_to_all.15.received = f32[80,2,128]{2,1,0:T(2,128)} all-to-all(f32[80,2,128]{2,1,0:T(2,128)} %route.1), channel_id=1, replica_groups={{0,1,2,3,4,5,6,7,8,9,10,11,12,13,14,15},{16,17,18,19,20,21,22,23,24,25,..., dimensions={0} | all-to-all | bytes 163840 | tf_op jit(solution)/shard_map/all_to_all | solution.py:488
  55.2 1.7 %readers.1 = (f32[32,128]{1,0:T(8,128)}, f32[8,128]{1,0:T(8,128)}, f32[8,128]{1,0:T(8,128)}) custom-call(s32[1,64]{1,0:T(1,128)} %owner.5, f32[80,2,128]{2,1,0:T(2,128)} %all_to_all.15.received), custom_call_target="tpu_custom_call" | custom-call | tf_op jit(solution)/shard_map/readers/pallas_call | solution.py:181
  56.9 0.0 copy-start.6
  56.9 5.1 %collective-permute-start.4 = (f32[8,128]{1,0:T(8,128)}, f32[8,128]{1,0:T(8,128)S(1)}, u32[]{:S(2)}, u32[]{:S(2)}) collective-permute-start(f32[8,128]{1,0:T(8,128)} %get-tuple-element.18), channel_id=1, source_target_pairs={{0,64},{64,128},{128,192},{192,256},{256,320},{320,384},{384,448},... | collective-permute-start | bytes 12296 | tf_op jit(solution)/shard_map/ppermute | solution.py:474
  62.0 0.0 copy-start.8
  62.0 0.0 copy-start.9
  62.0 0.0 copy-start.10
  62.0 2.1 %collective-permute-start.5 = (f32[8,128]{1,0:T(8,128)}, f32[8,128]{1,0:T(8,128)S(1)}, u32[]{:S(2)}, u32[]{:S(2)}) collective-permute-start(f32[8,128]{1,0:T(8,128)} %get-tuple-element.19), channel_id=1, source_target_pairs={{64,0},{128,64},{192,128},{256,192},{320,256},{384,320},{448,384},... | collective-permute-start | bytes 12296 | tf_op jit(solution)/shard_map/ppermute | solution.py:474
  64.1 0.0 collective-permute-done.4.wind_up
  64.1 3.2 %collective-permute-done.5.wind_down = f32[8,128]{1,0:T(8,128)S(1)} collective-permute-done((f32[8,128]{1,0:T(8,128)}, f32[8,128]{1,0:T(8,128)S(1)}, u32[]{:S(2)}, u32[]{:S(2)}) %collective-permute-start.5) | collective-permute-done | bytes 4128 | tf_op jit(solution)/shard_map/ppermute | solution.py:474
  67.3 0.0 collective-permute-done.2.from_up
  67.3 0.0 collective-permute-done.3.from_down
  67.3 0.0 copy-done
  67.3 0.0 copy-done.1
  67.3 0.0 copy-done.3
  67.3 0.0 copy-done.5
  67.4 0.0 copy-done.6
  67.4 0.0 copy-done.8
  67.4 0.0 copy-done.9
  67.4 0.0 copy-done.10
  67.4 0.0 copy-start.7
  67.4 0.7 copy-done.7
  68.1 19.2 %slab.1 = (f32[320,640]{1,0:T(8,128)}, f32[64,4,128]{2,1,0:T(4,128)S(1)}) custom-call(f32[320,640]{1,0:T(8,128)S(1)} %copy-done, s32[320,640]{1,0:T(8,128)S(1)} %copy-done.1, f32[328,128]{1,0:T(8,128)S(1)} %copy-done.3, f32[328,128]{1,0:T(8,128)S(1)} %copy-done.5, f32[104,768]{1,0:T(8,128)S(1)} %collective-permute-done.2.from_up, ...), custom_call_target="tpu_custom_call" | custom-call | tf_op jit(solution)/shard_map/slab/pallas_call | solution.py:428
  87.3 21.4 %all_to_all.16.received = f32[64,4,128]{2,1,0:T(4,128)} all-to-all(f32[64,4,128]{2,1,0:T(4,128)S(1)} %get-tuple-element.21), channel_id=1, replica_groups=mesh['grp'=8,'tile'=64] {'tile'}, dimensions={0} | all-to-all | bytes 262144 | tf_op jit(solution)/shard_map/all_to_all | solution.py:496
  108.7 1.7 %final.1 = f32[2,16,32]{2,1,0:T(8,128)} custom-call(s32[1,64]{1,0:T(1,128)} %owner.5, f32[64,4,128]{2,1,0:T(4,128)} %all_to_all.16.received, f32[2,16,32]{2,1,0:T(8,128)} %wind.3), custom_call_target="tpu_custom_call" | custom-call | tf_op jit(solution)/shard_map/final/pallas_call | solution.py:466
Async XLA Ops:
  4.0 17.9 %collective-permute-start = (f32[328,128]{1,0:T(8,128)}, f32[328,128]{1,0:T(8,128)S(1)}, u32[]{:S(2)}, u32[]{:S(2)}) collective-permute-start(f32[328,128]{1,0:T(8,128)} %get-tuple-element.12), channel_id=1, source_target_pairs={{0,1},{1,2},{2,3},{3,4},{4,5},{5,6},{6,7},{7,8},{8,9},{9,10},{10,1... | collective-permute-start | bytes 503816 | tf_op jit(solution)/shard_map/ppermute | solution.py:474
  8.3 13.5 %collective-permute-start.1 = (f32[328,128]{1,0:T(8,128)}, f32[328,128]{1,0:T(8,128)S(1)}, u32[]{:S(2)}, u32[]{:S(2)}) collective-permute-start(f32[328,128]{1,0:T(8,128)} %get-tuple-element.13), channel_id=1, source_target_pairs={{1,0},{2,1},{3,2},{4,3},{5,4},{6,5},{7,6},{8,7},{9,8},{10,9},{11,1... | collective-permute-start | bytes 503816 | tf_op jit(solution)/shard_map/ppermute | solution.py:474
  9.6 22.3 %all-to-all-start = ((f32[4,8,128]{2,1,0:T(8,128)}), f32[4,8,128]{2,1,0:T(8,128)S(1)}, u32[]{:S(2)}, u32[]{:S(2)}) async-start(f32[4,8,128]{2,1,0:T(8,128)} %get-tuple-element.16), calls=%async_computation | async-start | bytes 32768 | tf_op jit(solution)/shard_map/all_to_all | solution.py:483
  21.9 0.7 copy-start.2
  22.5 0.7 copy-start.4
  23.2 44.1 %copy-start = (f32[320,640]{1,0:T(8,128)S(1)}, f32[320,640]{1,0:T(8,128)}, u32[]{:S(2)}) copy-start(f32[320,640]{1,0:T(8,128)} %level.1) | copy-start | bytes 2457604
  23.2 44.1 %copy-start.1 = (s32[320,640]{1,0:T(8,128)S(1)}, s32[320,640]{1,0:T(8,128)}, u32[]{:S(2)}) copy-start(s32[320,640]{1,0:T(8,128)} %fuel.1) | copy-start | bytes 2457604
  25.6 41.8 %collective-permute-start.2 = (f32[104,768]{1,0:T(8,128)}, f32[104,768]{1,0:T(8,128)S(1)}, u32[]{:S(2)}, u32[]{:S(2)}) collective-permute-start(f32[104,768]{1,0:T(8,128)} %get-tuple-element.14), channel_id=1, source_target_pairs={{0,64},{64,128},{128,192},{192,256},{256,320},{320,384},{384,448},... | collective-permute-start | bytes 958472 | tf_op jit(solution)/shard_map/ppermute | solution.py:474
  29.9 37.5 %copy-start.3 = (f32[328,128]{1,0:T(8,128)S(1)}, f32[328,128]{1,0:T(8,128)}, u32[]{:S(2)}) copy-start(f32[328,128]{1,0:T(8,128)} %copy-done.2) | copy-start | bytes 503812
  29.9 37.5 %copy-start.5 = (f32[328,128]{1,0:T(8,128)S(1)}, f32[328,128]{1,0:T(8,128)}, u32[]{:S(2)}) copy-start(f32[328,128]{1,0:T(8,128)} %copy-done.4) | copy-start | bytes 503812
  29.9 37.4 %collective-permute-start.3 = (f32[104,768]{1,0:T(8,128)}, f32[104,768]{1,0:T(8,128)S(1)}, u32[]{:S(2)}, u32[]{:S(2)}) collective-permute-start(f32[104,768]{1,0:T(8,128)} %get-tuple-element.15), channel_id=1, source_target_pairs={{64,0},{128,64},{192,128},{256,192},{320,256},{384,320},{448,384},... | collective-permute-start | bytes 958472 | tf_op jit(solution)/shard_map/ppermute | solution.py:474
  32.0 0.6 copy-start.11
  56.9 10.5 %copy-start.6 = (s32[4,1,1]{2,1,0:T(1,128)S(1)}, s32[4,1,1]{2,1,0:T(1,128)}, u32[]{:S(2)}) copy-start(s32[4,1,1]{2,1,0:T(1,128)} %copy.10.active) | copy-start | bytes 52
  56.9 7.2 %collective-permute-start.4 = (f32[8,128]{1,0:T(8,128)}, f32[8,128]{1,0:T(8,128)S(1)}, u32[]{:S(2)}, u32[]{:S(2)}) collective-permute-start(f32[8,128]{1,0:T(8,128)} %get-tuple-element.18), channel_id=1, source_target_pairs={{0,64},{64,128},{128,192},{192,256},{256,320},{320,384},{384,448},... | collective-permute-start | bytes 12296 | tf_op jit(solution)/shard_map/ppermute | solution.py:474
  62.0 5.4 %copy-start.8 = (f32[13]{0:T(128)S(1)}, f32[13]{0:T(128)}, u32[]{:S(2)}) copy-start(f32[13]{0:T(128)} %fuel_rate.1) | copy-start | bytes 160
  62.0 5.4 %copy-start.9 = (f32[13]{0:T(128)S(1)}, f32[13]{0:T(128)}, u32[]{:S(2)}) copy-start(f32[13]{0:T(128)} %fuel_wind.1) | copy-start | bytes 160
  62.0 5.4 %copy-start.10 = (f32[13]{0:T(128)S(1)}, f32[13]{0:T(128)}, u32[]{:S(2)}) copy-start(f32[13]{0:T(128)} %fuel_heat.1) | copy-start | bytes 160
  62.0 5.3 %collective-permute-start.5 = (f32[8,128]{1,0:T(8,128)}, f32[8,128]{1,0:T(8,128)S(1)}, u32[]{:S(2)}, u32[]{:S(2)}) collective-permute-start(f32[8,128]{1,0:T(8,128)} %get-tuple-element.19), channel_id=1, source_target_pairs={{64,0},{128,64},{192,128},{256,192},{320,256},{384,320},{448,384},... | collective-permute-start | bytes 12296 | tf_op jit(solution)/shard_map/ppermute | solution.py:474
  67.4 0.7 copy-start.7

commit v2 on v1

v2 whole, which is shorter than its diff:
```python
import jax
import jax.numpy as jnp
from jax import lax
from jax.experimental import pallas as pl
from jax.experimental.pallas import tpu as pltpu
from jax.sharding import PartitionSpec as P

R = 20
AY = 16
AX = 32
FY = 320
FX = 640
STEPS = 2
SUBSTEPS = 2
NZ = 16
NX = 4
HALO = 48
HALF = 64
PAD = 8
TOP = PAD + HALO
ROWS = TOP + FY + HALO + PAD
COLS = FX + 2 * HALF
NL = COLS // 128
RIGHT = 40
LEFT = 51
CR = 24

VM = pl.BlockSpec(memory_space=pltpu.VMEM)
SM = pl.BlockSpec(memory_space=pltpu.SMEM)
PARAMS = pltpu.CompilerParams(vmem_limit_bytes=40 * 1024 * 1024)


def lanes(shape):
    return lax.broadcasted_iota(jnp.int32, shape, 1)


def f32(*shape):
    return jax.ShapeDtypeStruct(shape, jnp.float32)


def thirds(x):
    high = x.astype(jnp.bfloat16)
    rest = x - high.astype(jnp.float32)
    middle = rest.astype(jnp.bfloat16)
    low = (rest - middle.astype(jnp.float32)).astype(jnp.bfloat16)
    return jnp.concatenate([high, middle, low], axis=0)


def exact_dot(x, onehot):
    n = x.shape[0]
    out = jnp.dot(thirds(x), onehot, preferred_element_type=jnp.float32)
    return out[:n] + out[n : 2 * n] + out[2 * n :]


def coarse_lane(fine):
    own = fine // R
    right = RIGHT + (fine - FX) // R
    left = LEFT - (COLS - 1 - fine) // R
    edge = jnp.where(fine < FX + 3 * R, right, jnp.where(fine >= COLS - 3 * R, left, -1))
    return jnp.where(fine < FX, own, edge)


def pack_kernel(level0, level4, fuel0, fuel4, wind, active, to_left, to_right, slots):
    lane = lanes((FY, 128))
    fuel_first = pltpu.roll(fuel0[...].astype(jnp.float32), HALF, 1)
    fuel_last = pltpu.roll(fuel4[...].astype(jnp.float32), HALF, 1)
    to_left[0:FY, :] = jnp.where(lane < HALF, level0[...], fuel_first)
    to_right[0:FY, :] = jnp.where(lane >= HALF, level4[...], fuel_last)
    for k in range(8):
        row = jnp.full((1, 128), flag_of(active, k), jnp.float32)
        to_left[FY + k : FY + k + 1, :] = row
        to_right[FY + k : FY + k + 1, :] = row
    parts = [wind[0, 0:8, :], wind[0, 8:16, :], wind[1, 0:8, :], wind[1, 8:16, :]]
    block = jnp.concatenate(parts, axis=1)
    for k in range(NX * NZ):
        slots[k] = block


def flag_of(active, k):
    return (active[0, 0, min(k, STEPS * SUBSTEPS - 1)] > 0).astype(jnp.float32)


def whole(*s):
    return pl.BlockSpec(s, lambda i: (0,) * len(s))


def pack(level, fuel, wind, active):
    edge0 = pl.BlockSpec((FY, 128), lambda i: (0, 0))
    edge4 = pl.BlockSpec((FY, 128), lambda i: (0, FX // 128 - 1))
    return pl.pallas_call(
        pack_kernel,
        grid=(1,),
        in_specs=[edge0, edge4, edge0, edge4, whole(2, AY, AX), SM],
        out_specs=[whole(FY + 8, 128), whole(FY + 8, 128), whole(NX * NZ, 8, 128)],
        out_shape=[f32(FY + 8, 128), f32(FY + 8, 128), f32(NX * NZ, 8, 128)],
        name="pack",
    )(level, level, fuel, fuel, wind, active)


def rows_kernel(
    level_top, level_bottom, fuel_top, fuel_bottom, from_left, from_right, blocks, owner, active,
    held, to_up, to_down,
):
    tile = lax.axis_index("tile")
    lane = lanes((HALO, 128))
    lane8 = lanes((8, 128))
    main = blocks[owner[0, tile]]
    left = blocks[owner[0, jnp.maximum(tile - 1, 0)]]
    right = blocks[owner[0, jnp.minimum(tile + 1, NX * NZ - 1)]]
    is_left = jnp.logical_and(lane8 >= LEFT - 2, lane8 <= LEFT)
    is_right = jnp.logical_and(lane8 >= RIGHT, lane8 <= RIGHT + 2)
    for q in range(4):
        own = pltpu.roll(main, (128 - 32 * q) % 128, 1)
        one = pltpu.roll(left, (LEFT - 31 - 32 * q) % 128, 1)
        two = pltpu.roll(right, (RIGHT - 32 * q) % 128, 1)
        held[8 * q : 8 * q + 8, :] = jnp.where(
            lane8 < AX, own, jnp.where(is_left, one, jnp.where(is_right, two, 0.0))
        )
    for out, level, fuel, start, cut, coarse in (
        (to_up, level_top, fuel_top, 0, 0, 0),
        (to_down, level_bottom, fuel_bottom, FY - HALO, 80 - HALO, AY - 3),
    ):
        out[0:HALO, 0:FX] = level[cut : cut + HALO, :]
        out[HALO : 2 * HALO, 0:FX] = fuel[cut : cut + HALO, :].astype(jnp.float32)
        one = from_left[start : start + HALO, :]
        two = from_right[start : start + HALO, :]
        out[0:HALO, FX:COLS] = jnp.where(lane < HALF, two, one)
        out[HALO : 2 * HALO, FX:COLS] = pltpu.roll(jnp.where(lane < HALF, one, two), HALF, 1)
        for k in range(4):
            row = 2 * HALO + k
            out[row : row + 1, 0:FX] = jnp.full((1, FX), flag_of(active, k), jnp.float32)
            out[row : row + 1, FX:COLS] = jnp.where(
                lane[0:1] < HALF, from_right[FY + k : FY + k + 1, :], from_left[FY + k : FY + k + 1, :]
            )
        row = 2 * HALO + 4
        for c in range(6):
            at = (c // 3) * AY + coarse + c % 3
            out[row : row + 1, 128 * c : 128 * c + 128] = held[at : at + 1, :]
        out[row + 1 : row + 4, :] = jnp.zeros((3, COLS), jnp.float32)


def rows(level, fuel, from_left, from_right, blocks, owner, active):
    top = pl.BlockSpec((80, FX), lambda i: (0, 0))
    bottom = pl.BlockSpec((80, FX), lambda i: (FY // 80 - 1, 0))
    shape = (2 * HALO + 8, COLS)
    return pl.pallas_call(
        rows_kernel,
        grid=(1,),
        in_specs=[top, bottom, top, bottom, whole(FY + 8, 128), whole(FY + 8, 128),
                  whole(NX * NZ, 8, 128), SM, SM],
        out_specs=[whole(2 * AY, 128), whole(*shape), whole(*shape)],
        out_shape=[f32(2 * AY, 128), f32(*shape), f32(*shape)],
        name="rows",
    )(level, level, fuel, fuel, from_left, from_right, blocks, owner, active)


def table(values):
    lane = lanes((8, 128))
    row = jnp.zeros((8, 128), jnp.float32)
    for c in range(values.shape[0]):
        row = jnp.where(lane == c, values[c], row)
    return row


def look(row, kinds):
    return jnp.take_along_axis(row, kinds, axis=1, mode="promise_in_bounds")


def values_kernel(fuel, from_left, from_right, after, fuel_rate, fuel_wind, fuel_heat, rate, drift, heat):
    lane8 = lanes((8, 128))
    tables = [(table(fuel_rate), rate), (table(fuel_wind), drift), (table(fuel_heat), heat)]

    def own_rows(i, _):
        at = pl.multiple_of(i * 8, 8)
        one = from_left[pl.ds(at, 8), :]
        two = from_right[pl.ds(at, 8), :]
        beside = pltpu.roll(jnp.where(lane8 < HALF, one, two), HALF, 1).astype(jnp.int32)
        for c in range(NL):
            kinds = beside if c == NL - 1 else fuel[pl.ds(at, 8), 128 * c : 128 * c + 128]
            for row, out in tables:
                out[pl.ds(at, 8), 128 * c : 128 * c + 128] = look(row, kinds)
        return 0

    lax.fori_loop(0, FY // 8, own_rows, 0, unroll=4)


def values(fuel, from_left, from_right, after, *names):
    return pl.pallas_call(
        values_kernel,
        in_specs=[VM, VM, VM, pl.BlockSpec(memory_space=pl.ANY), SM, SM, SM],
        out_specs=[VM, VM, VM],
        out_shape=[f32(FY, COLS)] * 3,
        compiler_params=PARAMS,
        name="values",
    )(fuel, from_left, from_right, after, *names)


def slab_kernel(
    level, from_left, from_right, from_up, from_down, held, rate, drift, heat,
    active, fuel_rate, fuel_wind, fuel_heat,
    level_out, slots,
    phi_a, phi_b, phi_c, edge_rate, edge_drift, edge_heat, east, north, winds, gates, sums, spread, gather,
):
    group = lax.axis_index("grp")
    tile = lax.axis_index("tile")
    first_row = group == 0
    last_row = group == lax.axis_size("grp") - 1
    first_col = tile == 0
    last_col = tile == lax.axis_size("tile") - 1
    lane8 = lanes((8, 128))
    sub8 = lax.broadcasted_iota(jnp.int32, (8, COLS), 0)

    zero = jnp.zeros((PAD, COLS), jnp.float32)
    phi_a[0:PAD, :] = zero
    phi_a[ROWS - PAD : ROWS, :] = zero
    phi_a[TOP - HALO : TOP, :] = from_up[0:HALO, :]
    phi_a[TOP + FY : TOP + FY + HALO, :] = from_down[0:HALO, :]

    def own_rows(i, _):
        at = pl.multiple_of(i * 8, 8)
        to = pl.multiple_of(i * 8 + TOP, 8)
        phi_a[pl.ds(to, 8), 0:FX] = level[pl.ds(at, 8), :]
        one = from_left[pl.ds(at, 8), :]
        two = from_right[pl.ds(at, 8), :]
        phi_a[pl.ds(to, 8), FX:COLS] = jnp.where(lane8 < HALF, two, one)
        return 0

    lax.fori_loop(0, FY // 8, own_rows, 0, unroll=4)
    tables = [(table(fuel_rate), edge_rate), (table(fuel_wind), edge_drift), (table(fuel_heat), edge_heat)]

    def halo_rows(i, _):
        at = pl.multiple_of(i * 8, 8)
        for source, start in ((from_up, 0), (from_down, HALO)):
            to = pl.multiple_of(at + start, 8)
            for c in range(NL):
                kinds = source[pl.ds(pl.multiple_of(at + HALO, 8), 8), 128 * c : 128 * c + 128]
                kinds = kinds.astype(jnp.int32)
                for row, out in tables:
                    out[pl.ds(to, 8), 128 * c : 128 * c + 128] = look(row, kinds)
        return 0

    lax.fori_loop(0, HALO // 8, halo_rows, 0, unroll=3)

    gates[0:8, :] = from_up[2 * HALO : 2 * HALO + 8, :]
    gates[16:24, :] = from_down[2 * HALO : 2 * HALO + 8, :]
    for k in range(STEPS * SUBSTEPS):
        gates[8 + k : 9 + k, 0:FX] = jnp.full((1, FX), flag_of(active, k), jnp.float32)
    gates[8:16, FX:COLS] = jnp.where(
        lane8 < HALF, from_right[FY : FY + 8, :], from_left[FY : FY + 8, :]
    )

    row = 2 * HALO + 4
    for comp in range(2):
        base = comp * CR
        for c in range(3):
            at = 128 * (3 * comp + c)
            winds[base + c : base + c + 1, :] = from_up[row : row + 1, at : at + 128]
            below = base + 3 + AY + c
            winds[below : below + 1, :] = from_down[row : row + 1, at : at + 128]
        winds[base + 3 : base + 3 + AY, :] = held[AY * comp : AY * comp + AY, :]
        winds[base + 6 + AY : base + CR, :] = jnp.zeros((CR - 6 - AY, 128), jnp.float32)

    spread[...] = (
        coarse_lane(lanes((128, COLS))) == lax.broadcasted_iota(jnp.int32, (128, COLS), 0)
    ).astype(jnp.bfloat16)
    gather[...] = (
        coarse_lane(lax.broadcasted_iota(jnp.int32, (COLS, 128), 0)) == lanes((COLS, 128))
    ).astype(jnp.bfloat16)

    def expand():
        wide = exact_dot(winds[...], spread[...])
        for comp, out in ((0, east), (1, north)):
            part = wide[comp * CR : comp * CR + CR]
            out[0:CR, :] = jnp.maximum(part, 0.0)
            out[CR : 2 * CR, :] = jnp.minimum(part, 0.0)

    def edges(phi):
        @pl.when(first_row)
        def _():
            phi[TOP - 1 : TOP, :] = phi[TOP : TOP + 1, :]

        @pl.when(last_row)
        def _():
            phi[TOP + FY : TOP + FY + 1, :] = phi[TOP + FY - 1 : TOP + FY, :]

        @pl.when(first_col)
        def _():
            old = phi[:, COLS - 128 : COLS]
            new = jnp.broadcast_to(phi[:, 0:1], (ROWS, 128))
            phi[:, COLS - 128 : COLS] = jnp.where(lanes((ROWS, 128)) == 127, new, old)

        @pl.when(last_col)
        def _():
            old = phi[:, FX : FX + 128]
            new = jnp.broadcast_to(phi[:, FX - 1 : FX], (ROWS, 128))
            phi[:, FX : FX + 128] = jnp.where(lanes((ROWS, 128)) == 0, new, old)

    own = (rate, drift, heat, TOP)
    upper_edge = (edge_rate, edge_drift, edge_heat, TOP - HALO)
    lower_edge = (edge_rate, edge_drift, edge_heat, TOP + FY - HALO)

    def update(phi, at, e, n, gate, fuels):
        before = phi[pl.ds(pl.multiple_of(at - 8, 8), 8), :]
        now = phi[pl.ds(at, 8), :]
        after = phi[pl.ds(pl.multiple_of(at + 8, 8), 8), :]
        south = jnp.where(sub8 == 0, pltpu.roll(before, 1, 0), pltpu.roll(now, 1, 0))
        above = jnp.where(sub8 == 7, pltpu.roll(after, 7, 0), pltpu.roll(now, 7, 0))
        west = pltpu.roll(now, 1, 1)
        east_cell = pltpu.roll(now, COLS - 1, 1)
        back_x = now - west
        ahead_x = east_cell - now
        back_y = now - south
        ahead_y = above - now
        bx = jnp.maximum(back_x, 0.0)
        ax = jnp.minimum(ahead_x, 0.0)
        by = jnp.maximum(back_y, 0.0)
        ay = jnp.minimum(ahead_y, 0.0)
        square = bx * bx + ax * ax + by * by + ay * ay + 1e-12
        slope = square * lax.rsqrt(square)
        carry = e[0] * back_x + e[1] * ahead_x + n[0] * back_y + n[1] * ahead_y
        there = pl.multiple_of(at - fuels[3], 8)
        change = fuels[0][pl.ds(there, 8), :] * slope + fuels[1][pl.ds(there, 8), :] * carry
        return now - gate * change

    def wind_row(ref, row):
        return tuple(jnp.broadcast_to(ref[pl.ds(row + part, 1), :], (8, COLS)) for part in (0, CR))

    def mix(a, b):
        return tuple(jnp.where(sub8 < 4, one, two) for one, two in zip(a, b))

    def band(phi, m, k, region, fuels, finish):
        at = pl.multiple_of(2 * PAD + 40 * m, 8)
        gate = jnp.broadcast_to(gates[region * 8 + k : region * 8 + k + 1, :], (8, COLS))
        row = 2 * m + 1
        for t in range(5):
            if t == 2:
                e = mix(wind_row(east, row), wind_row(east, row + 1))
                n = mix(wind_row(north, row), wind_row(north, row + 1))
            else:
                e, n = (wind_row(ref, row + t // 3) for ref in (east, north))
            here = pl.multiple_of(at + 8 * t, 8)
            finish(here, update(phi, here, e, n, gate, fuels), fuels)

    def tile_rows(phi, at, row, region, k, fuels):
        gate = jnp.broadcast_to(gates[region * 8 + k : region * 8 + k + 1, :], (8, COLS))
        return update(phi, at, wind_row(east, row), wind_row(north, row), gate, fuels)

    def own_bands(body):
        def step(m, _):
            body(m, 1, own)
            return 0

        lax.fori_loop(1, 9, step, 0)

    def store_to(out):
        def finish(here, new, fuels):
            out[pl.ds(here, 8), :] = new

        return finish

    def flux_band(before, phi, out, k):
        def body(m, region, fuels):
            parts = []

            def finish(here, new, fuels):
                if out is not None:
                    out[pl.ds(here, 8), :] = new
                else:
                    level_out[pl.ds(pl.multiple_of(here - TOP, 8), 8), :] = new[:, 0:FX]
                old = before[pl.ds(here, 8), :]
                there = pl.multiple_of(here - fuels[3], 8)
                parts.append(fuels[2][pl.ds(there, 8), :] * (jnp.tanh(old) - jnp.tanh(new)))

            band(phi, m, k, region, fuels, finish)
            low = parts[0] + parts[1] + jnp.where(sub8 < 4, parts[2], 0.0)
            high = parts[3] + parts[4] + jnp.where(sub8 >= 4, parts[2], 0.0)
            sums[pl.ds(2 * m + 1, 1), :] = jnp.sum(low, axis=0, keepdims=True)
            sums[pl.ds(2 * m + 2, 1), :] = jnp.sum(high, axis=0, keepdims=True)

        return body

    def pooled():
        return exact_dot(sums[...], gather[...]) * (0.5 / (R * R))

    lane_c = lanes((CR, 128))
    row_c = lax.broadcasted_iota(jnp.int32, (CR, 128), 0)
    sums[...] = jnp.zeros((CR, COLS), jnp.float32)

    expand()
    edges(phi_a)
    phi_b[PAD : PAD + 8, :] = tile_rows(phi_a, PAD, 0, 0, 0, upper_edge)
    phi_b[ROWS - 2 * PAD : ROWS - PAD, :] = tile_rows(phi_a, ROWS - 2 * PAD, AY + 5, 2, 0, lower_edge)
    band(phi_a, 0, 0, 0, upper_edge, store_to(phi_b))
    band(phi_a, 9, 0, 2, lower_edge, store_to(phi_b))
    own_bands(lambda m, region, fuels: band(phi_a, m, 0, region, fuels, store_to(phi_b)))
    edges(phi_b)
    second = flux_band(phi_a, phi_b, phi_c, 1)
    second(0, 0, upper_edge)
    second(9, 2, lower_edge)
    own_bands(second)
    edges(phi_c)

    flux0 = pooled()
    ahead = jnp.where(jnp.logical_or(lane_c == AX - 1, lane_c == LEFT), flux0, pltpu.roll(flux0, 127, 1))
    back = jnp.where(jnp.logical_or(lane_c == 0, lane_c == RIGHT), flux0, pltpu.roll(flux0, 1, 1))
    last_rows = jnp.logical_or(row_c == 2, row_c == AY + 2)
    first_rows = jnp.logical_or(row_c == 3, row_c == AY + 3)
    below = jnp.where(last_rows, flux0, pltpu.roll(flux0, CR - 1, 0))
    upper = jnp.where(first_rows, flux0, pltpu.roll(flux0, 1, 0))
    winds[0:CR, :] = 0.9 * winds[0:CR, :] + 20.0 * (ahead - back)
    winds[CR : 2 * CR, :] = 0.9 * winds[CR : 2 * CR, :] + 20.0 * (below - upper)
    expand()

    top = TOP - 8
    bottom = TOP + FY
    phi_b[top : top + 8, :] = tile_rows(phi_c, top, 2, 0, 2, upper_edge)
    phi_b[bottom : bottom + 8, :] = tile_rows(phi_c, bottom, AY + 3, 2, 2, lower_edge)
    own_bands(lambda m, region, fuels: band(phi_c, m, 2, region, fuels, store_to(phi_b)))
    edges(phi_b)
    own_bands(flux_band(phi_c, phi_b, None, 3))
    total = 0.9 * flux0 + pooled()

    packed = jnp.zeros((4, 128), jnp.float32)
    lane4 = lanes((4, 128))
    for q in range(4):
        moved = pltpu.roll(total, 32 * q, 1)[3 + 4 * q : 7 + 4 * q]
        packed = jnp.where(lane4 // AX == q, moved, packed)
    for k in range(NX * NZ):
        slots[k] = packed


def slab(*args):
    big = pltpu.VMEM((ROWS, COLS), jnp.float32)
    edge = pltpu.VMEM((2 * HALO, COLS), jnp.float32)
    return pl.pallas_call(
        slab_kernel,
        in_specs=[VM] * 9 + [SM] * 4,
        out_specs=[VM, VM],
        out_shape=[f32(FY, FX), f32(NX * NZ, 4, 128)],
        scratch_shapes=[big] * 3
        + [edge] * 3
        + [
            pltpu.VMEM((2 * CR, COLS), jnp.float32),
            pltpu.VMEM((2 * CR, COLS), jnp.float32),
            pltpu.VMEM((2 * CR, 128), jnp.float32),
            pltpu.VMEM((CR, COLS), jnp.float32),
            pltpu.VMEM((CR, COLS), jnp.float32),
            pltpu.VMEM((128, COLS), jnp.bfloat16),
            pltpu.VMEM((COLS, 128), jnp.bfloat16),
        ],
        compiler_params=PARAMS,
        name="slab",
    )(*args)


def final_kernel(owner, received, wind, wind_out):
    tile = lax.axis_index("tile")
    source = jnp.int32(0)
    for t in range(NX * NZ):
        source = jnp.where(owner[0, t] == tile, t, source)
    block = received[source]
    flux = jnp.concatenate([pltpu.roll(block, (128 - 32 * q) % 128, 1) for q in range(4)], axis=0)
    lane = lanes((AY, 128))
    row = lax.broadcasted_iota(jnp.int32, (AY, 128), 0)
    ahead = jnp.where(lane == AX - 1, flux, pltpu.roll(flux, 127, 1))
    back = jnp.where(lane == 0, flux, pltpu.roll(flux, 1, 1))
    below = jnp.where(row == AY - 1, flux, pltpu.roll(flux, AY - 1, 0))
    upper = jnp.where(row == 0, flux, pltpu.roll(flux, 1, 0))
    wind_out[0] = 0.81 * wind[0] + 20.0 * (ahead - back)[:, 0:AX]
    wind_out[1] = 0.81 * wind[1] + 20.0 * (below - upper)[:, 0:AX]


def final(owner, received, wind):
    return pl.pallas_call(
        final_kernel, in_specs=[SM, VM, VM], out_specs=VM, out_shape=f32(2, AY, AX), name="final"
    )(owner, received, wind)


def shift(value, axis, step):
    size = lax.axis_size(axis)
    pairs = [(i, i + step) for i in range(size) if 0 <= i + step < size]
    return lax.ppermute(value, axis, pairs)


def shards(level, fuel, wind, owner, active, fuel_rate, fuel_wind, fuel_heat):
    active = jnp.transpose(active, (1, 2, 0))
    tables = (fuel_rate, fuel_wind, fuel_heat)
    to_left, to_right, blocks = pack(level, fuel, wind, active)
    from_right = shift(to_left, "tile", -1)
    from_left = shift(to_right, "tile", 1)
    blocks = lax.all_to_all(blocks, "tile", 0, 0, tiled=True)
    held, to_up, to_down = rows(level, fuel, from_left, from_right, blocks, owner, active)
    from_down = shift(to_up, "grp", -1)
    from_up = shift(to_down, "grp", 1)
    rate, drift, heat = values(fuel, from_left, from_right, held, *tables)
    level_out, flux = slab(
        level, from_left, from_right, from_up, from_down, held, rate, drift, heat, active, *tables
    )
    flux = lax.all_to_all(flux, "tile", 0, 0, tiled=True)
    return (level_out, final(owner, flux, wind))


def solution(mesh):
    in_specs = (
        P("grp", "tile"),
        P("grp", "tile"),
        P(None, "grp", "tile"),
        P("grp", None),
        P(None, "grp", "tile"),
        P(),
        P(),
        P(),
    )
    out_specs = (P("grp", "tile"), P(None, "grp", "tile"))
    return jax.shard_map(shards, mesh=mesh, in_specs=in_specs, out_specs=out_specs, check_vma=False)
```

time: 111 us -> 98.3 us (0.89)
  blocking collectives: 42.2 us -> 23.2 us
  waiting for transfers between devices: 3.21 us -> 15.8 us
  Pallas kernels: 28.7 us -> 21.3 us
    all_to_all x1 -> x0, blocking collectives: 20.8 us -> none  [shards(): lax.all_to_all(slots, 'tile', 0, 0, tiled=True, axis_index_groups=along_z)]
    ppermute x6 -> x4, waiting for transfers between devices: 3.21 us -> 12.3 us  [shift(): return lax.ppermute(value, axis, pairs)]
    all_to_all x1, starting transfers between devices: 12.2 us -> 19.2 us  [shards(): blocks = lax.all_to_all(blocks, 'tile', 0, 0, tiled=True)]
    pallas_call x1, Pallas kernels: 19.2 us -> 12.2 us  [slab(): pl.pallas_call(slab_kernel, in_specs=[VM] * 9 + [SM] * 4, out_specs=[VM,...]
    ppermute x6 -> x4, starting transfers between devices: 19.2 us -> 12.9 us  [shift(): return lax.ppermute(value, axis, pairs)]
    all_to_all x1, waiting for transfers between devices: 0.01 us -> 3.44 us  [shards(): blocks = lax.all_to_all(blocks, 'tile', 0, 0, tiled=True)]
    all_to_all x1, blocking collectives: 21.4 us -> 23.2 us  [shards(): flux = lax.all_to_all(flux, 'tile', 0, 0, tiled=True)]
    pallas_call x2 -> x1, Pallas kernels: 3.48 us -> 2.86 us  [values(): pl.pallas_call(values_kernel, in_specs=[VM, VM, VM, pl.BlockSpec(memory_s...]
  transfers between devices with their start and end apart: 7 -> 5, of which waited for: 1 -> 4; matrix products, arithmetic and copies ran while one was open for 0% -> 0% of each run, Pallas kernels for 5% -> 3%
where the time goes in v2:
time: 98.3 us; the launch traced here: 97.1 us
  starting transfers between devices  32.1 us (33%)
  blocking collectives  23.2 us (24%)
  Pallas kernels  21.3 us (22%)
  waiting for transfers between devices  15.8 us (16%)
  local copies, waits for them, and re-layouts  3.92 us (4%)
    all_to_all x1, blocking collectives, shards(): flux = lax.all_to_all(flux, 'tile', 0, 0, tiled=True)  23.2 us
    all_to_all x1, starting transfers between devices, shards(): blocks = lax.all_to_all(blocks, 'tile', 0, 0, tiled=True)  19.2 us
    ppermute x4, starting transfers between devices, shift(): return lax.ppermute(value, axis, pairs)  12.9 us
    ppermute x4, waiting for transfers between devices, shift(): return lax.ppermute(value, axis, pairs)  12.3 us
    pallas_call x1, Pallas kernels, slab(): pl.pallas_call(slab_kernel, in_specs=[VM] * 9 + [SM] * 4, out_specs=[VM,...  12.2 us
    unnamed x30, local copies, waits for them, and re-layouts  3.92 us
    all_to_all x1, waiting for transfers between devices, shards(): blocks = lax.all_to_all(blocks, 'tile', 0, 0, tiled=True)  3.44 us
    pallas_call x1, Pallas kernels, values(): pl.pallas_call(values_kernel, in_specs=[VM, VM, VM, pl.BlockSpec(memory_s...  2.86 us
  transfers between devices with their start and end apart: 5, of which 4 were waited for; matrix products, arithmetic and copies ran while one was open for 0% of the time, Pallas kernels for 3%

profile of v2, /device:TPU:1, one launch (start us, length us, event | category | flops | bytes accessed | tf_op | source)
XLA Modules:
  0.0 97.1 jit_solution(18311688592249675612)
XLA Ops:
  0.6 2.1 %pack.1 = (f32[328,128]{1,0:T(8,128)}, f32[328,128]{1,0:T(8,128)}, f32[64,8,128]{2,1,0:T(8,128)}) custom-call(f32[320,640]{1,0:T(8,128)} %level.1, f32[320,640]{1,0:T(8,128)} %level.1, s32[320,640]{1,0:T(8,128)} %fuel.1, s32[320,640]{1,0:T(8,128)} %fuel.1, f32[2,16,32]{2,1,0:T(8,128)} %wind.3, s32[1,1,4]{2,1,0:T(1,128)} %bitcast.1), custom_call_target="tpu_custom_call" | custom-call | tf_op jit(solution)/shard_map/pack/pallas_call | solution.py:90
  2.7 0.0 copy-start.14
  2.7 0.0 copy-start.13
  2.7 19.2 %all-to-all-start = ((f32[64,8,128]{2,1,0:T(8,128)}), f32[64,8,128]{2,1,0:T(8,128)S(1)}, u32[]{:S(2)}, u32[]{:S(2)}) async-start(f32[64,8,128]{2,1,0:T(8,128)} %get-tuple-element.15), calls=%async_computation | async-start | bytes 524288 | tf_op jit(solution)/shard_map/all_to_all | solution.py:491
  22.0 0.0 copy-done.14
  22.0 2.9 %collective-permute-start = (f32[328,128]{1,0:T(8,128)S(1)}, f32[328,128]{1,0:T(8,128)S(1)}, u32[]{:S(2)}, u32[]{:S(2)}) collective-permute-start(f32[328,128]{1,0:T(8,128)S(1)} %copy-done.14), channel_id=1, source_target_pairs={{0,1},{1,2},{2,3},{3,4},{4,5},{5,6},{6,7},{7,8},{8,9},{9,10},{10,1... | collective-permute-start | bytes 503816 | tf_op jit(solution)/shard_map/ppermute | solution.py:482
  24.9 0.0 copy-done.13
  24.9 0.0 copy-start
  25.0 1.4 %collective-permute-start.1 = (f32[328,128]{1,0:T(8,128)S(1)}, f32[328,128]{1,0:T(8,128)S(1)}, u32[]{:S(2)}, u32[]{:S(2)}) collective-permute-start(f32[328,128]{1,0:T(8,128)S(1)} %copy-done.13), channel_id=1, source_target_pairs={{1,0},{2,1},{3,2},{4,3},{5,4},{6,5},{7,6},{8,7},{9,8},{10,9},{11,1... | collective-permute-start | bytes 503816 | tf_op jit(solution)/shard_map/ppermute | solution.py:482
  26.4 9.4 %collective-permute-done.from_left = f32[328,128]{1,0:T(8,128)S(1)} collective-permute-done((f32[328,128]{1,0:T(8,128)S(1)}, f32[328,128]{1,0:T(8,128)S(1)}, u32[]{:S(2)}, u32[]{:S(2)}) %collective-permute-start) | collective-permute-done | bytes 167968 | tf_op jit(solution)/shard_map/ppermute | solution.py:482
  35.8 0.0 copy-start.2
  35.8 1.8 %collective-permute-done.1.from_right = f32[328,128]{1,0:T(8,128)S(1)} collective-permute-done((f32[328,128]{1,0:T(8,128)S(1)}, f32[328,128]{1,0:T(8,128)S(1)}, u32[]{:S(2)}, u32[]{:S(2)}) %collective-permute-start.1) | collective-permute-done | bytes 167968 | tf_op jit(solution)/shard_map/ppermute | solution.py:482
  37.6 0.0 copy-start.5
  37.6 3.4 %all-to-all-done.blocks = f32[64,8,128]{2,1,0:T(8,128)S(1)} async-done(((f32[64,8,128]{2,1,0:T(8,128)}), f32[64,8,128]{2,1,0:T(8,128)S(1)}, u32[]{:S(2)}, u32[]{:S(2)}) %all-to-all-start) | async-done | bytes 262176 | tf_op jit(solution)/shard_map/all_to_all | solution.py:491
  41.0 0.0 copy-done.2
  41.0 0.0 copy-done.5
  41.1 0.0 copy-start.12
  41.1 0.7 copy-done.12
  41.7 0.0 copy-start.9
  41.7 0.0 copy-start.10
  41.7 0.0 copy-start.11
  41.8 2.4 %rows.1 = (f32[32,128]{1,0:T(8,128)}, f32[104,768]{1,0:T(8,128)}, f32[104,768]{1,0:T(8,128)}) custom-call(f32[320,640]{1,0:T(8,128)} %level.1, f32[320,640]{1,0:T(8,128)} %level.1, s32[320,640]{1,0:T(8,128)} %fuel.1, s32[320,640]{1,0:T(8,128)} %fuel.1, f32[328,128]{1,0:T(8,128)} %copy-done.2, f32[328,128]{1,0:T(8,128)} %copy-done.5, ...), custom_call_target="tpu_custom_call" | custom-call | tf_op jit(solution)/shard_map/rows/pallas_call | solution.py:146
  44.1 0.0 copy-start.1
  44.1 6.6 %collective-permute-start.2 = (f32[104,768]{1,0:T(8,128)}, f32[104,768]{1,0:T(8,128)S(1)}, u32[]{:S(2)}, u32[]{:S(2)}) collective-permute-start(f32[104,768]{1,0:T(8,128)} %get-tuple-element.16), channel_id=1, source_target_pairs={{0,64},{64,128},{128,192},{192,256},{256,320},{320,384},{384,448},... | collective-permute-start | bytes 958472 | tf_op jit(solution)/shard_map/ppermute | solution.py:482
  50.7 1.9 %collective-permute-start.3 = (f32[104,768]{1,0:T(8,128)}, f32[104,768]{1,0:T(8,128)S(1)}, u32[]{:S(2)}, u32[]{:S(2)}) collective-permute-start(f32[104,768]{1,0:T(8,128)} %get-tuple-element.17), channel_id=1, source_target_pairs={{64,0},{128,64},{192,128},{256,192},{320,256},{384,320},{448,384},... | collective-permute-start | bytes 958472 | tf_op jit(solution)/shard_map/ppermute | solution.py:482
  52.7 0.0 copy-done
  52.7 0.0 copy-done.9
  52.7 0.0 copy-done.10
  52.7 0.0 copy-done.11
  52.7 0.0 copy-start.3
  52.7 0.9 copy-done.3
  53.6 0.0 copy-start.6
  53.6 0.9 copy-done.6
  54.5 0.0 copy-start.7
  54.5 0.7 copy-done.7
  55.3 0.0 copy-start.4
  55.3 2.9 %values.1 = (f32[320,768]{1,0:T(8,128)S(1)}, f32[320,768]{1,0:T(8,128)S(1)}, f32[320,768]{1,0:T(8,128)S(1)}) custom-call(s32[320,640]{1,0:T(8,128)S(1)} %copy-done, f32[328,128]{1,0:T(8,128)S(1)} %copy-done.3, f32[328,128]{1,0:T(8,128)S(1)} %copy-done.6, f32[32,128]{1,0:T(8,128)S(1)} %copy-done.7, f32[13]{0:T(128)S(1)} %copy-done.9, f32[13]{0:T(128)S(1)} %copy-done.10, ...), custom_call_target="tpu_custom_call" | custom-call | tf_op jit(solution)/shard_map/values/pallas_call | solution.py:188
  58.1 0.0 collective-permute-done.2.from_up
  58.1 1.1 %collective-permute-done.3.from_down = f32[104,768]{1,0:T(8,128)S(1)} collective-permute-done((f32[104,768]{1,0:T(8,128)}, f32[104,768]{1,0:T(8,128)S(1)}, u32[]{:S(2)}, u32[]{:S(2)}) %collective-permute-start.3) | collective-permute-done | bytes 319520 | tf_op jit(solution)/shard_map/ppermute | solution.py:482
  59.3 0.0 copy-start.8
  59.3 0.0 copy-done.1
  59.3 0.0 copy-done.4
  59.3 0.6 copy-done.8
  59.9 12.2 %slab.1 = (f32[320,640]{1,0:T(8,128)}, f32[64,4,128]{2,1,0:T(4,128)S(1)}) custom-call(f32[320,640]{1,0:T(8,128)S(1)} %copy-done.1, f32[328,128]{1,0:T(8,128)S(1)} %copy-done.4, f32[328,128]{1,0:T(8,128)S(1)} %copy-done.6, f32[104,768]{1,0:T(8,128)S(1)} %collective-permute-done.2.from_up, f32[104,768]{1,0:T(8,128)S(1)} %collective-permute-done.3.from_down, ...), custom_call_target="tpu_custom_call" | custom-call | tf_op jit(solution)/shard_map/slab/pallas_call | solution.py:435
  72.1 23.2 %all_to_all.10.received = f32[64,4,128]{2,1,0:T(4,128)} all-to-all(f32[64,4,128]{2,1,0:T(4,128)S(1)} %get-tuple-element.23), channel_id=1, replica_groups=mesh['grp'=8,'tile'=64] {'tile'}, dimensions={0} | all-to-all | bytes 262144 | tf_op jit(solution)/shard_map/all_to_all | solution.py:499
  95.3 1.7 %final.1 = f32[2,16,32]{2,1,0:T(8,128)} custom-call(s32[1,64]{1,0:T(1,128)} %owner.3, f32[64,4,128]{2,1,0:T(4,128)} %all_to_all.10.received, f32[2,16,32]{2,1,0:T(8,128)} %wind.3), custom_call_target="tpu_custom_call" | custom-call | tf_op jit(solution)/shard_map/final/pallas_call | solution.py:474
Async XLA Ops:
  2.7 19.3 %copy-start.14 = (f32[328,128]{1,0:T(8,128)S(1)}, f32[328,128]{1,0:T(8,128)}, u32[]{:S(2)}) copy-start(f32[328,128]{1,0:T(8,128)} %get-tuple-element.13) | copy-start | bytes 503812
  2.7 22.2 %copy-start.13 = (f32[328,128]{1,0:T(8,128)S(1)}, f32[328,128]{1,0:T(8,128)}, u32[]{:S(2)}) copy-start(f32[328,128]{1,0:T(8,128)} %get-tuple-element.14) | copy-start | bytes 503812
  2.7 38.3 %all-to-all-start = ((f32[64,8,128]{2,1,0:T(8,128)}), f32[64,8,128]{2,1,0:T(8,128)S(1)}, u32[]{:S(2)}, u32[]{:S(2)}) async-start(f32[64,8,128]{2,1,0:T(8,128)} %get-tuple-element.15), calls=%async_computation | async-start | bytes 524288 | tf_op jit(solution)/shard_map/all_to_all | solution.py:491
  22.0 13.8 %collective-permute-start = (f32[328,128]{1,0:T(8,128)S(1)}, f32[328,128]{1,0:T(8,128)S(1)}, u32[]{:S(2)}, u32[]{:S(2)}) collective-permute-start(f32[328,128]{1,0:T(8,128)S(1)} %copy-done.14), channel_id=1, source_target_pairs={{0,1},{1,2},{2,3},{3,4},{4,5},{5,6},{6,7},{7,8},{8,9},{9,10},{10,1... | collective-permute-start | bytes 503816 | tf_op jit(solution)/shard_map/ppermute | solution.py:482
  24.9 27.7 %copy-start = (s32[320,640]{1,0:T(8,128)S(1)}, s32[320,640]{1,0:T(8,128)}, u32[]{:S(2)}) copy-start(s32[320,640]{1,0:T(8,128)} %fuel.1) | copy-start | bytes 2457604
  25.0 12.7 %collective-permute-start.1 = (f32[328,128]{1,0:T(8,128)S(1)}, f32[328,128]{1,0:T(8,128)S(1)}, u32[]{:S(2)}, u32[]{:S(2)}) collective-permute-start(f32[328,128]{1,0:T(8,128)S(1)} %copy-done.13), channel_id=1, source_target_pairs={{1,0},{2,1},{3,2},{4,3},{5,4},{6,5},{7,6},{8,7},{9,8},{10,9},{11,1... | collective-permute-start | bytes 503816 | tf_op jit(solution)/shard_map/ppermute | solution.py:482
  35.8 5.2 %copy-start.2 = (f32[328,128]{1,0:T(8,128)}, f32[328,128]{1,0:T(8,128)S(1)}, u32[]{:S(2)}) copy-start(f32[328,128]{1,0:T(8,128)S(1)} %collective-permute-done.from_left) | copy-start | bytes 503812
  37.6 3.4 %copy-start.5 = (f32[328,128]{1,0:T(8,128)}, f32[328,128]{1,0:T(8,128)S(1)}, u32[]{:S(2)}) copy-start(f32[328,128]{1,0:T(8,128)S(1)} %collective-permute-done.1.from_right) | copy-start | bytes 503812
  41.1 0.7 copy-start.12
  41.7 10.9 %copy-start.9 = (f32[13]{0:T(128)S(1)}, f32[13]{0:T(128)}, u32[]{:S(2)}) copy-start(f32[13]{0:T(128)} %fuel_rate.3) | copy-start | bytes 160
  41.7 10.9 %copy-start.10 = (f32[13]{0:T(128)S(1)}, f32[13]{0:T(128)}, u32[]{:S(2)}) copy-start(f32[13]{0:T(128)} %fuel_wind.3) | copy-start | bytes 160
  41.7 10.9 %copy-start.11 = (f32[13]{0:T(128)S(1)}, f32[13]{0:T(128)}, u32[]{:S(2)}) copy-start(f32[13]{0:T(128)} %fuel_heat.3) | copy-start | bytes 160
  44.1 15.1 %copy-start.1 = (f32[320,640]{1,0:T(8,128)S(1)}, f32[320,640]{1,0:T(8,128)}, u32[]{:S(2)}) copy-start(f32[320,640]{1,0:T(8,128)} %level.1) | copy-start | bytes 2457604
  44.1 14.0 %collective-permute-start.2 = (f32[104,768]{1,0:T(8,128)}, f32[104,768]{1,0:T(8,128)S(1)}, u32[]{:S(2)}, u32[]{:S(2)}) collective-permute-start(f32[104,768]{1,0:T(8,128)} %get-tuple-element.16), channel_id=1, source_target_pairs={{0,64},{64,128},{128,192},{192,256},{256,320},{320,384},{384,448},... | collective-permute-start | bytes 958472 | tf_op jit(solution)/shard_map/ppermute | solution.py:482
  50.7 8.5 %collective-permute-start.3 = (f32[104,768]{1,0:T(8,128)}, f32[104,768]{1,0:T(8,128)S(1)}, u32[]{:S(2)}, u32[]{:S(2)}) collective-permute-start(f32[104,768]{1,0:T(8,128)} %get-tuple-element.17), channel_id=1, source_target_pairs={{64,0},{128,64},{192,128},{256,192},{320,256},{384,320},{448,384},... | collective-permute-start | bytes 958472 | tf_op jit(solution)/shard_map/ppermute | solution.py:482
  52.7 0.9 copy-start.3
  53.6 0.9 copy-start.6
  54.5 0.7 copy-start.7
  55.3 4.0 %copy-start.4 = (f32[328,128]{1,0:T(8,128)S(1)}, f32[328,128]{1,0:T(8,128)}, u32[]{:S(2)}) copy-start(f32[328,128]{1,0:T(8,128)} %copy-done.2) | copy-start | bytes 503812
  59.3 0.7 copy-start.8

commit v3 on v2

--- a/solution.py
+++ b/solution.py
@@ -27,6 +27,7 @@
 
 VM = pl.BlockSpec(memory_space=pltpu.VMEM)
 SM = pl.BlockSpec(memory_space=pltpu.SMEM)
+ANY = pl.BlockSpec(memory_space=pl.ANY)
 PARAMS = pltpu.CompilerParams(vmem_limit_bytes=40 * 1024 * 1024)
 
 
@@ -60,46 +61,66 @@
     return jnp.where(fine < FX, own, edge)
 
 
-def pack_kernel(level0, level4, fuel0, fuel4, wind, active, to_left, to_right, slots):
-    lane = lanes((FY, 128))
-    fuel_first = pltpu.roll(fuel0[...].astype(jnp.float32), HALF, 1)
-    fuel_last = pltpu.roll(fuel4[...].astype(jnp.float32), HALF, 1)
-    to_left[0:FY, :] = jnp.where(lane < HALF, level0[...], fuel_first)
-    to_right[0:FY, :] = jnp.where(lane >= HALF, level4[...], fuel_last)
+def strips_kernel(level, fuel, active, to_left, to_right, left_level, right_level, left_fuel, right_fuel, arrived):
+    first, last = pl.ds(0, 128), pl.ds(FX - 128, 128)
+    moves = [
+        pltpu.make_async_copy(source.at[:, part], buf, arrived.at[i])
+        for i, (source, part, buf) in enumerate((
+            (level, first, left_level), (fuel, first, left_fuel),
+            (level, last, right_level), (fuel, last, right_fuel),
+        ))
+    ]
+    for move in moves:
+        move.start()
     for k in range(8):
         row = jnp.full((1, 128), flag_of(active, k), jnp.float32)
         to_left[FY + k : FY + k + 1, :] = row
         to_right[FY + k : FY + k + 1, :] = row
+    lane = lanes((FY, 128))
+    moves[0].wait()
+    moves[1].wait()
+    to_left[0:FY, :] = jnp.where(
+        lane < HALF, left_level[...], pltpu.roll(left_fuel[...].astype(jnp.float32), HALF, 1)
+    )
+    moves[2].wait()
+    moves[3].wait()
+    to_right[0:FY, :] = jnp.where(
+        lane >= HALF, right_level[...], pltpu.roll(right_fuel[...].astype(jnp.float32), HALF, 1)
+    )
+
+
+def strips(level, fuel, active):
+    strip = pltpu.VMEM((FY, 128), jnp.float32)
+    kinds = pltpu.VMEM((FY, 128), jnp.int32)
+    return pl.pallas_call(
+        strips_kernel,
+        in_specs=[ANY, ANY, SM],
+        out_specs=[VM, VM],
+        out_shape=[f32(FY + 8, 128), f32(FY + 8, 128)],
+        scratch_shapes=[strip, strip, kinds, kinds, pltpu.SemaphoreType.DMA((4,))],
+        name="strips",
+    )(level, fuel, active)
+
+
+def flag_of(active, k):
+    return (active[0, 0, min(k, STEPS * SUBSTEPS - 1)] > 0).astype(jnp.float32)
+
+
+def blocks_kernel(wind, after, slots):
     parts = [wind[0, 0:8, :], wind[0, 8:16, :], wind[1, 0:8, :], wind[1, 8:16, :]]
     block = jnp.concatenate(parts, axis=1)
     for k in range(NX * NZ):
         slots[k] = block
 
 
-def flag_of(active, k):
-    return (active[0, 0, min(k, STEPS * SUBSTEPS - 1)] > 0).astype(jnp.float32)
-
-
-def whole(*s):
-    return pl.BlockSpec(s, lambda i: (0,) * len(s))
-
-
-def pack(level, fuel, wind, active):
-    edge0 = pl.BlockSpec((FY, 128), lambda i: (0, 0))
-    edge4 = pl.BlockSpec((FY, 128), lambda i: (0, FX // 128 - 1))
+def blocks_of(wind, after):
     return pl.pallas_call(
-        pack_kernel,
-        grid=(1,),
-        in_specs=[edge0, edge4, edge0, edge4, whole(2, AY, AX), SM],
-        out_specs=[whole(FY + 8, 128), whole(FY + 8, 128), whole(NX * NZ, 8, 128)],
-        out_shape=[f32(FY + 8, 128), f32(FY + 8, 128), f32(NX * NZ, 8, 128)],
-        name="pack",
-    )(level, level, fuel, fuel, wind, active)
+        blocks_kernel, in_specs=[VM, ANY], out_specs=VM, out_shape=f32(NX * NZ, 8, 128), name="blocks"
+    )(wind, after)
 
 
 def rows_kernel(
-    level_top, level_bottom, fuel_top, fuel_bottom, from_left, from_right, blocks, owner, active,
-    held, to_up, to_down,
+    level, fuel, from_left, from_right, blocks, owner, active, held, to_up, to_down,
 ):
     tile = lax.axis_index("tile")
     lane = lanes((HALO, 128))
@@ -116,12 +137,11 @@
         held[8 * q : 8 * q + 8, :] = jnp.where(
             lane8 < AX, own, jnp.where(is_left, one, jnp.where(is_right, two, 0.0))
         )
-    for out, level, fuel, start, cut, coarse in (
-        (to_up, level_top, fuel_top, 0, 0, 0),
-        (to_down, level_bottom, fuel_bottom, FY - HALO, 80 - HALO, AY - 3),
-    ):
-        out[0:HALO, 0:FX] = level[cut : cut + HALO, :]
-        out[HALO : 2 * HALO, 0:FX] = fuel[cut : cut + HALO, :].astype(jnp.float32)
+    for k in range(8):
+        held[2 * AY + k : 2 * AY + k + 1, :] = jnp.full((1, 128), flag_of(active, k), jnp.float32)
+    for out, start, coarse in ((to_up, 0, 0), (to_down, FY - HALO, AY - 3)):
+        out[0:HALO, 0:FX] = level[start : start + HALO, :]
+        out[HALO : 2 * HALO, 0:FX] = fuel[start : start + HALO, :].astype(jnp.float32)
         one = from_left[start : start + HALO, :]
         two = from_right[start : start + HALO, :]
         out[0:HALO, FX:COLS] = jnp.where(lane < HALF, two, one)
@@ -140,18 +160,15 @@
 
 
 def rows(level, fuel, from_left, from_right, blocks, owner, active):
-    top = pl.BlockSpec((80, FX), lambda i: (0, 0))
-    bottom = pl.BlockSpec((80, FX), lambda i: (FY // 80 - 1, 0))
     shape = (2 * HALO + 8, COLS)
     return pl.pallas_call(
         rows_kernel,
-        grid=(1,),
-        in_specs=[top, bottom, top, bottom, whole(FY + 8, 128), whole(FY + 8, 128),
-                  whole(NX * NZ, 8, 128), SM, SM],
-        out_specs=[whole(2 * AY, 128), whole(*shape), whole(*shape)],
-        out_shape=[f32(2 * AY, 128), f32(*shape), f32(*shape)],
+        in_specs=[VM] * 5 + [SM, SM],
+        out_specs=[VM, VM, VM],
+        out_shape=[f32(2 * AY + 8, 128), f32(*shape), f32(*shape)],
+        compiler_params=PARAMS,
         name="rows",
-    )(level, level, fuel, fuel, from_left, from_right, blocks, owner, active)
+    )(level, fuel, from_left, from_right, blocks, owner, active)
 
 
 def table(values):
@@ -166,9 +183,13 @@
     return jnp.take_along_axis(row, kinds, axis=1, mode="promise_in_bounds")
 
 
-def values_kernel(fuel, from_left, from_right, after, fuel_rate, fuel_wind, fuel_heat, rate, drift, heat):
+def values_kernel(
+    fuel, from_left, from_right, after, fuel_rate, fuel_wind, fuel_heat, rate, drift, heat, three
+):
     lane8 = lanes((8, 128))
     tables = [(table(fuel_rate), rate), (table(fuel_wind), drift), (table(fuel_heat), heat)]
+    for i in range(3):
+        three[8 * i : 8 * i + 8, :] = tables[i][0]
 
     def own_rows(i, _):
         at = pl.multiple_of(i * 8, 8)
@@ -187,17 +208,16 @@
 def values(fuel, from_left, from_right, after, *names):
     return pl.pallas_call(
         values_kernel,
-        in_specs=[VM, VM, VM, pl.BlockSpec(memory_space=pl.ANY), SM, SM, SM],
-        out_specs=[VM, VM, VM],
-        out_shape=[f32(FY, COLS)] * 3,
+        in_specs=[VM, VM, VM, ANY, SM, SM, SM],
+        out_specs=[VM] * 4,
+        out_shape=[f32(FY, COLS)] * 3 + [f32(24, 128)],
         compiler_params=PARAMS,
         name="values",
     )(fuel, from_left, from_right, after, *names)
 
 
 def slab_kernel(
-    level, from_left, from_right, from_up, from_down, held, rate, drift, heat,
-    active, fuel_rate, fuel_wind, fuel_heat,
+    level, from_left, from_right, from_up, from_down, held, rate, drift, heat, three,
     level_out, slots,
     phi_a, phi_b, phi_c, edge_rate, edge_drift, edge_heat, east, north, winds, gates, sums, spread, gather,
 ):
@@ -226,7 +246,9 @@
         return 0
 
     lax.fori_loop(0, FY // 8, own_rows, 0, unroll=4)
-    tables = [(table(fuel_rate), edge_rate), (table(fuel_wind), edge_drift), (table(fuel_heat), edge_heat)]
+    tables = [
+        (three[8 * i : 8 * i + 8, :], out) for i, out in enumerate((edge_rate, edge_drift, edge_heat))
+    ]
 
     def halo_rows(i, _):
         at = pl.multiple_of(i * 8, 8)
@@ -243,8 +265,8 @@
 
     gates[0:8, :] = from_up[2 * HALO : 2 * HALO + 8, :]
     gates[16:24, :] = from_down[2 * HALO : 2 * HALO + 8, :]
-    for k in range(STEPS * SUBSTEPS):
-        gates[8 + k : 9 + k, 0:FX] = jnp.full((1, FX), flag_of(active, k), jnp.float32)
+    for c in range(FX // 128):
+        gates[8:16, 128 * c : 128 * c + 128] = held[2 * AY : 2 * AY + 8, :]
     gates[8:16, FX:COLS] = jnp.where(
         lane8 < HALF, from_right[FY : FY + 8, :], from_left[FY : FY + 8, :]
     )
@@ -434,7 +456,7 @@
     edge = pltpu.VMEM((2 * HALO, COLS), jnp.float32)
     return pl.pallas_call(
         slab_kernel,
-        in_specs=[VM] * 9 + [SM] * 4,
+        in_specs=[VM] * 10,
         out_specs=[VM, VM],
         out_shape=[f32(FY, FX), f32(NX * NZ, 4, 128)],
         scratch_shapes=[big] * 3
@@ -484,18 +506,17 @@
 
 def shards(level, fuel, wind, owner, active, fuel_rate, fuel_wind, fuel_heat):
     active = jnp.transpose(active, (1, 2, 0))
-    tables = (fuel_rate, fuel_wind, fuel_heat)
-    to_left, to_right, blocks = pack(level, fuel, wind, active)
+    to_left, to_right = strips(level, fuel, active)
     from_right = shift(to_left, "tile", -1)
     from_left = shift(to_right, "tile", 1)
+    blocks = blocks_of(wind, to_left)
+    blocks, from_left, from_right = lax.optimization_barrier((blocks, from_left, from_right))
     blocks = lax.all_to_all(blocks, "tile", 0, 0, tiled=True)
     held, to_up, to_down = rows(level, fuel, from_left, from_right, blocks, owner, active)
     from_down = shift(to_up, "grp", -1)
     from_up = shift(to_down, "grp", 1)
-    rate, drift, heat = values(fuel, from_left, from_right, held, *tables)
-    level_out, flux = slab(
-        level, from_left, from_right, from_up, from_down, held, rate, drift, heat, active, *tables
-    )
+    coefficients = values(fuel, from_left, from_right, held, fuel_rate, fuel_wind, fuel_heat)
+    level_out, flux = slab(level, from_left, from_right, from_up, from_down, held, *coefficients)
     flux = lax.all_to_all(flux, "tile", 0, 0, tiled=True)
     return (level_out, final(owner, flux, wind))
 

time: 98.3 us -> 101 us (1.027)
  blocking collectives: 23.2 us -> 55.9 us
  starting transfers between devices: 32.1 us -> 15.2 us
  waiting for transfers between devices: 15.8 us -> 7.16 us
  local copies, waits for them, and re-layouts: 3.92 us -> 0.04 us
    all_to_all x0 -> x1, blocking collectives: none -> 36.3 us  [shards(): blocks = lax.all_to_all(blocks, 'tile', 0, 0, tiled=True)]
    all_to_all x1 -> x0, starting transfers between devices: 19.2 us -> none  [shards(): blocks = lax.all_to_all(blocks, 'tile', 0, 0, tiled=True)]
    ppermute x4, waiting for transfers between devices: 12.3 us -> 7.16 us  [shift(): return lax.ppermute(value, axis, pairs)]
    unnamed x30 -> x14, local copies, waits for them, and re-layouts: 3.92 us -> 0.04 us
    all_to_all x1, blocking collectives: 23.2 us -> 19.5 us  [shards(): flux = lax.all_to_all(flux, 'tile', 0, 0, tiled=True)]
    all_to_all x1 -> x0, waiting for transfers between devices: 3.44 us -> none  [shards(): blocks = lax.all_to_all(blocks, 'tile', 0, 0, tiled=True)]
    ppermute x4, starting transfers between devices: 12.9 us -> 15.2 us  [shift(): return lax.ppermute(value, axis, pairs)]
    pallas_call x4 -> x5, Pallas kernels: 19.6 us -> 19.5 us  [the longest x1 11.7 us: slab(): pl.pallas_call(slab_kernel, in_specs=[VM] * 10, out_specs=[VM, VM], out_s...]
  transfers between devices with their start and end apart: 5 -> 4, of which waited for: 4 -> 2; matrix products, arithmetic and copies ran while one was open for 0% -> 0% of each run, Pallas kernels for 3% -> 4%
where the time goes in v3:
time: 101 us; the launch traced here: 100 us
  blocking collectives  55.9 us (55%)
  Pallas kernels  21.2 us (21%)
  starting transfers between devices  15.2 us (15%)
  waiting for transfers between devices  7.16 us (7%)
    all_to_all x1, blocking collectives, shards(): blocks = lax.all_to_all(blocks, 'tile', 0, 0, tiled=True)  36.3 us
    all_to_all x1, blocking collectives, shards(): flux = lax.all_to_all(flux, 'tile', 0, 0, tiled=True)  19.5 us
    ppermute x4, starting transfers between devices, shift(): return lax.ppermute(value, axis, pairs)  15.2 us
    pallas_call x1, Pallas kernels, slab(): pl.pallas_call(slab_kernel, in_specs=[VM] * 10, out_specs=[VM, VM], out_s...  11.7 us
    ppermute x4, waiting for transfers between devices, shift(): return lax.ppermute(value, axis, pairs)  7.16 us
    pallas_call x1, Pallas kernels, values(): pl.pallas_call(values_kernel, in_specs=[VM, VM, VM, ANY, SM, SM, SM], out...  2.87 us
    pallas_call x1, Pallas kernels, strips(): pl.pallas_call(strips_kernel, in_specs=[ANY, ANY, SM], out_specs=[VM, VM]...  2.77 us
  transfers between devices with their start and end apart: 4, of which 2 were waited for; matrix products, arithmetic and copies ran while one was open for 0% of the time, Pallas kernels for 4%

profile of v3, /device:TPU:1, one launch (start us, length us, event | category | flops | bytes accessed | tf_op | source)
XLA Modules:
  0.0 100.2 jit_solution(1443550153564891436)
XLA Ops:
  0.6 0.0 copy-start.1
  0.6 2.8 %strips.1 = (f32[328,128]{1,0:T(8,128)}, f32[328,128]{1,0:T(8,128)}) custom-call(f32[320,640]{1,0:T(8,128)} %level.5, s32[320,640]{1,0:T(8,128)} %fuel.5, s32[1,1,4]{2,1,0:T(1,128)} %bitcast.1), custom_call_target="tpu_custom_call" | custom-call | tf_op jit(solution)/shard_map/strips/pallas_call | solution.py:95
  3.4 0.0 copy-start
  3.4 4.5 %collective-permute-start = (f32[328,128]{1,0:T(8,128)}, f32[328,128]{1,0:T(8,128)S(1)}, u32[]{:S(2)}, u32[]{:S(2)}) collective-permute-start(f32[328,128]{1,0:T(8,128)} %get-tuple-element.17), channel_id=1, source_target_pairs={{0,1},{1,2},{2,3},{3,4},{4,5},{5,6},{6,7},{7,8},{8,9},{9,10},{10,1... | collective-permute-start | bytes 503816 | tf_op jit(solution)/shard_map/ppermute | solution.py:504
  7.9 1.3 %collective-permute-start.1 = (f32[328,128]{1,0:T(8,128)}, f32[328,128]{1,0:T(8,128)S(1)}, u32[]{:S(2)}, u32[]{:S(2)}) collective-permute-start(f32[328,128]{1,0:T(8,128)} %get-tuple-element.16.after), channel_id=1, source_target_pairs={{1,0},{2,1},{3,2},{4,3},{5,4},{6,5},{7,6},{8,7},{9,8},{10,9},{11,1... | collective-permute-start | bytes 503816 | tf_op jit(solution)/shard_map/ppermute | solution.py:504
  9.2 1.5 %blocks.1 = f32[64,8,128]{2,1,0:T(8,128)} custom-call(f32[2,16,32]{2,1,0:T(8,128)} %wind.3, f32[328,128]{1,0:T(8,128)} %get-tuple-element.16.after), custom_call_target="tpu_custom_call" | custom-call | tf_op jit(solution)/shard_map/blocks/pallas_call | solution.py:117
  10.8 0.0 copy-start.2
  10.8 0.0 copy-start.3
  10.8 0.0 collective-permute-done.from_left
  10.8 3.7 %collective-permute-done.1.from_right = f32[328,128]{1,0:T(8,128)S(1)} collective-permute-done((f32[328,128]{1,0:T(8,128)}, f32[328,128]{1,0:T(8,128)S(1)}, u32[]{:S(2)}, u32[]{:S(2)}) %collective-permute-start.1) | collective-permute-done | bytes 167968 | tf_op jit(solution)/shard_map/ppermute | solution.py:504
  14.4 36.3 %all_to_all.10.blocks = f32[64,8,128]{2,1,0:T(8,128)S(1)} all-to-all(f32[64,8,128]{2,1,0:T(8,128)} %blocks.1), channel_id=1, replica_groups=mesh['grp'=8,'tile'=64] {'tile'}, dimensions={0} | all-to-all | bytes 524288 | tf_op jit(solution)/shard_map/all_to_all | solution.py:514
  50.8 0.0 copy-done.1
  50.8 0.0 copy-done
  50.8 0.0 copy-done.2
  50.8 0.0 copy-done.3
  50.8 0.6 rows.1
  51.5 7.3 %collective-permute-start.2 = (f32[104,768]{1,0:T(8,128)S(1)}, f32[104,768]{1,0:T(8,128)S(1)}, u32[]{:S(2)}, u32[]{:S(2)}) collective-permute-start(f32[104,768]{1,0:T(8,128)S(1)} %get-tuple-element.21), channel_id=1, source_target_pairs={{0,64},{64,128},{128,192},{192,256},{256,320},{320,384},{384,448},... | collective-permute-start | bytes 958472 | tf_op jit(solution)/shard_map/ppermute | solution.py:504
  58.8 0.0 copy-start.4
  58.8 0.0 copy-start.5
  58.8 0.0 copy-start.6
  58.8 2.1 %collective-permute-start.3 = (f32[104,768]{1,0:T(8,128)S(1)}, f32[104,768]{1,0:T(8,128)S(1)}, u32[]{:S(2)}, u32[]{:S(2)}) collective-permute-start(f32[104,768]{1,0:T(8,128)S(1)} %get-tuple-element.22), channel_id=1, source_target_pairs={{64,0},{128,64},{192,128},{256,192},{320,256},{384,320},{448,384},... | collective-permute-start | bytes 958472 | tf_op jit(solution)/shard_map/ppermute | solution.py:504
  60.9 0.0 copy-done.4
  60.9 0.0 copy-done.5
  60.9 0.0 copy-done.6
  60.9 2.9 %values.1 = (f32[320,768]{1,0:T(8,128)S(1)}, f32[320,768]{1,0:T(8,128)S(1)}, f32[320,768]{1,0:T(8,128)S(1)}, f32[24,128]{1,0:T(8,128)S(1)}) custom-call(s32[320,640]{1,0:T(8,128)S(1)} %copy-done.1, f32[328,128]{1,0:T(8,128)S(1)} %collective-permute-done.from_left, f32[328,128]{1,0:T(8,128)S(1)} %collective-permute-done.1.from_right, ...), custom_call_target="tpu_custom_call" | custom-call | tf_op jit(solution)/shard_map/values/pallas_call | solution.py:209
  63.7 0.0 collective-permute-done.2.from_up
  63.8 3.5 %collective-permute-done.3.from_down = f32[104,768]{1,0:T(8,128)S(1)} collective-permute-done((f32[104,768]{1,0:T(8,128)S(1)}, f32[104,768]{1,0:T(8,128)S(1)}, u32[]{:S(2)}, u32[]{:S(2)}) %collective-permute-start.3) | collective-permute-done | bytes 319520 | tf_op jit(solution)/shard_map/ppermute | solution.py:504
  67.2 11.7 %slab.1 = (f32[320,640]{1,0:T(8,128)}, f32[64,4,128]{2,1,0:T(4,128)S(1)}) custom-call(f32[320,640]{1,0:T(8,128)S(1)} %copy-done, f32[328,128]{1,0:T(8,128)S(1)} %collective-permute-done.from_left, f32[328,128]{1,0:T(8,128)S(1)} %collective-permute-done.1.from_right, f32[104,768]{1,0:T(8,128)S(1)} %collective-permute-done.2.from_up, ...), custom_call_target="tpu_custom_call" | custom-call | tf_op jit(solution)/shard_map/slab/pallas_call | solution.py:457
  78.9 19.5 %all_to_all.11.received = f32[64,4,128]{2,1,0:T(4,128)} all-to-all(f32[64,4,128]{2,1,0:T(4,128)S(1)} %get-tuple-element.29), channel_id=1, replica_groups=mesh['grp'=8,'tile'=64] {'tile'}, dimensions={0} | all-to-all | bytes 262144 | tf_op jit(solution)/shard_map/all_to_all | solution.py:520
  98.4 1.7 %final.1 = f32[2,16,32]{2,1,0:T(8,128)} custom-call(s32[1,64]{1,0:T(1,128)} %owner.3, f32[64,4,128]{2,1,0:T(4,128)} %all_to_all.11.received, f32[2,16,32]{2,1,0:T(8,128)} %wind.3), custom_call_target="tpu_custom_call" | custom-call | tf_op jit(solution)/shard_map/final/pallas_call | solution.py:496
Async XLA Ops:
  0.6 50.1 %copy-start.1 = (s32[320,640]{1,0:T(8,128)S(1)}, s32[320,640]{1,0:T(8,128)}, u32[]{:S(2)}) copy-start(s32[320,640]{1,0:T(8,128)} %fuel.5) | copy-start | bytes 2457604
  3.4 47.4 %copy-start = (f32[320,640]{1,0:T(8,128)S(1)}, f32[320,640]{1,0:T(8,128)}, u32[]{:S(2)}) copy-start(f32[320,640]{1,0:T(8,128)} %level.5) | copy-start | bytes 2457604
  3.4 7.3 %collective-permute-start = (f32[328,128]{1,0:T(8,128)}, f32[328,128]{1,0:T(8,128)S(1)}, u32[]{:S(2)}, u32[]{:S(2)}) collective-permute-start(f32[328,128]{1,0:T(8,128)} %get-tuple-element.17), channel_id=1, source_target_pairs={{0,1},{1,2},{2,3},{3,4},{4,5},{5,6},{6,7},{7,8},{8,9},{9,10},{10,1... | collective-permute-start | bytes 503816 | tf_op jit(solution)/shard_map/ppermute | solution.py:504
  7.9 6.5 %collective-permute-start.1 = (f32[328,128]{1,0:T(8,128)}, f32[328,128]{1,0:T(8,128)S(1)}, u32[]{:S(2)}, u32[]{:S(2)}) collective-permute-start(f32[328,128]{1,0:T(8,128)} %get-tuple-element.16.after), channel_id=1, source_target_pairs={{1,0},{2,1},{3,2},{4,3},{5,4},{6,5},{7,6},{8,7},{9,8},{10,9},{11,1... | collective-permute-start | bytes 503816 | tf_op jit(solution)/shard_map/ppermute | solution.py:504
  10.8 40.0 %copy-start.2 = (s32[4,1,1]{0,2,1:T(1,128)S(1)}, s32[4,1,1]{0,2,1:T(1,128)}, u32[]{:S(2)}) copy-start(s32[4,1,1]{0,2,1:T(1,128)} %param.12) | copy-start | bytes 52
  10.8 40.0 %copy-start.3 = (s32[1,64]{1,0:T(1,128)S(1)}, s32[1,64]{1,0:T(1,128)}, u32[]{:S(2)}) copy-start(s32[1,64]{1,0:T(1,128)} %owner.3) | copy-start | bytes 772
  51.5 12.3 %collective-permute-start.2 = (f32[104,768]{1,0:T(8,128)S(1)}, f32[104,768]{1,0:T(8,128)S(1)}, u32[]{:S(2)}, u32[]{:S(2)}) collective-permute-start(f32[104,768]{1,0:T(8,128)S(1)} %get-tuple-element.21), channel_id=1, source_target_pairs={{0,64},{64,128},{128,192},{192,256},{256,320},{320,384},{384,448},... | collective-permute-start | bytes 958472 | tf_op jit(solution)/shard_map/ppermute | solution.py:504
  58.8 2.1 %copy-start.4 = (f32[13]{0:T(128)S(1)}, f32[13]{0:T(128)}, u32[]{:S(2)}) copy-start(f32[13]{0:T(128)} %fuel_rate.1) | copy-start | bytes 160
  58.8 2.1 %copy-start.5 = (f32[13]{0:T(128)S(1)}, f32[13]{0:T(128)}, u32[]{:S(2)}) copy-start(f32[13]{0:T(128)} %fuel_wind.1) | copy-start | bytes 160
  58.8 2.1 %copy-start.6 = (f32[13]{0:T(128)S(1)}, f32[13]{0:T(128)}, u32[]{:S(2)}) copy-start(f32[13]{0:T(128)} %fuel_heat.1) | copy-start | bytes 160
  58.8 8.4 %collective-permute-start.3 = (f32[104,768]{1,0:T(8,128)S(1)}, f32[104,768]{1,0:T(8,128)S(1)}, u32[]{:S(2)}, u32[]{:S(2)}) collective-permute-start(f32[104,768]{1,0:T(8,128)S(1)} %get-tuple-element.22), channel_id=1, source_target_pairs={{64,0},{128,64},{192,128},{256,192},{320,256},{384,320},{448,384},... | collective-permute-start | bytes 958472 | tf_op jit(solution)/shard_map/ppermute | solution.py:504

commit v4 on v3

v4 whole, which is shorter than its diff:
```python
import jax
import jax.numpy as jnp
from jax import lax
from jax.experimental import pallas as pl
from jax.experimental.pallas import tpu as pltpu
from jax.sharding import PartitionSpec as P

R = 20
AY = 16
AX = 32
FY = 320
FX = 640
STEPS = 2
SUBSTEPS = 2
NZ = 16
NX = 4
HALO = 48
HALF = 64
PAD = 8
TOP = PAD + HALO
ROWS = TOP + FY + HALO + PAD
COLS = FX + 2 * HALF
NL = COLS // 128
RIGHT = 40
LEFT = 51
CR = 24

VM = pl.BlockSpec(memory_space=pltpu.VMEM)
SM = pl.BlockSpec(memory_space=pltpu.SMEM)
ANY = pl.BlockSpec(memory_space=pl.ANY)
SMALL = pltpu.CompilerParams(vmem_limit_bytes=4 * 1024 * 1024)
LARGE = pltpu.CompilerParams(vmem_limit_bytes=12 * 1024 * 1024)


def lanes(shape):
    return lax.broadcasted_iota(jnp.int32, shape, 1)


def f32(*shape):
    return jax.ShapeDtypeStruct(shape, jnp.float32)


def thirds(x):
    high = x.astype(jnp.bfloat16)
    rest = x - high.astype(jnp.float32)
    middle = rest.astype(jnp.bfloat16)
    low = (rest - middle.astype(jnp.float32)).astype(jnp.bfloat16)
    return jnp.concatenate([high, middle, low], axis=0)


def exact_dot(x, onehot):
    n = x.shape[0]
    out = jnp.dot(thirds(x), onehot, preferred_element_type=jnp.float32)
    return out[:n] + out[n : 2 * n] + out[2 * n :]


def coarse_lane(fine):
    own = fine // R
    right = RIGHT + (fine - FX) // R
    left = LEFT - (COLS - 1 - fine) // R
    edge = jnp.where(fine < FX + 3 * R, right, jnp.where(fine >= COLS - 3 * R, left, -1))
    return jnp.where(fine < FX, own, edge)


def strips_kernel(level, fuel, active, after, to_left, to_right, done, left_level, right_level, left_fuel, right_fuel, arrived):
    first, last = pl.ds(0, 128), pl.ds(FX - 128, 128)
    moves = [
        pltpu.make_async_copy(source.at[:, part], buf, arrived.at[i])
        for i, (source, part, buf) in enumerate((
            (level, first, left_level), (fuel, first, left_fuel),
            (level, last, right_level), (fuel, last, right_fuel),
        ))
    ]
    for move in moves:
        move.start()
    done[...] = jnp.zeros((8, 128), jnp.float32)
    for k in range(8):
        row = jnp.full((1, 128), flag_of(active, k), jnp.float32)
        to_left[FY + k : FY + k + 1, :] = row
        to_right[FY + k : FY + k + 1, :] = row
    lane = lanes((FY, 128))
    moves[0].wait()
    moves[1].wait()
    to_left[0:FY, :] = jnp.where(
        lane < HALF, left_level[...], pltpu.roll(left_fuel[...].astype(jnp.float32), HALF, 1)
    )
    moves[2].wait()
    moves[3].wait()
    to_right[0:FY, :] = jnp.where(
        lane >= HALF, right_level[...], pltpu.roll(right_fuel[...].astype(jnp.float32), HALF, 1)
    )


def strips(level, fuel, active, after):
    strip = pltpu.VMEM((FY, 128), jnp.float32)
    kinds = pltpu.VMEM((FY, 128), jnp.int32)
    return pl.pallas_call(
        strips_kernel,
        in_specs=[ANY, ANY, SM, ANY],
        out_specs=[VM, VM, VM],
        out_shape=[f32(FY + 8, 128), f32(FY + 8, 128), f32(8, 128)],
        scratch_shapes=[strip, strip, kinds, kinds, pltpu.SemaphoreType.DMA((4,))],
        name="strips",
    )(level, fuel, active, after)


def flag_of(active, k):
    return (active[0, 0, min(k, STEPS * SUBSTEPS - 1)] > 0).astype(jnp.float32)


def blocks_kernel(wind, slots):
    parts = [wind[0, 0:8, :], wind[0, 8:16, :], wind[1, 0:8, :], wind[1, 8:16, :]]
    block = jnp.concatenate(parts, axis=1)
    for k in range(NX * NZ):
        slots[k] = block


def blocks_of(wind):
    return pl.pallas_call(
        blocks_kernel, in_specs=[VM], out_specs=VM, out_shape=f32(NX * NZ, 8, 128), name="blocks"
    )(wind)


def rows_kernel(
    from_left, from_right, blocks, owner, active, up, down, held, to_up, to_down,
):
    tile = lax.axis_index("tile")
    lane = lanes((HALO, 128))
    lane8 = lanes((8, 128))
    main = blocks[owner[0, tile]]
    left = blocks[owner[0, jnp.maximum(tile - 1, 0)]]
    right = blocks[owner[0, jnp.minimum(tile + 1, NX * NZ - 1)]]
    is_left = jnp.logical_and(lane8 >= LEFT - 2, lane8 <= LEFT)
    is_right = jnp.logical_and(lane8 >= RIGHT, lane8 <= RIGHT + 2)
    for q in range(4):
        own = pltpu.roll(main, (128 - 32 * q) % 128, 1)
        one = pltpu.roll(left, (LEFT - 31 - 32 * q) % 128, 1)
        two = pltpu.roll(right, (RIGHT - 32 * q) % 128, 1)
        held[8 * q : 8 * q + 8, :] = jnp.where(
            lane8 < AX, own, jnp.where(is_left, one, jnp.where(is_right, two, 0.0))
        )
    for k in range(8):
        held[2 * AY + k : 2 * AY + k + 1, :] = jnp.full((1, 128), flag_of(active, k), jnp.float32)
    for out, part, start, coarse in ((to_up, up, 0, 0), (to_down, down, FY - HALO, AY - 3)):
        out[0 : 2 * HALO, 0:FX] = part[...]
        one = from_left[start : start + HALO, :]
        two = from_right[start : start + HALO, :]
        out[0:HALO, FX:COLS] = jnp.where(lane < HALF, two, one)
        out[HALO : 2 * HALO, FX:COLS] = pltpu.roll(jnp.where(lane < HALF, one, two), HALF, 1)
        for k in range(4):
            row = 2 * HALO + k
            out[row : row + 1, 0:FX] = jnp.full((1, FX), flag_of(active, k), jnp.float32)
            out[row : row + 1, FX:COLS] = jnp.where(
                lane[0:1] < HALF, from_right[FY + k : FY + k + 1, :], from_left[FY + k : FY + k + 1, :]
            )
        row = 2 * HALO + 4
        for c in range(6):
            at = (c // 3) * AY + coarse + c % 3
            out[row : row + 1, 128 * c : 128 * c + 128] = held[at : at + 1, :]
        out[row + 1 : row + 4, :] = jnp.zeros((3, COLS), jnp.float32)


def rows(from_left, from_right, blocks, owner, active, up, down):
    shape = (2 * HALO + 8, COLS)
    return pl.pallas_call(
        rows_kernel,
        in_specs=[VM] * 3 + [SM, SM, VM, VM],
        out_specs=[VM, VM, VM],
        out_shape=[f32(2 * AY + 8, 128), f32(*shape), f32(*shape)],
        compiler_params=SMALL,
        name="rows",
    )(from_left, from_right, blocks, owner, active, up, down)


def table(values):
    lane = lanes((8, 128))
    row = jnp.zeros((8, 128), jnp.float32)
    for c in range(values.shape[0]):
        row = jnp.where(lane == c, values[c], row)
    return row


def look(row, kinds):
    return jnp.take_along_axis(row, kinds, axis=1, mode="promise_in_bounds")


def values_kernel(
    level, fuel, after, fuel_rate, fuel_wind, fuel_heat, rate, drift, three, to_up, to_down, kinds, arrived
):
    moves = [
        pltpu.make_async_copy(source, buf, arrived.at[i])
        for i, (source, buf) in enumerate((
            (fuel, kinds),
            (level.at[0:HALO, :], to_up.at[0:HALO, :]),
            (level.at[FY - HALO : FY, :], to_down.at[0:HALO, :]),
        ))
    ]
    for move in moves:
        move.start()
    tables = [table(fuel_rate), table(fuel_wind), table(fuel_heat)]
    for i in range(3):
        three[8 * i : 8 * i + 8, :] = tables[i]
    moves[0].wait()
    for out, start in ((to_up, 0), (to_down, FY - HALO)):
        out[HALO : 2 * HALO, :] = kinds[start : start + HALO, :].astype(jnp.float32)

    def own_rows(i):
        at = pl.multiple_of(i * 8, 8)
        return [(kinds[pl.ds(at, 8), c : c + 128], at, c) for c in range(0, FX, 128)]

    look_edges(own_rows, tables[0:2], (rate, drift), FY // 8)
    moves[1].wait()
    moves[2].wait()


def values(level, fuel, after, *names):
    shape = (2 * HALO, FX)
    return pl.pallas_call(
        values_kernel,
        in_specs=[ANY, ANY, ANY, SM, SM, SM],
        out_specs=[VM] * 5,
        out_shape=[f32(FY, FX)] * 2 + [f32(24, 128), f32(*shape), f32(*shape)],
        scratch_shapes=[pltpu.VMEM((FY, FX), jnp.int32), pltpu.SemaphoreType.DMA((3,))],
        name="values",
    )(level, fuel, after, *names)


def look_edges(source, tables, outs, steps):
    def body(i, _):
        for kinds, at, col in source(i):
            for row, out in zip(tables, outs):
                out[pl.ds(at, 8), col : col + 128] = look(row, kinds)
        return 0

    lax.fori_loop(0, steps, body, 0, unroll=min(steps, 4))


def level_rows(phi, first, level, from_left, from_right):
    lane8 = lanes((8, 128))

    def own_rows(i, _):
        at = pl.multiple_of(i * 8, 8)
        to = pl.multiple_of(i * 8 + first, 8)
        phi[pl.ds(to, 8), 0:FX] = level[pl.ds(at, 8), :]
        one = from_left[pl.ds(at, 8), :]
        two = from_right[pl.ds(at, 8), :]
        phi[pl.ds(to, 8), FX:COLS] = jnp.where(lane8 < HALF, two, one)
        return 0

    lax.fori_loop(0, FY // 8, own_rows, 0, unroll=4)


def own_flags(out, held, from_left, from_right):
    for c in range(FX // 128):
        out[:, 128 * c : 128 * c + 128] = held[2 * AY : 2 * AY + 8, :]
    out[:, FX:COLS] = jnp.where(
        lanes((8, 128)) < HALF, from_right[FY : FY + 8, :], from_left[FY : FY + 8, :]
    )


def spread_matrix():
    return (
        coarse_lane(lanes((128, COLS))) == lax.broadcasted_iota(jnp.int32, (128, COLS), 0)
    ).astype(jnp.bfloat16)


def expand(winds, spread, east, north):
    wide = exact_dot(winds[...], spread[...])
    rows_each = winds.shape[0] // 2
    for comp, out in ((0, east), (1, north)):
        part = wide[comp * rows_each : comp * rows_each + rows_each]
        out[0:rows_each, :] = jnp.maximum(part, 0.0)
        out[rows_each : 2 * rows_each, :] = jnp.minimum(part, 0.0)


def edge_columns(phi):
    tile = lax.axis_index("tile")
    count = phi.shape[0]

    @pl.when(tile == 0)
    def _():
        old = phi[:, COLS - 128 : COLS]
        new = jnp.broadcast_to(phi[:, 0:1], (count, 128))
        phi[:, COLS - 128 : COLS] = jnp.where(lanes((count, 128)) == 127, new, old)

    @pl.when(tile == lax.axis_size("tile") - 1)
    def _():
        old = phi[:, FX : FX + 128]
        new = jnp.broadcast_to(phi[:, FX - 1 : FX], (count, 128))
        phi[:, FX : FX + 128] = jnp.where(lanes((count, 128)) == 0, new, old)


def fuel_value(refs, at):
    parts = [ref[pl.ds(at, 8), :] for ref in refs]
    return parts[0] if len(parts) == 1 else jnp.concatenate(parts, axis=1)


def update(phi, at, e, n, gate, fuels):
    sub8 = lax.broadcasted_iota(jnp.int32, (8, COLS), 0)
    before = phi[pl.ds(pl.multiple_of(at - 8, 8), 8), :]
    now = phi[pl.ds(at, 8), :]
    after = phi[pl.ds(pl.multiple_of(at + 8, 8), 8), :]
    south = jnp.where(sub8 == 0, pltpu.roll(before, 1, 0), pltpu.roll(now, 1, 0))
    above = jnp.where(sub8 == 7, pltpu.roll(after, 7, 0), pltpu.roll(now, 7, 0))
    west = pltpu.roll(now, 1, 1)
    east_cell = pltpu.roll(now, COLS - 1, 1)
    back_x = now - west
    ahead_x = east_cell - now
    back_y = now - south
    ahead_y = above - now
    bx = jnp.maximum(back_x, 0.0)
    ax = jnp.minimum(ahead_x, 0.0)
    by = jnp.maximum(back_y, 0.0)
    ay = jnp.minimum(ahead_y, 0.0)
    square = bx * bx + ax * ax + by * by + ay * ay + 1e-12
    slope = square * lax.rsqrt(square)
    carry = e[0] * back_x + e[1] * ahead_x + n[0] * back_y + n[1] * ahead_y
    there = pl.multiple_of(at - fuels[3], 8)
    change = fuel_value(fuels[0], there) * slope + fuel_value(fuels[1], there) * carry
    return now - gate * change


def wind_row(ref, row):
    half = ref.shape[0] // 2
    return tuple(jnp.broadcast_to(ref[pl.ds(row + part, 1), :], (8, COLS)) for part in (0, half))


def mix(a, b):
    sub8 = lax.broadcasted_iota(jnp.int32, (8, COLS), 0)
    return tuple(jnp.where(sub8 < 4, one, two) for one, two in zip(a, b))


def band(phi, at, row, winds, gate, fuels, finish):
    east, north = winds
    for t in range(5):
        if t == 2:
            e = mix(wind_row(east, row), wind_row(east, row + 1))
            n = mix(wind_row(north, row), wind_row(north, row + 1))
        else:
            e, n = (wind_row(ref, row + t // 3) for ref in (east, north))
        here = pl.multiple_of(at + 8 * t, 8)
        finish(here, update(phi, here, e, n, gate, fuels), fuels)


def early_kernel(
    level, fuel, from_left, from_right, held, rate, drift, three, once, heat, side_rate, side_drift, side_heat,
    phi, east, north, winds, gates, spread,
):
    lane8 = lanes((8, 128))
    tables = [three[8 * i : 8 * i + 8, :] for i in range(3)]

    def beside(i):
        at = pl.multiple_of(i * 8, 8)
        kinds = jnp.where(lane8 < HALF, from_left[pl.ds(at, 8), :], from_right[pl.ds(at, 8), :])
        return [(pltpu.roll(kinds, HALF, 1).astype(jnp.int32), at, 0)]

    def own_rows(i):
        at = pl.multiple_of(i * 8, 8)
        return [(fuel[pl.ds(at, 8), c : c + 128], at, c) for c in range(0, FX, 128)]

    look_edges(beside, tables, (side_rate, side_drift, side_heat), FY // 8)
    look_edges(own_rows, tables[2:3], (heat,), FY // 8)
    phi[0:8, :] = jnp.zeros((8, COLS), jnp.float32)
    phi[FY + 8 : FY + 16, :] = jnp.zeros((8, COLS), jnp.float32)
    level_rows(phi, 8, level, from_left, from_right)
    own_flags(gates, held, from_left, from_right)
    winds[...] = held[0 : 2 * AY, :]
    spread[...] = spread_matrix()
    expand(winds, spread, east, north)
    edge_columns(phi)
    gate = jnp.broadcast_to(gates[0:1, :], (8, COLS))
    fuels = ((rate, side_rate), (drift, side_drift), None, 8)

    def store(here, new, fuels):
        once[pl.ds(pl.multiple_of(here - 8, 8), 8), :] = new

    def step(m, _):
        at = pl.multiple_of(40 * m + 8, 8)
        band(phi, at, 2 * m, (east, north), gate, fuels, store)
        return 0

    lax.fori_loop(0, FY // 40, step, 0)


def early(*args):
    return pl.pallas_call(
        early_kernel,
        in_specs=[VM] * 8,
        out_specs=[VM] * 5,
        out_shape=[f32(FY, COLS), f32(FY, FX)] + [f32(FY, 128)] * 3,
        scratch_shapes=[
            pltpu.VMEM((FY + 16, COLS), jnp.float32),
            pltpu.VMEM((2 * AY, COLS), jnp.float32),
            pltpu.VMEM((2 * AY, COLS), jnp.float32),
            pltpu.VMEM((2 * AY, 128), jnp.float32),
            pltpu.VMEM((8, COLS), jnp.float32),
            pltpu.VMEM((128, COLS), jnp.bfloat16),
        ],
        compiler_params=SMALL,
        name="early",
    )(*args)


def slab_kernel(
    level, from_left, from_right, from_up, from_down, held, rate, drift, heat, three,
    once, side_rate, side_drift, side_heat,
    level_out, slots,
    phi_a, phi_b, phi_c, edge_rate, edge_drift, edge_heat, east, north, winds, gates, sums, spread, gather,
):
    group = lax.axis_index("grp")
    sub8 = lax.broadcasted_iota(jnp.int32, (8, COLS), 0)

    zero = jnp.zeros((PAD, COLS), jnp.float32)
    phi_a[0:PAD, :] = zero
    phi_a[ROWS - PAD : ROWS, :] = zero
    phi_a[TOP - HALO : TOP, :] = from_up[0:HALO, :]
    phi_a[TOP + FY : TOP + FY + HALO, :] = from_down[0:HALO, :]
    level_rows(phi_a, TOP, level, from_left, from_right)

    def halo(i):
        at = pl.multiple_of(i * 8, 8)
        found = []
        for source, start in ((from_up, 0), (from_down, HALO)):
            for c in range(NL):
                kinds = source[pl.ds(pl.multiple_of(at + HALO, 8), 8), 128 * c : 128 * c + 128]
                found.append((kinds.astype(jnp.int32), pl.multiple_of(at + start, 8), 128 * c))
        return found

    tables = [three[8 * i : 8 * i + 8, :] for i in range(3)]
    look_edges(halo, tables, (edge_rate, edge_drift, edge_heat), HALO // 8)

    gates[0:8, :] = from_up[2 * HALO : 2 * HALO + 8, :]
    gates[16:24, :] = from_down[2 * HALO : 2 * HALO + 8, :]
    own_flags(gates.at[8:16, :], held, from_left, from_right)

    row = 2 * HALO + 4
    for comp in range(2):
        base = comp * CR
        for c in range(3):
            at = 128 * (3 * comp + c)
            winds[base + c : base + c + 1, :] = from_up[row : row + 1, at : at + 128]
            below = base + 3 + AY + c
            winds[below : below + 1, :] = from_down[row : row + 1, at : at + 128]
        winds[base + 3 : base + 3 + AY, :] = held[AY * comp : AY * comp + AY, :]
        winds[base + 6 + AY : base + CR, :] = jnp.zeros((CR - 6 - AY, 128), jnp.float32)

    spread[...] = spread_matrix()
    gather[...] = (
        coarse_lane(lax.broadcasted_iota(jnp.int32, (COLS, 128), 0)) == lanes((COLS, 128))
    ).astype(jnp.bfloat16)

    def edges(phi):
        @pl.when(group == 0)
        def _():
            phi[TOP - 1 : TOP, :] = phi[TOP : TOP + 1, :]

        @pl.when(group == lax.axis_size("grp") - 1)
        def _():
            phi[TOP + FY : TOP + FY + 1, :] = phi[TOP + FY - 1 : TOP + FY, :]

        edge_columns(phi)

    own = ((rate, side_rate), (drift, side_drift), (heat, side_heat), TOP)
    upper_edge = ((edge_rate,), (edge_drift,), (edge_heat,), TOP - HALO)
    lower_edge = ((edge_rate,), (edge_drift,), (edge_heat,), TOP + FY - HALO)
    both = (east, north)

    def gate_row(region, k):
        return jnp.broadcast_to(gates[region * 8 + k : region * 8 + k + 1, :], (8, COLS))

    def forty(phi, m, k, region, fuels, finish):
        at = pl.multiple_of(2 * PAD + 40 * m, 8)
        band(phi, at, 2 * m + 1, both, gate_row(region, k), fuels, finish)

    def tile_rows(phi, out, at, row, region, k, fuels):
        new = update(phi, at, wind_row(east, row), wind_row(north, row), gate_row(region, k), fuels)
        out[at : at + 8, :] = new

    def own_bands(body):
        def step(m, _):
            body(m, 1, own)
            return 0

        lax.fori_loop(1, 9, step, 0)

    def store_to(out):
        def finish(here, new, fuels):
            out[pl.ds(here, 8), :] = new

        return finish

    def flux_band(before, phi, out, k):
        def body(m, region, fuels):
            parts = []

            def finish(here, new, fuels):
                if out is not None:
                    out[pl.ds(here, 8), :] = new
                else:
                    level_out[pl.ds(pl.multiple_of(here - TOP, 8), 8), :] = new[:, 0:FX]
                old = before[pl.ds(here, 8), :]
                there = pl.multiple_of(here - fuels[3], 8)
                parts.append(fuel_value(fuels[2], there) * (jnp.tanh(old) - jnp.tanh(new)))

            forty(phi, m, k, region, fuels, finish)
            low = parts[0] + parts[1] + jnp.where(sub8 < 4, parts[2], 0.0)
            high = parts[3] + parts[4] + jnp.where(sub8 >= 4, parts[2], 0.0)
            sums[pl.ds(2 * m + 1, 1), :] = jnp.sum(low, axis=0, keepdims=True)
            sums[pl.ds(2 * m + 2, 1), :] = jnp.sum(high, axis=0, keepdims=True)

        return body

    def pooled():
        return exact_dot(sums[...], gather[...]) * (0.5 / (R * R))

    lane_c = lanes((CR, 128))
    row_c = lax.broadcasted_iota(jnp.int32, (CR, 128), 0)
    sums[...] = jnp.zeros((CR, COLS), jnp.float32)

    expand(winds, spread, east, north)
    edges(phi_a)
    phi_b[TOP : TOP + FY, :] = once[...]
    tile_rows(phi_a, phi_b, PAD, 0, 0, 0, upper_edge)
    forty(phi_a, 0, 0, 0, upper_edge, store_to(phi_b))
    tile_rows(phi_a, phi_b, TOP, 3, 1, 0, own)
    tile_rows(phi_a, phi_b, TOP + FY - 8, AY + 2, 1, 0, own)
    forty(phi_a, 9, 0, 2, lower_edge, store_to(phi_b))
    tile_rows(phi_a, phi_b, ROWS - 2 * PAD, AY + 5, 2, 0, lower_edge)
    edges(phi_b)
    second = flux_band(phi_a, phi_b, phi_c, 1)
    second(0, 0, upper_edge)
    second(9, 2, lower_edge)
    own_bands(second)
    edges(phi_c)

    flux0 = pooled()
    ahead = jnp.where(jnp.logical_or(lane_c == AX - 1, lane_c == LEFT), flux0, pltpu.roll(flux0, 127, 1))
    back = jnp.where(jnp.logical_or(lane_c == 0, lane_c == RIGHT), flux0, pltpu.roll(flux0, 1, 1))
    last_rows = jnp.logical_or(row_c == 2, row_c == AY + 2)
    first_rows = jnp.logical_or(row_c == 3, row_c == AY + 3)
    below = jnp.where(last_rows, flux0, pltpu.roll(flux0, CR - 1, 0))
    upper = jnp.where(first_rows, flux0, pltpu.roll(flux0, 1, 0))
    winds[0:CR, :] = 0.9 * winds[0:CR, :] + 20.0 * (ahead - back)
    winds[CR : 2 * CR, :] = 0.9 * winds[CR : 2 * CR, :] + 20.0 * (below - upper)
    expand(winds, spread, east, north)

    tile_rows(phi_c, phi_b, TOP - 8, 2, 0, 2, upper_edge)
    tile_rows(phi_c, phi_b, TOP + FY, AY + 3, 2, 2, lower_edge)
    own_bands(lambda m, region, fuels: forty(phi_c, m, 2, region, fuels, store_to(phi_b)))
    edges(phi_b)
    own_bands(flux_band(phi_c, phi_b, None, 3))
    total = 0.9 * flux0 + pooled()

    packed = jnp.zeros((4, 128), jnp.float32)
    lane4 = lanes((4, 128))
    for q in range(4):
        moved = pltpu.roll(total, 32 * q, 1)[3 + 4 * q : 7 + 4 * q]
        packed = jnp.where(lane4 // AX == q, moved, packed)
    for k in range(NX * NZ):
        slots[k] = packed


def slab(*args):
    big = pltpu.VMEM((ROWS, COLS), jnp.float32)
    edge = pltpu.VMEM((2 * HALO, COLS), jnp.float32)
    return pl.pallas_call(
        slab_kernel,
        in_specs=[VM] * 14,
        out_specs=[VM, VM],
        out_shape=[f32(FY, FX), f32(NX * NZ, 4, 128)],
        scratch_shapes=[big] * 3
        + [edge] * 3
        + [
            pltpu.VMEM((2 * CR, COLS), jnp.float32),
            pltpu.VMEM((2 * CR, COLS), jnp.float32),
            pltpu.VMEM((2 * CR, 128), jnp.float32),
            pltpu.VMEM((CR, COLS), jnp.float32),
            pltpu.VMEM((CR, COLS), jnp.float32),
            pltpu.VMEM((128, COLS), jnp.bfloat16),
            pltpu.VMEM((COLS, 128), jnp.bfloat16),
        ],
        compiler_params=LARGE,
        name="slab",
    )(*args)


def final_kernel(owner, received, wind, wind_out):
    tile = lax.axis_index("tile")
    source = jnp.int32(0)
    for t in range(NX * NZ):
        source = jnp.where(owner[0, t] == tile, t, source)
    block = received[source]
    flux = jnp.concatenate([pltpu.roll(block, (128 - 32 * q) % 128, 1) for q in range(4)], axis=0)
    lane = lanes((AY, 128))
    row = lax.broadcasted_iota(jnp.int32, (AY, 128), 0)
    ahead = jnp.where(lane == AX - 1, flux, pltpu.roll(flux, 127, 1))
    back = jnp.where(lane == 0, flux, pltpu.roll(flux, 1, 1))
    below = jnp.where(row == AY - 1, flux, pltpu.roll(flux, AY - 1, 0))
    upper = jnp.where(row == 0, flux, pltpu.roll(flux, 1, 0))
    wind_out[0] = 0.81 * wind[0] + 20.0 * (ahead - back)[:, 0:AX]
    wind_out[1] = 0.81 * wind[1] + 20.0 * (below - upper)[:, 0:AX]


def final(owner, received, wind):
    return pl.pallas_call(
        final_kernel, in_specs=[SM, VM, VM], out_specs=VM, out_shape=f32(2, AY, AX),
        compiler_params=SMALL, name="final"
    )(owner, received, wind)


def shift(value, axis, step):
    size = lax.axis_size(axis)
    pairs = [(i, i + step) for i in range(size) if 0 <= i + step < size]
    return lax.ppermute(value, axis, pairs)


def shards(level, fuel, wind, owner, active, fuel_rate, fuel_wind, fuel_heat):
    active = jnp.transpose(active, (1, 2, 0))
    mine = blocks_of(wind)
    blocks = lax.all_to_all(mine, "tile", 0, 0, tiled=True)
    to_left, to_right, done = strips(level, fuel, active, mine)
    from_right = shift(to_left, "tile", -1)
    from_left = shift(to_right, "tile", 1)
    rate, drift, three, up, down = values(level, fuel, done, fuel_rate, fuel_wind, fuel_heat)
    held, to_up, to_down = rows(from_left, from_right, blocks, owner, active, up, down)
    from_down = shift(to_up, "grp", -1)
    from_up = shift(to_down, "grp", 1)
    once, heat, *sides = early(level, fuel, from_left, from_right, held, rate, drift, three)
    level_out, flux = slab(
        level, from_left, from_right, from_up, from_down, held, rate, drift, heat, three, once, *sides
    )
    flux = lax.all_to_all(flux, "tile", 0, 0, tiled=True)
    return (level_out, final(owner, flux, wind))


def solution(mesh):
    in_specs = (
        P("grp", "tile"),
        P("grp", "tile"),
        P(None, "grp", "tile"),
        P("grp", None),
        P(None, "grp", "tile"),
        P(),
        P(),
        P(),
    )
    out_specs = (P("grp", "tile"), P(None, "grp", "tile"))
    return jax.shard_map(shards, mesh=mesh, in_specs=in_specs, out_specs=out_specs, check_vma=False)
```

time: 101 us -> 94.7 us (0.938)
  blocking collectives: 55.9 us -> 23.2 us
  starting transfers between devices: 15.2 us -> 31.9 us
  Pallas kernels: 21.2 us -> 26.3 us
  local copies, waits for them, and re-layouts: 0.04 us -> 4.21 us
    all_to_all x1 -> x0, blocking collectives: 36.3 us -> none  [shards(): blocks = lax.all_to_all(blocks, 'tile', 0, 0, tiled=True)]
    all_to_all x0 -> x1, starting transfers between devices: none -> 19.1 us  [shards(): blocks = lax.all_to_all(mine, 'tile', 0, 0, tiled=True)]
    pallas_call x5 -> x6, Pallas kernels: 19.5 us -> 25 us  [the longest x1 10.1 us: slab(): pl.pallas_call(slab_kernel, in_specs=[VM] * 14, out_specs=[VM, VM], out_s...]
    unnamed x14 -> x24, local copies, waits for them, and re-layouts: 0.04 us -> 4.21 us
    all_to_all x1, blocking collectives: 19.5 us -> 23.2 us  [shards(): flux = lax.all_to_all(flux, 'tile', 0, 0, tiled=True)]
    all_to_all x0 -> x1, waiting for transfers between devices: none -> 2.61 us  [shards(): blocks = lax.all_to_all(mine, 'tile', 0, 0, tiled=True)]
    ppermute x4, waiting for transfers between devices: 7.16 us -> 4.57 us  [shift(): return lax.ppermute(value, axis, pairs)]
    ppermute x4, starting transfers between devices: 15.2 us -> 12.7 us  [shift(): return lax.ppermute(value, axis, pairs)]
  transfers between devices with their start and end apart: 4 -> 5, of which waited for: 2 -> 3; matrix products, arithmetic and copies ran while one was open for 0% -> 0% of each run, Pallas kernels for 4% -> 14%
where the time goes in v4:
time: 94.7 us; the launch traced here: 93.6 us
  starting transfers between devices  31.9 us (34%)
  Pallas kernels  26.3 us (28%)
  blocking collectives  23.2 us (24%)
  waiting for transfers between devices  7.18 us (8%)
  local copies, waits for them, and re-layouts  4.21 us (4%)
    all_to_all x1, blocking collectives, shards(): flux = lax.all_to_all(flux, 'tile', 0, 0, tiled=True)  23.2 us
    all_to_all x1, starting transfers between devices, shards(): blocks = lax.all_to_all(mine, 'tile', 0, 0, tiled=True)  19.1 us
    ppermute x4, starting transfers between devices, shift(): return lax.ppermute(value, axis, pairs)  12.7 us
    pallas_call x1, Pallas kernels, slab(): pl.pallas_call(slab_kernel, in_specs=[VM] * 14, out_specs=[VM, VM], out_s...  10.1 us
    pallas_call x1, Pallas kernels, early(): pl.pallas_call(early_kernel, in_specs=[VM] * 8, out_specs=[VM] * 5, out_s...  5.05 us
    pallas_call x1, Pallas kernels, values(): pl.pallas_call(values_kernel, in_specs=[ANY, ANY, ANY, SM, SM, SM], out_s...  4.94 us
    ppermute x4, waiting for transfers between devices, shift(): return lax.ppermute(value, axis, pairs)  4.57 us
    unnamed x24, local copies, waits for them, and re-layouts  4.21 us
  transfers between devices with their start and end apart: 5, of which 3 were waited for; matrix products, arithmetic and copies ran while one was open for 0% of the time, Pallas kernels for 14%

profile of v4, /device:TPU:1, one launch (start us, length us, event | category | flops | bytes accessed | tf_op | source)
XLA Modules:
  0.0 93.6 jit_solution(6815014390386515437)
XLA Ops:
  0.6 1.5 %blocks.1.after = f32[64,8,128]{2,1,0:T(8,128)} custom-call(f32[2,16,32]{2,1,0:T(8,128)} %wind.3), custom_call_target="tpu_custom_call" | custom-call | tf_op jit(solution)/shard_map/blocks/pallas_call | solution.py:119
  2.1 19.1 %all-to-all-start = ((f32[64,8,128]{2,1,0:T(8,128)}), f32[64,8,128]{2,1,0:T(8,128)S(1)}, u32[]{:S(2)}, u32[]{:S(2)}) async-start(f32[64,8,128]{2,1,0:T(8,128)} %blocks.1.after), calls=%async_computation | async-start | bytes 524288 | tf_op jit(solution)/shard_map/all_to_all | solution.py:620
  21.3 2.6 %strips.1 = (f32[328,128]{1,0:T(8,128)}, f32[328,128]{1,0:T(8,128)}, f32[8,128]{1,0:T(8,128)}) custom-call(f32[320,640]{1,0:T(8,128)} %level.7, s32[320,640]{1,0:T(8,128)} %fuel.5, s32[1,1,4]{2,1,0:T(1,128)} %bitcast.1, f32[64,8,128]{2,1,0:T(8,128)} %blocks.1.after), custom_call_target="tpu_custom_call" | custom-call | tf_op jit(solution)/shard_map/strips/pallas_call | solution.py:97
  23.9 2.9 %collective-permute-start = (f32[328,128]{1,0:T(8,128)}, f32[328,128]{1,0:T(8,128)S(1)}, u32[]{:S(2)}, u32[]{:S(2)}) collective-permute-start(f32[328,128]{1,0:T(8,128)} %get-tuple-element.20), channel_id=1, source_target_pairs={{0,1},{1,2},{2,3},{3,4},{4,5},{5,6},{6,7},{7,8},{8,9},{9,10},{10,1... | collective-permute-start | bytes 503816 | tf_op jit(solution)/shard_map/ppermute | solution.py:614
  26.9 1.3 %collective-permute-start.1 = (f32[328,128]{1,0:T(8,128)}, f32[328,128]{1,0:T(8,128)S(1)}, u32[]{:S(2)}, u32[]{:S(2)}) collective-permute-start(f32[328,128]{1,0:T(8,128)} %get-tuple-element.21), channel_id=1, source_target_pairs={{1,0},{2,1},{3,2},{4,3},{5,4},{6,5},{7,6},{8,7},{9,8},{10,9},{11,1... | collective-permute-start | bytes 503816 | tf_op jit(solution)/shard_map/ppermute | solution.py:614
  28.2 0.0 copy-start.10
  28.2 0.0 copy-start.11
  28.2 0.0 copy-start.1
  28.2 4.9 %values.1 = (f32[320,640]{1,0:T(8,128)}, f32[320,640]{1,0:T(8,128)}, f32[24,128]{1,0:T(8,128)}, f32[96,640]{1,0:T(8,128)}, f32[96,640]{1,0:T(8,128)}) custom-call(f32[320,640]{1,0:T(8,128)} %level.7, s32[320,640]{1,0:T(8,128)} %fuel.5, f32[8,128]{1,0:T(8,128)} %get-tuple-element.22.after, f32[13]{0:T(128)} %fuel_rate.1, f32[13]{0:T(128)} %fuel_wind.1, ...), custom_call_target="tpu_custom_call" | custom-call | tf_op jit(solution)/shard_map/values/pallas_call | solution.py:218
  33.1 0.0 copy-start
  33.2 2.5 %collective-permute-done.from_left = f32[328,128]{1,0:T(8,128)S(1)} collective-permute-done((f32[328,128]{1,0:T(8,128)}, f32[328,128]{1,0:T(8,128)S(1)}, u32[]{:S(2)}, u32[]{:S(2)}) %collective-permute-start) | collective-permute-done | bytes 167968 | tf_op jit(solution)/shard_map/ppermute | solution.py:614
  35.6 2.1 %collective-permute-done.1.from_right = f32[328,128]{1,0:T(8,128)S(1)} collective-permute-done((f32[328,128]{1,0:T(8,128)}, f32[328,128]{1,0:T(8,128)S(1)}, u32[]{:S(2)}, u32[]{:S(2)}) %collective-permute-start.1) | collective-permute-done | bytes 167968 | tf_op jit(solution)/shard_map/ppermute | solution.py:614
  37.7 2.6 %all-to-all-done.blocks = f32[64,8,128]{2,1,0:T(8,128)S(1)} async-done(((f32[64,8,128]{2,1,0:T(8,128)}), f32[64,8,128]{2,1,0:T(8,128)S(1)}, u32[]{:S(2)}, u32[]{:S(2)}) %all-to-all-start) | async-done | bytes 262176 | tf_op jit(solution)/shard_map/all_to_all | solution.py:620
  40.3 0.0 copy-done.10
  40.3 0.0 copy-done.11
  40.3 0.0 copy-start.6
  40.3 0.9 %copy-done.6 = f32[96,640]{1,0:T(8,128)S(1)} copy-done((f32[96,640]{1,0:T(8,128)S(1)}, f32[96,640]{1,0:T(8,128)}, u32[]{:S(2)}) %copy-start.6) | copy-done | bytes 245784
  41.3 0.0 copy-start.7
  41.3 0.9 %copy-done.7 = f32[96,640]{1,0:T(8,128)S(1)} copy-done((f32[96,640]{1,0:T(8,128)S(1)}, f32[96,640]{1,0:T(8,128)}, u32[]{:S(2)}) %copy-start.7) | copy-done | bytes 245784
  42.2 0.0 copy-start.9
  42.2 0.6 rows.1
  42.9 6.6 %collective-permute-start.2 = (f32[104,768]{1,0:T(8,128)S(1)}, f32[104,768]{1,0:T(8,128)S(1)}, u32[]{:S(2)}, u32[]{:S(2)}) collective-permute-start(f32[104,768]{1,0:T(8,128)S(1)} %get-tuple-element.25), channel_id=1, source_target_pairs={{0,64},{64,128},{128,192},{192,256},{256,320},{320,384},{384,448},... | collective-permute-start | bytes 958472 | tf_op jit(solution)/shard_map/ppermute | solution.py:614
  49.5 1.9 %collective-permute-start.3 = (f32[104,768]{1,0:T(8,128)S(1)}, f32[104,768]{1,0:T(8,128)S(1)}, u32[]{:S(2)}, u32[]{:S(2)}) collective-permute-start(f32[104,768]{1,0:T(8,128)S(1)} %get-tuple-element.26), channel_id=1, source_target_pairs={{64,0},{128,64},{192,128},{256,192},{320,256},{384,320},{448,384},... | collective-permute-start | bytes 958472 | tf_op jit(solution)/shard_map/ppermute | solution.py:614
  51.4 0.0 copy-done.1
  51.4 0.0 copy-done
  51.5 0.0 copy-done.9
  51.5 0.0 copy-start.2
  51.5 1.1 %copy-done.2 = f32[320,640]{1,0:T(8,128)S(1)} copy-done((f32[320,640]{1,0:T(8,128)S(1)}, f32[320,640]{1,0:T(8,128)}, u32[]{:S(2)}) %copy-start.2) | copy-done | bytes 819224
  52.6 0.0 copy-start.4
  52.6 1.1 %copy-done.4 = f32[320,640]{1,0:T(8,128)S(1)} copy-done((f32[320,640]{1,0:T(8,128)S(1)}, f32[320,640]{1,0:T(8,128)}, u32[]{:S(2)}) %copy-start.4) | copy-done | bytes 819224
  53.8 0.0 copy-start.3
  53.8 0.0 copy-start.5
  53.8 5.1 %early.1 = (f32[320,768]{1,0:T(8,128)S(1)}, f32[320,640]{1,0:T(8,128)S(1)}, f32[320,128]{1,0:T(8,128)S(1)}, f32[320,128]{1,0:T(8,128)S(1)}, f32[320,128]{1,0:T(8,128)S(1)}) custom-call(f32[320,640]{1,0:T(8,128)S(1)} %copy-done, s32[320,640]{1,0:T(8,128)S(1)} %copy-done.1, f32[328,128]{1,0:T(8,128)S(1)} %collective-permute-done.from_left, ...), custom_call_target="tpu_custom_call" | custom-call | tf_op jit(solution)/shard_map/early/pallas_call | solution.py:386
  58.8 0.0 collective-permute-done.2.from_up
  58.8 0.0 collective-permute-done.3.from_down
  58.8 0.0 copy-done.3
  58.9 0.0 copy-done.5
  58.9 10.1 %slab.1 = (f32[320,640]{1,0:T(8,128)}, f32[64,4,128]{2,1,0:T(4,128)S(1)}) custom-call(f32[320,640]{1,0:T(8,128)S(1)} %copy-done, f32[328,128]{1,0:T(8,128)S(1)} %collective-permute-done.from_left, f32[328,128]{1,0:T(8,128)S(1)} %collective-permute-done.1.from_right, f32[104,768]{1,0:T(8,128)S(1)} %collective-permute-done.2.from_up, ...), custom_call_target="tpu_custom_call" | custom-call | tf_op jit(solution)/shard_map/slab/pallas_call | solution.py:566
  69.0 0.0 copy-start.8
  69.0 23.2 %all_to_all.10.received = f32[64,4,128]{2,1,0:T(4,128)S(1)} all-to-all(f32[64,4,128]{2,1,0:T(4,128)S(1)} %get-tuple-element.37), channel_id=1, replica_groups=mesh['grp'=8,'tile'=64] {'tile'}, dimensions={0} | all-to-all | bytes 262144 | tf_op jit(solution)/shard_map/all_to_all | solution.py:632
  92.2 0.0 copy-done.8
  92.2 1.3 %final.1 = f32[2,16,32]{2,1,0:T(8,128)} custom-call(s32[1,64]{1,0:T(1,128)S(1)} %copy-done.11, f32[64,4,128]{2,1,0:T(4,128)S(1)} %all_to_all.10.received, f32[2,16,32]{2,1,0:T(8,128)S(1)} %copy-done.8), custom_call_target="tpu_custom_call" | custom-call | tf_op jit(solution)/shard_map/final/pallas_call | solution.py:605
Async XLA Ops:
  2.1 38.2 %all-to-all-start = ((f32[64,8,128]{2,1,0:T(8,128)}), f32[64,8,128]{2,1,0:T(8,128)S(1)}, u32[]{:S(2)}, u32[]{:S(2)}) async-start(f32[64,8,128]{2,1,0:T(8,128)} %blocks.1.after), calls=%async_computation | async-start | bytes 524288 | tf_op jit(solution)/shard_map/all_to_all | solution.py:620
  23.9 11.7 %collective-permute-start = (f32[328,128]{1,0:T(8,128)}, f32[328,128]{1,0:T(8,128)S(1)}, u32[]{:S(2)}, u32[]{:S(2)}) collective-permute-start(f32[328,128]{1,0:T(8,128)} %get-tuple-element.20), channel_id=1, source_target_pairs={{0,1},{1,2},{2,3},{3,4},{4,5},{5,6},{6,7},{7,8},{8,9},{9,10},{10,1... | collective-permute-start | bytes 503816 | tf_op jit(solution)/shard_map/ppermute | solution.py:614
  26.9 10.9 %collective-permute-start.1 = (f32[328,128]{1,0:T(8,128)}, f32[328,128]{1,0:T(8,128)S(1)}, u32[]{:S(2)}, u32[]{:S(2)}) collective-permute-start(f32[328,128]{1,0:T(8,128)} %get-tuple-element.21), channel_id=1, source_target_pairs={{1,0},{2,1},{3,2},{4,3},{5,4},{6,5},{7,6},{8,7},{9,8},{10,9},{11,1... | collective-permute-start | bytes 503816 | tf_op jit(solution)/shard_map/ppermute | solution.py:614
  28.2 12.2 %copy-start.10 = (s32[4,1,1]{0,2,1:T(1,128)S(1)}, s32[4,1,1]{0,2,1:T(1,128)}, u32[]{:S(2)}) copy-start(s32[4,1,1]{0,2,1:T(1,128)} %param.12) | copy-start | bytes 52
  28.2 12.2 %copy-start.11 = (s32[1,64]{1,0:T(1,128)S(1)}, s32[1,64]{1,0:T(1,128)}, u32[]{:S(2)}) copy-start(s32[1,64]{1,0:T(1,128)} %owner.3) | copy-start | bytes 772
  28.2 23.3 %copy-start.1 = (s32[320,640]{1,0:T(8,128)S(1)}, s32[320,640]{1,0:T(8,128)}, u32[]{:S(2)}) copy-start(s32[320,640]{1,0:T(8,128)} %fuel.5) | copy-start | bytes 2457604
  33.1 18.3 %copy-start = (f32[320,640]{1,0:T(8,128)S(1)}, f32[320,640]{1,0:T(8,128)}, u32[]{:S(2)}) copy-start(f32[320,640]{1,0:T(8,128)} %level.7) | copy-start | bytes 2457604
  40.3 0.9 %copy-start.6 = (f32[96,640]{1,0:T(8,128)S(1)}, f32[96,640]{1,0:T(8,128)}, u32[]{:S(2)}) copy-start(f32[96,640]{1,0:T(8,128)} %get-tuple-element.23.up) | copy-start | bytes 737284
  41.3 0.9 %copy-start.7 = (f32[96,640]{1,0:T(8,128)S(1)}, f32[96,640]{1,0:T(8,128)}, u32[]{:S(2)}) copy-start(f32[96,640]{1,0:T(8,128)} %get-tuple-element.24.down) | copy-start | bytes 737284
  42.2 9.2 %copy-start.9 = (f32[24,128]{1,0:T(8,128)S(1)}, f32[24,128]{1,0:T(8,128)}, u32[]{:S(2)}) copy-start(f32[24,128]{1,0:T(8,128)} %get-tuple-element.30.three) | copy-start | bytes 36868
  42.9 15.9 %collective-permute-start.2 = (f32[104,768]{1,0:T(8,128)S(1)}, f32[104,768]{1,0:T(8,128)S(1)}, u32[]{:S(2)}, u32[]{:S(2)}) collective-permute-start(f32[104,768]{1,0:T(8,128)S(1)} %get-tuple-element.25), channel_id=1, source_target_pairs={{0,64},{64,128},{128,192},{192,256},{256,320},{320,384},{384,448},... | collective-permute-start | bytes 958472 | tf_op jit(solution)/shard_map/ppermute | solution.py:614
  49.5 9.3 %collective-permute-start.3 = (f32[104,768]{1,0:T(8,128)S(1)}, f32[104,768]{1,0:T(8,128)S(1)}, u32[]{:S(2)}, u32[]{:S(2)}) collective-permute-start(f32[104,768]{1,0:T(8,128)S(1)} %get-tuple-element.26), channel_id=1, source_target_pairs={{64,0},{128,64},{192,128},{256,192},{320,256},{384,320},{448,384},... | collective-permute-start | bytes 958472 | tf_op jit(solution)/shard_map/ppermute | solution.py:614
  51.5 1.1 %copy-start.2 = (f32[320,640]{1,0:T(8,128)S(1)}, f32[320,640]{1,0:T(8,128)}, u32[]{:S(2)}) copy-start(f32[320,640]{1,0:T(8,128)} %get-tuple-element.28.rate) | copy-start | bytes 2457604
  52.6 1.1 %copy-start.4 = (f32[320,640]{1,0:T(8,128)S(1)}, f32[320,640]{1,0:T(8,128)}, u32[]{:S(2)}) copy-start(f32[320,640]{1,0:T(8,128)} %get-tuple-element.29.drift) | copy-start | bytes 2457604
  53.8 5.1 %copy-start.3 = (f32[320,640]{1,0:T(8,128)S(1)}, f32[320,640]{1,0:T(8,128)}, u32[]{:S(2)}) copy-start(f32[320,640]{1,0:T(8,128)} %get-tuple-element.28.rate) | copy-start | bytes 2457604
  53.8 5.1 %copy-start.5 = (f32[320,640]{1,0:T(8,128)S(1)}, f32[320,640]{1,0:T(8,128)}, u32[]{:S(2)}) copy-start(f32[320,640]{1,0:T(8,128)} %get-tuple-element.29.drift) | copy-start | bytes 2457604
  69.0 23.2 %copy-start.8 = (f32[2,16,32]{2,1,0:T(8,128)S(1)}, f32[2,16,32]{2,1,0:T(8,128)}, u32[]{:S(2)}) copy-start(f32[2,16,32]{2,1,0:T(8,128)} %wind.3) | copy-start | bytes 12292

commit v5 on v3

--- a/solution.py
+++ b/solution.py
@@ -28,7 +28,8 @@
 VM = pl.BlockSpec(memory_space=pltpu.VMEM)
 SM = pl.BlockSpec(memory_space=pltpu.SMEM)
 ANY = pl.BlockSpec(memory_space=pl.ANY)
-PARAMS = pltpu.CompilerParams(vmem_limit_bytes=40 * 1024 * 1024)
+SMALL = pltpu.CompilerParams(vmem_limit_bytes=4 * 1024 * 1024)
+LARGE = pltpu.CompilerParams(vmem_limit_bytes=12 * 1024 * 1024)
 
 
 def lanes(shape):
@@ -61,7 +62,7 @@
     return jnp.where(fine < FX, own, edge)
 
 
-def strips_kernel(level, fuel, active, to_left, to_right, left_level, right_level, left_fuel, right_fuel, arrived):
+def strips_kernel(level, fuel, active, after, to_left, to_right, left_level, right_level, left_fuel, right_fuel, arrived):
     first, last = pl.ds(0, 128), pl.ds(FX - 128, 128)
     moves = [
         pltpu.make_async_copy(source.at[:, part], buf, arrived.at[i])
@@ -89,34 +90,34 @@
     )
 
 
-def strips(level, fuel, active):
+def strips(level, fuel, active, after):
     strip = pltpu.VMEM((FY, 128), jnp.float32)
     kinds = pltpu.VMEM((FY, 128), jnp.int32)
     return pl.pallas_call(
         strips_kernel,
-        in_specs=[ANY, ANY, SM],
+        in_specs=[ANY, ANY, SM, ANY],
         out_specs=[VM, VM],
         out_shape=[f32(FY + 8, 128), f32(FY + 8, 128)],
         scratch_shapes=[strip, strip, kinds, kinds, pltpu.SemaphoreType.DMA((4,))],
         name="strips",
-    )(level, fuel, active)
+    )(level, fuel, active, after)
 
 
 def flag_of(active, k):
     return (active[0, 0, min(k, STEPS * SUBSTEPS - 1)] > 0).astype(jnp.float32)
 
 
-def blocks_kernel(wind, after, slots):
+def blocks_kernel(wind, slots):
     parts = [wind[0, 0:8, :], wind[0, 8:16, :], wind[1, 0:8, :], wind[1, 8:16, :]]
     block = jnp.concatenate(parts, axis=1)
     for k in range(NX * NZ):
         slots[k] = block
 
 
-def blocks_of(wind, after):
+def blocks_of(wind):
     return pl.pallas_call(
-        blocks_kernel, in_specs=[VM, ANY], out_specs=VM, out_shape=f32(NX * NZ, 8, 128), name="blocks"
-    )(wind, after)
+        blocks_kernel, in_specs=[VM], out_specs=VM, out_shape=f32(NX * NZ, 8, 128), name="blocks"
+    )(wind)
 
 
 def rows_kernel(
@@ -166,7 +167,7 @@
         in_specs=[VM] * 5 + [SM, SM],
         out_specs=[VM, VM, VM],
         out_shape=[f32(2 * AY + 8, 128), f32(*shape), f32(*shape)],
-        compiler_params=PARAMS,
+        compiler_params=SMALL,
         name="rows",
     )(level, fuel, from_left, from_right, blocks, owner, active)
 
@@ -211,7 +212,7 @@
         in_specs=[VM, VM, VM, ANY, SM, SM, SM],
         out_specs=[VM] * 4,
         out_shape=[f32(FY, COLS)] * 3 + [f32(24, 128)],
-        compiler_params=PARAMS,
+        compiler_params=SMALL,
         name="values",
     )(fuel, from_left, from_right, after, *names)
 
@@ -470,7 +471,7 @@
             pltpu.VMEM((128, COLS), jnp.bfloat16),
             pltpu.VMEM((COLS, 128), jnp.bfloat16),
         ],
-        compiler_params=PARAMS,
+        compiler_params=LARGE,
         name="slab",
     )(*args)
 
@@ -494,7 +495,8 @@
 
 def final(owner, received, wind):
     return pl.pallas_call(
-        final_kernel, in_specs=[SM, VM, VM], out_specs=VM, out_shape=f32(2, AY, AX), name="final"
+        final_kernel, in_specs=[SM, VM, VM], out_specs=VM, out_shape=f32(2, AY, AX),
+        compiler_params=SMALL, name="final"
     )(owner, received, wind)
 
 
@@ -506,12 +508,11 @@
 
 def shards(level, fuel, wind, owner, active, fuel_rate, fuel_wind, fuel_heat):
     active = jnp.transpose(active, (1, 2, 0))
-    to_left, to_right = strips(level, fuel, active)
+    mine = blocks_of(wind)
+    blocks = lax.all_to_all(mine, "tile", 0, 0, tiled=True)
+    to_left, to_right = strips(level, fuel, active, mine)
     from_right = shift(to_left, "tile", -1)
     from_left = shift(to_right, "tile", 1)
-    blocks = blocks_of(wind, to_left)
-    blocks, from_left, from_right = lax.optimization_barrier((blocks, from_left, from_right))
-    blocks = lax.all_to_all(blocks, "tile", 0, 0, tiled=True)
     held, to_up, to_down = rows(level, fuel, from_left, from_right, blocks, owner, active)
     from_down = shift(to_up, "grp", -1)
     from_up = shift(to_down, "grp", 1)

time: 101 us -> 92.2 us (0.913)
  blocking collectives: 55.9 us -> 22.1 us
  starting transfers between devices: 15.2 us -> 31.9 us
  waiting for transfers between devices: 7.16 us -> 15.5 us
    all_to_all x1 -> x0, blocking collectives: 36.3 us -> none  [shards(): blocks = lax.all_to_all(blocks, 'tile', 0, 0, tiled=True)]
    all_to_all x0 -> x1, starting transfers between devices: none -> 19.1 us  [shards(): blocks = lax.all_to_all(mine, 'tile', 0, 0, tiled=True)]
    ppermute x4, waiting for transfers between devices: 7.16 us -> 12.9 us  [shift(): return lax.ppermute(value, axis, pairs)]
    all_to_all x1, blocking collectives: 19.5 us -> 22.1 us  [shards(): flux = lax.all_to_all(flux, 'tile', 0, 0, tiled=True)]
    all_to_all x0 -> x1, waiting for transfers between devices: none -> 2.54 us  [shards(): blocks = lax.all_to_all(mine, 'tile', 0, 0, tiled=True)]
    ppermute x4, starting transfers between devices: 15.2 us -> 12.8 us  [shift(): return lax.ppermute(value, axis, pairs)]
  transfers between devices with their start and end apart: 4 -> 5, of which waited for: 2 -> 4; matrix products, arithmetic and copies ran while one was open for 0% -> 0% of each run, Pallas kernels for 4% -> 6%
where the time goes in v5:
time: 92.2 us; the launch traced here: 91.2 us
  starting transfers between devices  31.9 us (35%)
  blocking collectives  22.1 us (24%)
  Pallas kernels  20.9 us (23%)
  waiting for transfers between devices  15.5 us (17%)
    all_to_all x1, blocking collectives, shards(): flux = lax.all_to_all(flux, 'tile', 0, 0, tiled=True)  22.1 us
    all_to_all x1, starting transfers between devices, shards(): blocks = lax.all_to_all(mine, 'tile', 0, 0, tiled=True)  19.1 us
    ppermute x4, waiting for transfers between devices, shift(): return lax.ppermute(value, axis, pairs)  12.9 us
    ppermute x4, starting transfers between devices, shift(): return lax.ppermute(value, axis, pairs)  12.8 us
    pallas_call x1, Pallas kernels, slab(): pl.pallas_call(slab_kernel, in_specs=[VM] * 10, out_specs=[VM, VM], out_s...  11.8 us
    pallas_call x1, Pallas kernels, values(): pl.pallas_call(values_kernel, in_specs=[VM, VM, VM, ANY, SM, SM, SM], out...  2.87 us
    pallas_call x1, Pallas kernels, strips(): pl.pallas_call(strips_kernel, in_specs=[ANY, ANY, SM, ANY], out_specs=[VM...  2.77 us
    all_to_all x1, waiting for transfers between devices, shards(): blocks = lax.all_to_all(mine, 'tile', 0, 0, tiled=True)  2.54 us
  transfers between devices with their start and end apart: 5, of which 4 were waited for; matrix products, arithmetic and copies ran while one was open for 0% of the time, Pallas kernels for 6%

profile of v5, /device:TPU:1, one launch (start us, length us, event | category | flops | bytes accessed | tf_op | source)
XLA Modules:
  0.0 91.2 jit_solution(13603038590244869091)
XLA Ops:
  0.6 1.5 %blocks.1.after = f32[64,8,128]{2,1,0:T(8,128)} custom-call(f32[2,16,32]{2,1,0:T(8,128)} %wind.3), custom_call_target="tpu_custom_call" | custom-call | tf_op jit(solution)/shard_map/blocks/pallas_call | solution.py:118
  2.1 19.1 %all-to-all-start = ((f32[64,8,128]{2,1,0:T(8,128)}), f32[64,8,128]{2,1,0:T(8,128)S(1)}, u32[]{:S(2)}, u32[]{:S(2)}) async-start(f32[64,8,128]{2,1,0:T(8,128)} %blocks.1.after), calls=%async_computation | async-start | bytes 524288 | tf_op jit(solution)/shard_map/all_to_all | solution.py:512
  21.3 0.0 copy-start
  21.3 0.0 copy-start.1
  21.3 2.8 %strips.1 = (f32[328,128]{1,0:T(8,128)}, f32[328,128]{1,0:T(8,128)}) custom-call(f32[320,640]{1,0:T(8,128)} %level.5, s32[320,640]{1,0:T(8,128)} %fuel.5, s32[1,1,4]{2,1,0:T(1,128)} %bitcast.1, f32[64,8,128]{2,1,0:T(8,128)} %blocks.1.after), custom_call_target="tpu_custom_call" | custom-call | tf_op jit(solution)/shard_map/strips/pallas_call | solution.py:96
  24.1 0.0 copy-start.3
  24.1 0.0 copy-start.4
  24.1 2.9 %collective-permute-start = (f32[328,128]{1,0:T(8,128)}, f32[328,128]{1,0:T(8,128)S(1)}, u32[]{:S(2)}, u32[]{:S(2)}) collective-permute-start(f32[328,128]{1,0:T(8,128)} %get-tuple-element.13), channel_id=1, source_target_pairs={{0,1},{1,2},{2,3},{3,4},{4,5},{5,6},{6,7},{7,8},{8,9},{9,10},{10,1... | collective-permute-start | bytes 503816 | tf_op jit(solution)/shard_map/ppermute | solution.py:506
  27.0 1.3 %collective-permute-start.1 = (f32[328,128]{1,0:T(8,128)}, f32[328,128]{1,0:T(8,128)S(1)}, u32[]{:S(2)}, u32[]{:S(2)}) collective-permute-start(f32[328,128]{1,0:T(8,128)} %get-tuple-element.14), channel_id=1, source_target_pairs={{1,0},{2,1},{3,2},{4,3},{5,4},{6,5},{7,6},{8,7},{9,8},{10,9},{11,1... | collective-permute-start | bytes 503816 | tf_op jit(solution)/shard_map/ppermute | solution.py:506
  28.3 7.2 %collective-permute-done.from_left = f32[328,128]{1,0:T(8,128)S(1)} collective-permute-done((f32[328,128]{1,0:T(8,128)}, f32[328,128]{1,0:T(8,128)S(1)}, u32[]{:S(2)}, u32[]{:S(2)}) %collective-permute-start) | collective-permute-done | bytes 167968 | tf_op jit(solution)/shard_map/ppermute | solution.py:506
  35.6 2.2 %collective-permute-done.1.from_right = f32[328,128]{1,0:T(8,128)S(1)} collective-permute-done((f32[328,128]{1,0:T(8,128)}, f32[328,128]{1,0:T(8,128)S(1)}, u32[]{:S(2)}, u32[]{:S(2)}) %collective-permute-start.1) | collective-permute-done | bytes 167968 | tf_op jit(solution)/shard_map/ppermute | solution.py:506
  37.8 2.5 %all-to-all-done.blocks = f32[64,8,128]{2,1,0:T(8,128)S(1)} async-done(((f32[64,8,128]{2,1,0:T(8,128)}), f32[64,8,128]{2,1,0:T(8,128)S(1)}, u32[]{:S(2)}, u32[]{:S(2)}) %all-to-all-start) | async-done | bytes 262176 | tf_op jit(solution)/shard_map/all_to_all | solution.py:512
  40.3 0.0 copy-done
  40.3 0.0 copy-done.1
  40.3 0.0 copy-done.3
  40.3 0.0 copy-done.4
  40.3 0.6 rows.1
  41.0 6.5 %collective-permute-start.2 = (f32[104,768]{1,0:T(8,128)S(1)}, f32[104,768]{1,0:T(8,128)S(1)}, u32[]{:S(2)}, u32[]{:S(2)}) collective-permute-start(f32[104,768]{1,0:T(8,128)S(1)} %get-tuple-element.15), channel_id=1, source_target_pairs={{0,64},{64,128},{128,192},{192,256},{256,320},{320,384},{384,448},... | collective-permute-start | bytes 958472 | tf_op jit(solution)/shard_map/ppermute | solution.py:506
  47.5 0.0 copy-start.5
  47.6 0.0 copy-start.6
  47.6 0.0 copy-start.7
  47.6 2.1 %collective-permute-start.3 = (f32[104,768]{1,0:T(8,128)S(1)}, f32[104,768]{1,0:T(8,128)S(1)}, u32[]{:S(2)}, u32[]{:S(2)}) collective-permute-start(f32[104,768]{1,0:T(8,128)S(1)} %get-tuple-element.16), channel_id=1, source_target_pairs={{64,0},{128,64},{192,128},{256,192},{320,256},{384,320},{448,384},... | collective-permute-start | bytes 958472 | tf_op jit(solution)/shard_map/ppermute | solution.py:506
  49.6 0.0 copy-done.5
  49.6 0.0 copy-done.6
  49.7 0.0 copy-done.7
  49.7 2.9 %values.1 = (f32[320,768]{1,0:T(8,128)S(1)}, f32[320,768]{1,0:T(8,128)S(1)}, f32[320,768]{1,0:T(8,128)S(1)}, f32[24,128]{1,0:T(8,128)S(1)}) custom-call(s32[320,640]{1,0:T(8,128)S(1)} %copy-done.1, f32[328,128]{1,0:T(8,128)S(1)} %collective-permute-done.from_left, f32[328,128]{1,0:T(8,128)S(1)} %collective-permute-done.1.from_right, ...), custom_call_target="tpu_custom_call" | custom-call | tf_op jit(solution)/shard_map/values/pallas_call | solution.py:210
  52.5 0.0 collective-permute-done.2.from_up
  52.5 3.5 %collective-permute-done.3.from_down = f32[104,768]{1,0:T(8,128)S(1)} collective-permute-done((f32[104,768]{1,0:T(8,128)S(1)}, f32[104,768]{1,0:T(8,128)S(1)}, u32[]{:S(2)}, u32[]{:S(2)}) %collective-permute-start.3) | collective-permute-done | bytes 319520 | tf_op jit(solution)/shard_map/ppermute | solution.py:506
  56.0 11.8 %slab.1 = (f32[320,640]{1,0:T(8,128)}, f32[64,4,128]{2,1,0:T(4,128)S(1)}) custom-call(f32[320,640]{1,0:T(8,128)S(1)} %copy-done, f32[328,128]{1,0:T(8,128)S(1)} %collective-permute-done.from_left, f32[328,128]{1,0:T(8,128)S(1)} %collective-permute-done.1.from_right, f32[104,768]{1,0:T(8,128)S(1)} %collective-permute-done.2.from_up, ...), custom_call_target="tpu_custom_call" | custom-call | tf_op jit(solution)/shard_map/slab/pallas_call | solution.py:458
  67.8 0.0 copy-start.2
  67.8 22.1 %all_to_all.10.received = f32[64,4,128]{2,1,0:T(4,128)S(1)} all-to-all(f32[64,4,128]{2,1,0:T(4,128)S(1)} %get-tuple-element.23), channel_id=1, replica_groups=mesh['grp'=8,'tile'=64] {'tile'}, dimensions={0} | all-to-all | bytes 262144 | tf_op jit(solution)/shard_map/all_to_all | solution.py:521
  89.9 0.0 copy-done.2
  89.9 1.3 %final.1 = f32[2,16,32]{2,1,0:T(8,128)} custom-call(s32[1,64]{1,0:T(1,128)S(1)} %copy-done.4, f32[64,4,128]{2,1,0:T(4,128)S(1)} %all_to_all.10.received, f32[2,16,32]{2,1,0:T(8,128)S(1)} %copy-done.2), custom_call_target="tpu_custom_call" | custom-call | tf_op jit(solution)/shard_map/final/pallas_call | solution.py:497
Async XLA Ops:
  2.1 38.2 %all-to-all-start = ((f32[64,8,128]{2,1,0:T(8,128)}), f32[64,8,128]{2,1,0:T(8,128)S(1)}, u32[]{:S(2)}, u32[]{:S(2)}) async-start(f32[64,8,128]{2,1,0:T(8,128)} %blocks.1.after), calls=%async_computation | async-start | bytes 524288 | tf_op jit(solution)/shard_map/all_to_all | solution.py:512
  21.3 19.1 %copy-start = (f32[320,640]{1,0:T(8,128)S(1)}, f32[320,640]{1,0:T(8,128)}, u32[]{:S(2)}) copy-start(f32[320,640]{1,0:T(8,128)} %level.5) | copy-start | bytes 2457604
  21.3 19.1 %copy-start.1 = (s32[320,640]{1,0:T(8,128)S(1)}, s32[320,640]{1,0:T(8,128)}, u32[]{:S(2)}) copy-start(s32[320,640]{1,0:T(8,128)} %fuel.5) | copy-start | bytes 2457604
  24.1 16.3 %copy-start.3 = (s32[4,1,1]{0,2,1:T(1,128)S(1)}, s32[4,1,1]{0,2,1:T(1,128)}, u32[]{:S(2)}) copy-start(s32[4,1,1]{0,2,1:T(1,128)} %param.12) | copy-start | bytes 52
  24.1 16.3 %copy-start.4 = (s32[1,64]{1,0:T(1,128)S(1)}, s32[1,64]{1,0:T(1,128)}, u32[]{:S(2)}) copy-start(s32[1,64]{1,0:T(1,128)} %owner.3) | copy-start | bytes 772
  24.1 11.5 %collective-permute-start = (f32[328,128]{1,0:T(8,128)}, f32[328,128]{1,0:T(8,128)S(1)}, u32[]{:S(2)}, u32[]{:S(2)}) collective-permute-start(f32[328,128]{1,0:T(8,128)} %get-tuple-element.13), channel_id=1, source_target_pairs={{0,1},{1,2},{2,3},{3,4},{4,5},{5,6},{6,7},{7,8},{8,9},{9,10},{10,1... | collective-permute-start | bytes 503816 | tf_op jit(solution)/shard_map/ppermute | solution.py:506
  27.0 10.8 %collective-permute-start.1 = (f32[328,128]{1,0:T(8,128)}, f32[328,128]{1,0:T(8,128)S(1)}, u32[]{:S(2)}, u32[]{:S(2)}) collective-permute-start(f32[328,128]{1,0:T(8,128)} %get-tuple-element.14), channel_id=1, source_target_pairs={{1,0},{2,1},{3,2},{4,3},{5,4},{6,5},{7,6},{8,7},{9,8},{10,9},{11,1... | collective-permute-start | bytes 503816 | tf_op jit(solution)/shard_map/ppermute | solution.py:506
  41.0 11.5 %collective-permute-start.2 = (f32[104,768]{1,0:T(8,128)S(1)}, f32[104,768]{1,0:T(8,128)S(1)}, u32[]{:S(2)}, u32[]{:S(2)}) collective-permute-start(f32[104,768]{1,0:T(8,128)S(1)} %get-tuple-element.15), channel_id=1, source_target_pairs={{0,64},{64,128},{128,192},{192,256},{256,320},{320,384},{384,448},... | collective-permute-start | bytes 958472 | tf_op jit(solution)/shard_map/ppermute | solution.py:506
  47.5 2.1 %copy-start.5 = (f32[13]{0:T(128)S(1)}, f32[13]{0:T(128)}, u32[]{:S(2)}) copy-start(f32[13]{0:T(128)} %fuel_rate.1) | copy-start | bytes 160
  47.6 2.1 %copy-start.6 = (f32[13]{0:T(128)S(1)}, f32[13]{0:T(128)}, u32[]{:S(2)}) copy-start(f32[13]{0:T(128)} %fuel_wind.1) | copy-start | bytes 160
  47.6 2.1 %copy-start.7 = (f32[13]{0:T(128)S(1)}, f32[13]{0:T(128)}, u32[]{:S(2)}) copy-start(f32[13]{0:T(128)} %fuel_heat.1) | copy-start | bytes 160
  47.6 8.4 %collective-permute-start.3 = (f32[104,768]{1,0:T(8,128)S(1)}, f32[104,768]{1,0:T(8,128)S(1)}, u32[]{:S(2)}, u32[]{:S(2)}) collective-permute-start(f32[104,768]{1,0:T(8,128)S(1)} %get-tuple-element.16), channel_id=1, source_target_pairs={{64,0},{128,64},{192,128},{256,192},{320,256},{384,320},{448,384},... | collective-permute-start | bytes 958472 | tf_op jit(solution)/shard_map/ppermute | solution.py:506
  67.8 22.1 %copy-start.2 = (f32[2,16,32]{2,1,0:T(8,128)S(1)}, f32[2,16,32]{2,1,0:T(8,128)}, u32[]{:S(2)}) copy-start(f32[2,16,32]{2,1,0:T(8,128)} %wind.3) | copy-start | bytes 12292

commit v6 on v5

--- a/solution.py
+++ b/solution.py
@@ -262,7 +262,7 @@
                     out[pl.ds(to, 8), 128 * c : 128 * c + 128] = look(row, kinds)
         return 0
 
-    lax.fori_loop(0, HALO // 8, halo_rows, 0, unroll=3)
+    lax.fori_loop(0, HALO // 8, halo_rows, 0, unroll=6)
 
     gates[0:8, :] = from_up[2 * HALO : 2 * HALO + 8, :]
     gates[16:24, :] = from_down[2 * HALO : 2 * HALO + 8, :]
@@ -292,10 +292,8 @@
 
     def expand():
         wide = exact_dot(winds[...], spread[...])
-        for comp, out in ((0, east), (1, north)):
-            part = wide[comp * CR : comp * CR + CR]
-            out[0:CR, :] = jnp.maximum(part, 0.0)
-            out[CR : 2 * CR, :] = jnp.minimum(part, 0.0)
+        east[...] = wide[0:CR]
+        north[...] = wide[CR : 2 * CR]
 
     def edges(phi):
         @pl.when(first_row)
@@ -340,16 +338,16 @@
         ay = jnp.minimum(ahead_y, 0.0)
         square = bx * bx + ax * ax + by * by + ay * ay + 1e-12
         slope = square * lax.rsqrt(square)
-        carry = e[0] * back_x + e[1] * ahead_x + n[0] * back_y + n[1] * ahead_y
+        carry = e * jnp.where(e > 0.0, back_x, ahead_x) + n * jnp.where(n > 0.0, back_y, ahead_y)
         there = pl.multiple_of(at - fuels[3], 8)
         change = fuels[0][pl.ds(there, 8), :] * slope + fuels[1][pl.ds(there, 8), :] * carry
         return now - gate * change
 
     def wind_row(ref, row):
-        return tuple(jnp.broadcast_to(ref[pl.ds(row + part, 1), :], (8, COLS)) for part in (0, CR))
+        return jnp.broadcast_to(ref[pl.ds(row, 1), :], (8, COLS))
 
     def mix(a, b):
-        return tuple(jnp.where(sub8 < 4, one, two) for one, two in zip(a, b))
+        return jnp.where(sub8 < 4, a, b)
 
     def band(phi, m, k, region, fuels, finish):
         at = pl.multiple_of(2 * PAD + 40 * m, 8)
@@ -373,7 +371,7 @@
             body(m, 1, own)
             return 0
 
-        lax.fori_loop(1, 9, step, 0)
+        lax.fori_loop(1, 9, step, 0, unroll=8)
 
     def store_to(out):
         def finish(here, new, fuels):
@@ -463,8 +461,8 @@
         scratch_shapes=[big] * 3
         + [edge] * 3
         + [
-            pltpu.VMEM((2 * CR, COLS), jnp.float32),
-            pltpu.VMEM((2 * CR, COLS), jnp.float32),
+            pltpu.VMEM((CR, COLS), jnp.float32),
+            pltpu.VMEM((CR, COLS), jnp.float32),
             pltpu.VMEM((2 * CR, 128), jnp.float32),
             pltpu.VMEM((CR, COLS), jnp.float32),
             pltpu.VMEM((CR, COLS), jnp.float32),

time: 92.2 us -> 89.7 us (0.973)
  Pallas kernels: 20.9 us -> 18.4 us
    pallas_call x1, Pallas kernels: 11.8 us -> 9.23 us  [slab(): pl.pallas_call(slab_kernel, in_specs=[VM] * 10, out_specs=[VM, VM], out_s...]
where the time goes in v6:
time: 89.7 us; the launch traced here: 88.7 us
  starting transfers between devices  31.9 us (36%)
  blocking collectives  22.1 us (25%)
  Pallas kernels  18.4 us (21%)
  waiting for transfers between devices  15.5 us (17%)
    all_to_all x1, blocking collectives, shards(): flux = lax.all_to_all(flux, 'tile', 0, 0, tiled=True)  22.1 us
    all_to_all x1, starting transfers between devices, shards(): blocks = lax.all_to_all(mine, 'tile', 0, 0, tiled=True)  19.1 us
    ppermute x4, waiting for transfers between devices, shift(): return lax.ppermute(value, axis, pairs)  12.9 us
    ppermute x4, starting transfers between devices, shift(): return lax.ppermute(value, axis, pairs)  12.8 us
    pallas_call x1, Pallas kernels, slab(): pl.pallas_call(slab_kernel, in_specs=[VM] * 10, out_specs=[VM, VM], out_s...  9.23 us
    pallas_call x1, Pallas kernels, values(): pl.pallas_call(values_kernel, in_specs=[VM, VM, VM, ANY, SM, SM, SM], out...  2.87 us
    pallas_call x1, Pallas kernels, strips(): pl.pallas_call(strips_kernel, in_specs=[ANY, ANY, SM, ANY], out_specs=[VM...  2.77 us
    all_to_all x1, waiting for transfers between devices, shards(): blocks = lax.all_to_all(mine, 'tile', 0, 0, tiled=True)  2.54 us
  transfers between devices with their start and end apart: 5, of which 4 were waited for; matrix products, arithmetic and copies ran while one was open for 0% of the time, Pallas kernels for 6%

profile of v6, /device:TPU:1, one launch (start us, length us, event | category | flops | bytes accessed | tf_op | source)
XLA Modules:
  0.0 88.7 jit_solution(13478249432431450266)
XLA Ops:
  0.6 1.5 %blocks.1.after = f32[64,8,128]{2,1,0:T(8,128)} custom-call(f32[2,16,32]{2,1,0:T(8,128)} %wind.3), custom_call_target="tpu_custom_call" | custom-call | tf_op jit(solution)/shard_map/blocks/pallas_call | solution.py:118
  2.1 19.1 %all-to-all-start = ((f32[64,8,128]{2,1,0:T(8,128)}), f32[64,8,128]{2,1,0:T(8,128)S(1)}, u32[]{:S(2)}, u32[]{:S(2)}) async-start(f32[64,8,128]{2,1,0:T(8,128)} %blocks.1.after), calls=%async_computation | async-start | bytes 524288 | tf_op jit(solution)/shard_map/all_to_all | solution.py:510
  21.3 0.0 copy-start
  21.3 0.0 copy-start.1
  21.3 2.8 %strips.1 = (f32[328,128]{1,0:T(8,128)}, f32[328,128]{1,0:T(8,128)}) custom-call(f32[320,640]{1,0:T(8,128)} %level.5, s32[320,640]{1,0:T(8,128)} %fuel.5, s32[1,1,4]{2,1,0:T(1,128)} %bitcast.1, f32[64,8,128]{2,1,0:T(8,128)} %blocks.1.after), custom_call_target="tpu_custom_call" | custom-call | tf_op jit(solution)/shard_map/strips/pallas_call | solution.py:96
  24.1 0.0 copy-start.3
  24.1 0.0 copy-start.4
  24.1 2.9 %collective-permute-start = (f32[328,128]{1,0:T(8,128)}, f32[328,128]{1,0:T(8,128)S(1)}, u32[]{:S(2)}, u32[]{:S(2)}) collective-permute-start(f32[328,128]{1,0:T(8,128)} %get-tuple-element.13), channel_id=1, source_target_pairs={{0,1},{1,2},{2,3},{3,4},{4,5},{5,6},{6,7},{7,8},{8,9},{9,10},{10,1... | collective-permute-start | bytes 503816 | tf_op jit(solution)/shard_map/ppermute | solution.py:504
  27.0 1.3 %collective-permute-start.1 = (f32[328,128]{1,0:T(8,128)}, f32[328,128]{1,0:T(8,128)S(1)}, u32[]{:S(2)}, u32[]{:S(2)}) collective-permute-start(f32[328,128]{1,0:T(8,128)} %get-tuple-element.14), channel_id=1, source_target_pairs={{1,0},{2,1},{3,2},{4,3},{5,4},{6,5},{7,6},{8,7},{9,8},{10,9},{11,1... | collective-permute-start | bytes 503816 | tf_op jit(solution)/shard_map/ppermute | solution.py:504
  28.3 7.2 %collective-permute-done.from_left = f32[328,128]{1,0:T(8,128)S(1)} collective-permute-done((f32[328,128]{1,0:T(8,128)}, f32[328,128]{1,0:T(8,128)S(1)}, u32[]{:S(2)}, u32[]{:S(2)}) %collective-permute-start) | collective-permute-done | bytes 167968 | tf_op jit(solution)/shard_map/ppermute | solution.py:504
  35.6 2.2 %collective-permute-done.1.from_right = f32[328,128]{1,0:T(8,128)S(1)} collective-permute-done((f32[328,128]{1,0:T(8,128)}, f32[328,128]{1,0:T(8,128)S(1)}, u32[]{:S(2)}, u32[]{:S(2)}) %collective-permute-start.1) | collective-permute-done | bytes 167968 | tf_op jit(solution)/shard_map/ppermute | solution.py:504
  37.8 2.5 %all-to-all-done.blocks = f32[64,8,128]{2,1,0:T(8,128)S(1)} async-done(((f32[64,8,128]{2,1,0:T(8,128)}), f32[64,8,128]{2,1,0:T(8,128)S(1)}, u32[]{:S(2)}, u32[]{:S(2)}) %all-to-all-start) | async-done | bytes 262176 | tf_op jit(solution)/shard_map/all_to_all | solution.py:510
  40.3 0.0 copy-done
  40.3 0.0 copy-done.1
  40.3 0.0 copy-done.3
  40.3 0.0 copy-done.4
  40.3 0.6 rows.1
  41.0 6.5 %collective-permute-start.2 = (f32[104,768]{1,0:T(8,128)S(1)}, f32[104,768]{1,0:T(8,128)S(1)}, u32[]{:S(2)}, u32[]{:S(2)}) collective-permute-start(f32[104,768]{1,0:T(8,128)S(1)} %get-tuple-element.15), channel_id=1, source_target_pairs={{0,64},{64,128},{128,192},{192,256},{256,320},{320,384},{384,448},... | collective-permute-start | bytes 958472 | tf_op jit(solution)/shard_map/ppermute | solution.py:504
  47.5 0.0 copy-start.5
  47.6 0.0 copy-start.6
  47.6 0.0 copy-start.7
  47.6 2.1 %collective-permute-start.3 = (f32[104,768]{1,0:T(8,128)S(1)}, f32[104,768]{1,0:T(8,128)S(1)}, u32[]{:S(2)}, u32[]{:S(2)}) collective-permute-start(f32[104,768]{1,0:T(8,128)S(1)} %get-tuple-element.16), channel_id=1, source_target_pairs={{64,0},{128,64},{192,128},{256,192},{320,256},{384,320},{448,384},... | collective-permute-start | bytes 958472 | tf_op jit(solution)/shard_map/ppermute | solution.py:504
  49.6 0.0 copy-done.5
  49.6 0.0 copy-done.6
  49.7 0.0 copy-done.7
  49.7 2.9 %values.1 = (f32[320,768]{1,0:T(8,128)S(1)}, f32[320,768]{1,0:T(8,128)S(1)}, f32[320,768]{1,0:T(8,128)S(1)}, f32[24,128]{1,0:T(8,128)S(1)}) custom-call(s32[320,640]{1,0:T(8,128)S(1)} %copy-done.1, f32[328,128]{1,0:T(8,128)S(1)} %collective-permute-done.from_left, f32[328,128]{1,0:T(8,128)S(1)} %collective-permute-done.1.from_right, ...), custom_call_target="tpu_custom_call" | custom-call | tf_op jit(solution)/shard_map/values/pallas_call | solution.py:210
  52.5 0.0 collective-permute-done.2.from_up
  52.5 3.5 %collective-permute-done.3.from_down = f32[104,768]{1,0:T(8,128)S(1)} collective-permute-done((f32[104,768]{1,0:T(8,128)S(1)}, f32[104,768]{1,0:T(8,128)S(1)}, u32[]{:S(2)}, u32[]{:S(2)}) %collective-permute-start.3) | collective-permute-done | bytes 319520 | tf_op jit(solution)/shard_map/ppermute | solution.py:504
  56.0 9.2 %slab.1 = (f32[320,640]{1,0:T(8,128)}, f32[64,4,128]{2,1,0:T(4,128)S(1)}) custom-call(f32[320,640]{1,0:T(8,128)S(1)} %copy-done, f32[328,128]{1,0:T(8,128)S(1)} %collective-permute-done.from_left, f32[328,128]{1,0:T(8,128)S(1)} %collective-permute-done.1.from_right, f32[104,768]{1,0:T(8,128)S(1)} %collective-permute-done.2.from_up, ...), custom_call_target="tpu_custom_call" | custom-call | tf_op jit(solution)/shard_map/slab/pallas_call | solution.py:456
  65.2 0.0 copy-start.2
  65.2 22.1 %all_to_all.10.received = f32[64,4,128]{2,1,0:T(4,128)S(1)} all-to-all(f32[64,4,128]{2,1,0:T(4,128)S(1)} %get-tuple-element.23), channel_id=1, replica_groups=mesh['grp'=8,'tile'=64] {'tile'}, dimensions={0} | all-to-all | bytes 262144 | tf_op jit(solution)/shard_map/all_to_all | solution.py:519
  87.3 0.0 copy-done.2
  87.3 1.3 %final.1 = f32[2,16,32]{2,1,0:T(8,128)} custom-call(s32[1,64]{1,0:T(1,128)S(1)} %copy-done.4, f32[64,4,128]{2,1,0:T(4,128)S(1)} %all_to_all.10.received, f32[2,16,32]{2,1,0:T(8,128)S(1)} %copy-done.2), custom_call_target="tpu_custom_call" | custom-call | tf_op jit(solution)/shard_map/final/pallas_call | solution.py:495
Async XLA Ops:
  2.1 38.2 %all-to-all-start = ((f32[64,8,128]{2,1,0:T(8,128)}), f32[64,8,128]{2,1,0:T(8,128)S(1)}, u32[]{:S(2)}, u32[]{:S(2)}) async-start(f32[64,8,128]{2,1,0:T(8,128)} %blocks.1.after), calls=%async_computation | async-start | bytes 524288 | tf_op jit(solution)/shard_map/all_to_all | solution.py:510
  21.3 19.1 %copy-start = (f32[320,640]{1,0:T(8,128)S(1)}, f32[320,640]{1,0:T(8,128)}, u32[]{:S(2)}) copy-start(f32[320,640]{1,0:T(8,128)} %level.5) | copy-start | bytes 2457604
  21.3 19.1 %copy-start.1 = (s32[320,640]{1,0:T(8,128)S(1)}, s32[320,640]{1,0:T(8,128)}, u32[]{:S(2)}) copy-start(s32[320,640]{1,0:T(8,128)} %fuel.5) | copy-start | bytes 2457604
  24.1 16.3 %copy-start.3 = (s32[4,1,1]{0,2,1:T(1,128)S(1)}, s32[4,1,1]{0,2,1:T(1,128)}, u32[]{:S(2)}) copy-start(s32[4,1,1]{0,2,1:T(1,128)} %param.12) | copy-start | bytes 52
  24.1 16.3 %copy-start.4 = (s32[1,64]{1,0:T(1,128)S(1)}, s32[1,64]{1,0:T(1,128)}, u32[]{:S(2)}) copy-start(s32[1,64]{1,0:T(1,128)} %owner.3) | copy-start | bytes 772
  24.1 11.5 %collective-permute-start = (f32[328,128]{1,0:T(8,128)}, f32[328,128]{1,0:T(8,128)S(1)}, u32[]{:S(2)}, u32[]{:S(2)}) collective-permute-start(f32[328,128]{1,0:T(8,128)} %get-tuple-element.13), channel_id=1, source_target_pairs={{0,1},{1,2},{2,3},{3,4},{4,5},{5,6},{6,7},{7,8},{8,9},{9,10},{10,1... | collective-permute-start | bytes 503816 | tf_op jit(solution)/shard_map/ppermute | solution.py:504
  27.0 10.8 %collective-permute-start.1 = (f32[328,128]{1,0:T(8,128)}, f32[328,128]{1,0:T(8,128)S(1)}, u32[]{:S(2)}, u32[]{:S(2)}) collective-permute-start(f32[328,128]{1,0:T(8,128)} %get-tuple-element.14), channel_id=1, source_target_pairs={{1,0},{2,1},{3,2},{4,3},{5,4},{6,5},{7,6},{8,7},{9,8},{10,9},{11,1... | collective-permute-start | bytes 503816 | tf_op jit(solution)/shard_map/ppermute | solution.py:504
  41.0 11.5 %collective-permute-start.2 = (f32[104,768]{1,0:T(8,128)S(1)}, f32[104,768]{1,0:T(8,128)S(1)}, u32[]{:S(2)}, u32[]{:S(2)}) collective-permute-start(f32[104,768]{1,0:T(8,128)S(1)} %get-tuple-element.15), channel_id=1, source_target_pairs={{0,64},{64,128},{128,192},{192,256},{256,320},{320,384},{384,448},... | collective-permute-start | bytes 958472 | tf_op jit(solution)/shard_map/ppermute | solution.py:504
  47.5 2.1 %copy-start.5 = (f32[13]{0:T(128)S(1)}, f32[13]{0:T(128)}, u32[]{:S(2)}) copy-start(f32[13]{0:T(128)} %fuel_rate.1) | copy-start | bytes 160
  47.6 2.1 %copy-start.6 = (f32[13]{0:T(128)S(1)}, f32[13]{0:T(128)}, u32[]{:S(2)}) copy-start(f32[13]{0:T(128)} %fuel_wind.1) | copy-start | bytes 160
  47.6 2.1 %copy-start.7 = (f32[13]{0:T(128)S(1)}, f32[13]{0:T(128)}, u32[]{:S(2)}) copy-start(f32[13]{0:T(128)} %fuel_heat.1) | copy-start | bytes 160
  47.6 8.4 %collective-permute-start.3 = (f32[104,768]{1,0:T(8,128)S(1)}, f32[104,768]{1,0:T(8,128)S(1)}, u32[]{:S(2)}, u32[]{:S(2)}) collective-permute-start(f32[104,768]{1,0:T(8,128)S(1)} %get-tuple-element.16), channel_id=1, source_target_pairs={{64,0},{128,64},{192,128},{256,192},{320,256},{384,320},{448,384},... | collective-permute-start | bytes 958472 | tf_op jit(solution)/shard_map/ppermute | solution.py:504
  65.2 22.1 %copy-start.2 = (f32[2,16,32]{2,1,0:T(8,128)S(1)}, f32[2,16,32]{2,1,0:T(8,128)}, u32[]{:S(2)}) copy-start(f32[2,16,32]{2,1,0:T(8,128)} %wind.3) | copy-start | bytes 12292

commit v7 on v6

--- a/solution.py
+++ b/solution.py
@@ -24,6 +24,9 @@
 RIGHT = 40
 LEFT = 51
 CR = 24
+BESIDE = 2 * HALO
+OWN = BESIDE + 8
+WIND = OWN + 8
 
 VM = pl.BlockSpec(memory_space=pltpu.VMEM)
 SM = pl.BlockSpec(memory_space=pltpu.SMEM)
@@ -62,13 +65,20 @@
     return jnp.where(fine < FX, own, edge)
 
 
-def strips_kernel(level, fuel, active, after, to_left, to_right, left_level, right_level, left_fuel, right_fuel, arrived):
-    first, last = pl.ds(0, 128), pl.ds(FX - 128, 128)
+def strips_kernel(
+    level, fuel, active, after, to_left, to_right, to_up, to_down, done,
+    left_level, right_level, left_fuel, right_fuel, up_fuel, down_fuel, arrived,
+):
+    first, last = (slice(None), pl.ds(0, 128)), (slice(None), pl.ds(FX - 128, 128))
+    top, bottom = (pl.ds(0, HALO), slice(None)), (pl.ds(FY - HALO, HALO), slice(None))
+    up_level, down_level = to_up.at[0:HALO, :], to_down.at[0:HALO, :]
     moves = [
-        pltpu.make_async_copy(source.at[:, part], buf, arrived.at[i])
+        pltpu.make_async_copy(source.at[part], buf, arrived.at[i])
         for i, (source, part, buf) in enumerate((
             (level, first, left_level), (fuel, first, left_fuel),
             (level, last, right_level), (fuel, last, right_fuel),
+            (level, top, up_level), (fuel, top, up_fuel),
+            (level, bottom, down_level), (fuel, bottom, down_fuel),
         ))
     ]
     for move in moves:
@@ -77,6 +87,7 @@
         row = jnp.full((1, 128), flag_of(active, k), jnp.float32)
         to_left[FY + k : FY + k + 1, :] = row
         to_right[FY + k : FY + k + 1, :] = row
+    done[...] = jnp.zeros((8, 128), jnp.float32)
     lane = lanes((FY, 128))
     moves[0].wait()
     moves[1].wait()
@@ -88,17 +99,22 @@
     to_right[0:FY, :] = jnp.where(
         lane >= HALF, right_level[...], pltpu.roll(right_fuel[...].astype(jnp.float32), HALF, 1)
     )
+    for move in moves[4:]:
+        move.wait()
+    to_up[HALO : 2 * HALO, :] = up_fuel[...].astype(jnp.float32)
+    to_down[HALO : 2 * HALO, :] = down_fuel[...].astype(jnp.float32)
 
 
 def strips(level, fuel, active, after):
     strip = pltpu.VMEM((FY, 128), jnp.float32)
     kinds = pltpu.VMEM((FY, 128), jnp.int32)
+    edge = pltpu.VMEM((HALO, FX), jnp.int32)
     return pl.pallas_call(
         strips_kernel,
         in_specs=[ANY, ANY, SM, ANY],
-        out_specs=[VM, VM],
-        out_shape=[f32(FY + 8, 128), f32(FY + 8, 128)],
-        scratch_shapes=[strip, strip, kinds, kinds, pltpu.SemaphoreType.DMA((4,))],
+        out_specs=[VM] * 5,
+        out_shape=[f32(FY + 8, 128)] * 2 + [f32(2 * HALO, FX)] * 2 + [f32(8, 128)],
+        scratch_shapes=[strip, strip, kinds, kinds, edge, edge, pltpu.SemaphoreType.DMA((8,))],
         name="strips",
     )(level, fuel, active, after)
 
@@ -120,9 +136,7 @@
     )(wind)
 
 
-def rows_kernel(
-    level, fuel, from_left, from_right, blocks, owner, active, held, to_up, to_down,
-):
+def corners_kernel(from_left, from_right, blocks, owner, active, after, held, to_up, to_down):
     tile = lax.axis_index("tile")
     lane = lanes((HALO, 128))
     lane8 = lanes((8, 128))
@@ -141,35 +155,29 @@
     for k in range(8):
         held[2 * AY + k : 2 * AY + k + 1, :] = jnp.full((1, 128), flag_of(active, k), jnp.float32)
     for out, start, coarse in ((to_up, 0, 0), (to_down, FY - HALO, AY - 3)):
-        out[0:HALO, 0:FX] = level[start : start + HALO, :]
-        out[HALO : 2 * HALO, 0:FX] = fuel[start : start + HALO, :].astype(jnp.float32)
         one = from_left[start : start + HALO, :]
         two = from_right[start : start + HALO, :]
-        out[0:HALO, FX:COLS] = jnp.where(lane < HALF, two, one)
-        out[HALO : 2 * HALO, FX:COLS] = pltpu.roll(jnp.where(lane < HALF, one, two), HALF, 1)
-        for k in range(4):
-            row = 2 * HALO + k
-            out[row : row + 1, 0:FX] = jnp.full((1, FX), flag_of(active, k), jnp.float32)
-            out[row : row + 1, FX:COLS] = jnp.where(
-                lane[0:1] < HALF, from_right[FY + k : FY + k + 1, :], from_left[FY + k : FY + k + 1, :]
-            )
-        row = 2 * HALO + 4
-        for c in range(6):
-            at = (c // 3) * AY + coarse + c % 3
-            out[row : row + 1, 128 * c : 128 * c + 128] = held[at : at + 1, :]
-        out[row + 1 : row + 4, :] = jnp.zeros((3, COLS), jnp.float32)
-
-
-def rows(level, fuel, from_left, from_right, blocks, owner, active):
-    shape = (2 * HALO + 8, COLS)
-    return pl.pallas_call(
-        rows_kernel,
-        in_specs=[VM] * 5 + [SM, SM],
+        out[0:HALO, :] = jnp.where(lane < HALF, two, one)
+        out[HALO : 2 * HALO, :] = pltpu.roll(jnp.where(lane < HALF, one, two), HALF, 1)
+        out[BESIDE : BESIDE + 8, :] = jnp.where(
+            lane8 < HALF, from_right[FY : FY + 8, :], from_left[FY : FY + 8, :]
+        )
+        out[OWN : OWN + 8, :] = held[2 * AY : 2 * AY + 8, :]
+        for comp in range(2):
+            at = comp * AY + coarse
+            out[WIND + 3 * comp : WIND + 3 * comp + 3, :] = held[at : at + 3, :]
+        out[WIND + 6 : WIND + 8, :] = jnp.zeros((2, 128), jnp.float32)
+
+
+def corners(from_left, from_right, blocks, owner, active, after):
+    return pl.pallas_call(
+        corners_kernel,
+        in_specs=[VM] * 3 + [SM, SM, ANY],
         out_specs=[VM, VM, VM],
-        out_shape=[f32(2 * AY + 8, 128), f32(*shape), f32(*shape)],
+        out_shape=[f32(2 * AY + 8, 128), f32(WIND + 8, 128), f32(WIND + 8, 128)],
         compiler_params=SMALL,
-        name="rows",
-    )(level, fuel, from_left, from_right, blocks, owner, active)
+        name="corners",
+    )(from_left, from_right, blocks, owner, active, after)
 
 
 def table(values):
@@ -184,44 +192,80 @@
     return jnp.take_along_axis(row, kinds, axis=1, mode="promise_in_bounds")
 
 
-def values_kernel(
-    fuel, from_left, from_right, after, fuel_rate, fuel_wind, fuel_heat, rate, drift, heat, three
-):
-    lane8 = lanes((8, 128))
-    tables = [(table(fuel_rate), rate), (table(fuel_wind), drift), (table(fuel_heat), heat)]
+def values_kernel(fuel, after, fuel_rate, fuel_wind, fuel_heat, rate, drift, heat, three, kinds, arrived):
+    move = pltpu.make_async_copy(fuel, kinds, arrived)
+    move.start()
+    tables = [table(fuel_rate), table(fuel_wind), table(fuel_heat)]
     for i in range(3):
-        three[8 * i : 8 * i + 8, :] = tables[i][0]
+        three[8 * i : 8 * i + 8, :] = tables[i]
+    move.wait()
 
     def own_rows(i, _):
         at = pl.multiple_of(i * 8, 8)
-        one = from_left[pl.ds(at, 8), :]
-        two = from_right[pl.ds(at, 8), :]
-        beside = pltpu.roll(jnp.where(lane8 < HALF, one, two), HALF, 1).astype(jnp.int32)
-        for c in range(NL):
-            kinds = beside if c == NL - 1 else fuel[pl.ds(at, 8), 128 * c : 128 * c + 128]
-            for row, out in tables:
-                out[pl.ds(at, 8), 128 * c : 128 * c + 128] = look(row, kinds)
+        for c in range(0, FX, 128):
+            found = kinds[pl.ds(at, 8), c : c + 128]
+            for row, out in zip(tables, (rate, drift, heat)):
+                out[pl.ds(at, 8), c : c + 128] = look(row, found)
         return 0
 
     lax.fori_loop(0, FY // 8, own_rows, 0, unroll=4)
 
 
-def values(fuel, from_left, from_right, after, *names):
+def values(fuel, after, *names):
     return pl.pallas_call(
         values_kernel,
-        in_specs=[VM, VM, VM, ANY, SM, SM, SM],
+        in_specs=[ANY, ANY, SM, SM, SM],
         out_specs=[VM] * 4,
-        out_shape=[f32(FY, COLS)] * 3 + [f32(24, 128)],
+        out_shape=[f32(FY, FX)] * 3 + [f32(24, 128)],
+        scratch_shapes=[pltpu.VMEM((FY, FX), jnp.int32), pltpu.SemaphoreType.DMA(())],
+        name="values",
+    )(fuel, after, *names)
+
+
+def sides_kernel(from_left, from_right, three, after, rate, drift, heat):
+    lane8 = lanes((8, 128))
+    tables = [three[8 * i : 8 * i + 8, :] for i in range(3)]
+
+    def own_rows(i, _):
+        at = pl.multiple_of(i * 8, 8)
+        kinds = jnp.where(lane8 < HALF, from_left[pl.ds(at, 8), :], from_right[pl.ds(at, 8), :])
+        kinds = pltpu.roll(kinds, HALF, 1).astype(jnp.int32)
+        for row, out in zip(tables, (rate, drift, heat)):
+            out[pl.ds(at, 8), :] = look(row, kinds)
+        return 0
+
+    lax.fori_loop(0, FY // 8, own_rows, 0, unroll=8)
+
+
+def sides(*args):
+    return pl.pallas_call(
+        sides_kernel,
+        in_specs=[VM, VM, VM, ANY],
+        out_specs=[VM] * 3,
+        out_shape=[f32(FY, 128)] * 3,
         compiler_params=SMALL,
-        name="values",
-    )(fuel, from_left, from_right, after, *names)
+        name="sides",
+    )(*args)
+
+
+def fuel_value(refs, at):
+    parts = [ref[pl.ds(at, 8), :] for ref in refs]
+    return parts[0] if len(parts) == 1 else jnp.concatenate(parts, axis=1)
 
 
 def slab_kernel(
-    level, from_left, from_right, from_up, from_down, held, rate, drift, heat, three,
+    level, from_left, from_right, from_up, from_down, corner_up, corner_down, held, three,
+    side_rate, side_drift, side_heat, all_rate, all_drift, all_heat,
     level_out, slots,
     phi_a, phi_b, phi_c, edge_rate, edge_drift, edge_heat, east, north, winds, gates, sums, spread, gather,
+    rate, drift, heat, arrived,
 ):
+    moves = [
+        pltpu.make_async_copy(source, buf, arrived.at[i])
+        for i, (source, buf) in enumerate(((all_rate, rate), (all_drift, drift), (all_heat, heat)))
+    ]
+    for move in moves:
+        move.start()
     group = lax.axis_index("grp")
     tile = lax.axis_index("tile")
     first_row = group == 0
@@ -234,8 +278,9 @@
     zero = jnp.zeros((PAD, COLS), jnp.float32)
     phi_a[0:PAD, :] = zero
     phi_a[ROWS - PAD : ROWS, :] = zero
-    phi_a[TOP - HALO : TOP, :] = from_up[0:HALO, :]
-    phi_a[TOP + FY : TOP + FY + HALO, :] = from_down[0:HALO, :]
+    for rows, corner, at in ((from_up, corner_up, TOP - HALO), (from_down, corner_down, TOP + FY)):
+        phi_a[at : at + HALO, 0:FX] = rows[0:HALO, :]
+        phi_a[at : at + HALO, FX:COLS] = corner[0:HALO, :]
 
     def own_rows(i, _):
         at = pl.multiple_of(i * 8, 8)
@@ -253,10 +298,11 @@
 
     def halo_rows(i, _):
         at = pl.multiple_of(i * 8, 8)
-        for source, start in ((from_up, 0), (from_down, HALO)):
+        for rows, corner, start in ((from_up, corner_up, 0), (from_down, corner_down, HALO)):
             to = pl.multiple_of(at + start, 8)
             for c in range(NL):
-                kinds = source[pl.ds(pl.multiple_of(at + HALO, 8), 8), 128 * c : 128 * c + 128]
+                source, col = (corner, 0) if c == NL - 1 else (rows, 128 * c)
+                kinds = source[pl.ds(pl.multiple_of(at + HALO, 8), 8), col : col + 128]
                 kinds = kinds.astype(jnp.int32)
                 for row, out in tables:
                     out[pl.ds(to, 8), 128 * c : 128 * c + 128] = look(row, kinds)
@@ -264,22 +310,22 @@
 
     lax.fori_loop(0, HALO // 8, halo_rows, 0, unroll=6)
 
-    gates[0:8, :] = from_up[2 * HALO : 2 * HALO + 8, :]
-    gates[16:24, :] = from_down[2 * HALO : 2 * HALO + 8, :]
     for c in range(FX // 128):
-        gates[8:16, 128 * c : 128 * c + 128] = held[2 * AY : 2 * AY + 8, :]
+        col = pl.ds(128 * c, 128)
+        gates[0:8, col] = corner_up[OWN : OWN + 8, :]
+        gates[8:16, col] = held[2 * AY : 2 * AY + 8, :]
+        gates[16:24, col] = corner_down[OWN : OWN + 8, :]
+    gates[0:8, FX:COLS] = corner_up[BESIDE : BESIDE + 8, :]
+    gates[16:24, FX:COLS] = corner_down[BESIDE : BESIDE + 8, :]
     gates[8:16, FX:COLS] = jnp.where(
         lane8 < HALF, from_right[FY : FY + 8, :], from_left[FY : FY + 8, :]
     )
 
-    row = 2 * HALO + 4
     for comp in range(2):
         base = comp * CR
-        for c in range(3):
-            at = 128 * (3 * comp + c)
-            winds[base + c : base + c + 1, :] = from_up[row : row + 1, at : at + 128]
-            below = base + 3 + AY + c
-            winds[below : below + 1, :] = from_down[row : row + 1, at : at + 128]
+        at = WIND + 3 * comp
+        winds[base : base + 3, :] = corner_up[at : at + 3, :]
+        winds[base + 3 + AY : base + 6 + AY, :] = corner_down[at : at + 3, :]
         winds[base + 3 : base + 3 + AY, :] = held[AY * comp : AY * comp + AY, :]
         winds[base + 6 + AY : base + CR, :] = jnp.zeros((CR - 6 - AY, 128), jnp.float32)
 
@@ -316,9 +362,9 @@
             new = jnp.broadcast_to(phi[:, FX - 1 : FX], (ROWS, 128))
             phi[:, FX : FX + 128] = jnp.where(lanes((ROWS, 128)) == 0, new, old)
 
-    own = (rate, drift, heat, TOP)
-    upper_edge = (edge_rate, edge_drift, edge_heat, TOP - HALO)
-    lower_edge = (edge_rate, edge_drift, edge_heat, TOP + FY - HALO)
+    own = ((rate, side_rate), (drift, side_drift), (heat, side_heat), TOP)
+    upper_edge = ((edge_rate,), (edge_drift,), (edge_heat,), TOP - HALO)
+    lower_edge = ((edge_rate,), (edge_drift,), (edge_heat,), TOP + FY - HALO)
 
     def update(phi, at, e, n, gate, fuels):
         before = phi[pl.ds(pl.multiple_of(at - 8, 8), 8), :]
@@ -340,7 +386,7 @@
         slope = square * lax.rsqrt(square)
         carry = e * jnp.where(e > 0.0, back_x, ahead_x) + n * jnp.where(n > 0.0, back_y, ahead_y)
         there = pl.multiple_of(at - fuels[3], 8)
-        change = fuels[0][pl.ds(there, 8), :] * slope + fuels[1][pl.ds(there, 8), :] * carry
+        change = fuel_value(fuels[0], there) * slope + fuel_value(fuels[1], there) * carry
         return now - gate * change
 
     def wind_row(ref, row):
@@ -390,7 +436,7 @@
                     level_out[pl.ds(pl.multiple_of(here - TOP, 8), 8), :] = new[:, 0:FX]
                 old = before[pl.ds(here, 8), :]
                 there = pl.multiple_of(here - fuels[3], 8)
-                parts.append(fuels[2][pl.ds(there, 8), :] * (jnp.tanh(old) - jnp.tanh(new)))
+                parts.append(fuel_value(fuels[2], there) * (jnp.tanh(old) - jnp.tanh(new)))
 
             band(phi, m, k, region, fuels, finish)
             low = parts[0] + parts[1] + jnp.where(sub8 < 4, parts[2], 0.0)
@@ -413,6 +459,8 @@
     phi_b[ROWS - 2 * PAD : ROWS - PAD, :] = tile_rows(phi_a, ROWS - 2 * PAD, AY + 5, 2, 0, lower_edge)
     band(phi_a, 0, 0, 0, upper_edge, store_to(phi_b))
     band(phi_a, 9, 0, 2, lower_edge, store_to(phi_b))
+    for move in moves:
+        move.wait()
     own_bands(lambda m, region, fuels: band(phi_a, m, 0, region, fuels, store_to(phi_b)))
     edges(phi_b)
     second = flux_band(phi_a, phi_b, phi_c, 1)
@@ -455,7 +503,7 @@
     edge = pltpu.VMEM((2 * HALO, COLS), jnp.float32)
     return pl.pallas_call(
         slab_kernel,
-        in_specs=[VM] * 10,
+        in_specs=[VM] * 12 + [ANY] * 3,
         out_specs=[VM, VM],
         out_shape=[f32(FY, FX), f32(NX * NZ, 4, 128)],
         scratch_shapes=[big] * 3
@@ -468,6 +516,10 @@
             pltpu.VMEM((CR, COLS), jnp.float32),
             pltpu.VMEM((128, COLS), jnp.bfloat16),
             pltpu.VMEM((COLS, 128), jnp.bfloat16),
+        ]
+        + [pltpu.VMEM((FY, FX), jnp.float32)] * 3
+        + [
+            pltpu.SemaphoreType.DMA((3,)),
         ],
         compiler_params=LARGE,
         name="slab",
@@ -508,14 +560,20 @@
     active = jnp.transpose(active, (1, 2, 0))
     mine = blocks_of(wind)
     blocks = lax.all_to_all(mine, "tile", 0, 0, tiled=True)
-    to_left, to_right = strips(level, fuel, active, mine)
+    to_left, to_right, to_up, to_down, done = strips(level, fuel, active, mine)
     from_right = shift(to_left, "tile", -1)
     from_left = shift(to_right, "tile", 1)
-    held, to_up, to_down = rows(level, fuel, from_left, from_right, blocks, owner, active)
     from_down = shift(to_up, "grp", -1)
     from_up = shift(to_down, "grp", 1)
-    coefficients = values(fuel, from_left, from_right, held, fuel_rate, fuel_wind, fuel_heat)
-    level_out, flux = slab(level, from_left, from_right, from_up, from_down, held, *coefficients)
+    *own, three = values(fuel, done, fuel_rate, fuel_wind, fuel_heat)
+    own = [pltpu.with_memory_space_constraint(value, pltpu.HBM) for value in own]
+    held, to_up, to_down = corners(from_left, from_right, blocks, owner, active, own[0])
+    corner_down = shift(to_up, "grp", -1)
+    corner_up = shift(to_down, "grp", 1)
+    beside = sides(from_left, from_right, three, held)
+    level_out, flux = slab(
+        level, from_left, from_right, from_up, from_down, corner_up, corner_down, held, three, *beside, *own
+    )
     flux = lax.all_to_all(flux, "tile", 0, 0, tiled=True)
     return (level_out, final(owner, flux, wind))
 

time: 89.7 us -> 93.7 us (1.045)
  waiting for transfers between devices: 15.5 us -> 3.06 us
  blocking collectives: 22.1 us -> 29.8 us
  starting transfers between devices: 31.9 us -> 37.2 us
  Pallas kernels: 18.4 us -> 22.1 us
    ppermute x4 -> x6, waiting for transfers between devices: 12.9 us -> 3.06 us  [shift(): return lax.ppermute(value, axis, pairs)]
    all_to_all x1, blocking collectives: 22.1 us -> 29.8 us  [shards(): flux = lax.all_to_all(flux, 'tile', 0, 0, tiled=True)]
    ppermute x4 -> x6, starting transfers between devices: 12.8 us -> 18.1 us  [shift(): return lax.ppermute(value, axis, pairs)]
    pallas_call x3 -> x4, Pallas kernels: 12.7 us -> 16.2 us  [the longest x1 9.46 us: slab(): pl.pallas_call(slab_kernel, in_specs=[VM] * 12 + [ANY] * 3, out_specs=[VM...]
    all_to_all x1, waiting for transfers between devices: 2.54 us -> 0.01 us  [shards(): blocks = lax.all_to_all(mine, 'tile', 0, 0, tiled=True)]
  transfers between devices with their start and end apart: 5 -> 7, of which waited for: 4 -> 2; matrix products, arithmetic and copies ran while one was open for 0% -> 0% of each run, Pallas kernels for 6% -> 10%
where the time goes in v7:
time: 93.7 us; the launch traced here: 93.1 us
  starting transfers between devices  37.2 us (40%)
  blocking collectives  29.8 us (32%)
  Pallas kernels  22.1 us (24%)
  waiting for transfers between devices  3.06 us (3%)
    all_to_all x1, blocking collectives, shards(): flux = lax.all_to_all(flux, 'tile', 0, 0, tiled=True)  29.8 us
    all_to_all x1, starting transfers between devices, shards(): blocks = lax.all_to_all(mine, 'tile', 0, 0, tiled=True)  19.1 us
    ppermute x6, starting transfers between devices, shift(): return lax.ppermute(value, axis, pairs)  18.1 us
    pallas_call x1, Pallas kernels, slab(): pl.pallas_call(slab_kernel, in_specs=[VM] * 12 + [ANY] * 3, out_specs=[VM...  9.46 us
    pallas_call x1, Pallas kernels, values(): pl.pallas_call(values_kernel, in_specs=[ANY, ANY, SM, SM, SM], out_specs=...  5.15 us
    ppermute x6, waiting for transfers between devices, shift(): return lax.ppermute(value, axis, pairs)  3.06 us
    pallas_call x1, Pallas kernels, strips(): pl.pallas_call(strips_kernel, in_specs=[ANY, ANY, SM, ANY], out_specs=[VM...  3.01 us
  transfers between devices with their start and end apart: 7, of which 2 were waited for; matrix products, arithmetic and copies ran while one was open for 0% of the time, Pallas kernels for 10%

profile of v7, /device:TPU:1, one launch (start us, length us, event | category | flops | bytes accessed | tf_op | source)
XLA Modules:
  0.0 93.1 jit_solution(2033913395107526936)
XLA Ops:
  0.6 1.5 %blocks.1.after = f32[64,8,128]{2,1,0:T(8,128)} custom-call(f32[2,16,32]{2,1,0:T(8,128)} %wind.3), custom_call_target="tpu_custom_call" | custom-call | tf_op jit(solution)/shard_map/blocks/pallas_call | solution.py:134
  2.1 19.1 %all-to-all-start = ((f32[64,8,128]{2,1,0:T(8,128)}), f32[64,8,128]{2,1,0:T(8,128)S(1)}, u32[]{:S(2)}, u32[]{:S(2)}) async-start(f32[64,8,128]{2,1,0:T(8,128)} %blocks.1.after), calls=%async_computation | async-start | bytes 524288 | tf_op jit(solution)/shard_map/all_to_all | solution.py:562
  21.3 3.0 %strips.1 = (f32[328,128]{1,0:T(8,128)}, f32[328,128]{1,0:T(8,128)}, f32[96,640]{1,0:T(8,128)}, f32[96,640]{1,0:T(8,128)}, f32[8,128]{1,0:T(8,128)}) custom-call(f32[320,640]{1,0:T(8,128)} %level.3, s32[320,640]{1,0:T(8,128)} %fuel.3, s32[1,1,4]{2,1,0:T(1,128)} %bitcast.1, f32[64,8,128]{2,1,0:T(8,128)} %blocks.1.after), custom_call_target="tpu_custom_call" | custom-call | tf_op jit(solution)/shard_map/strips/pallas_call | solution.py:112
  24.3 4.0 %collective-permute-start.2 = (f32[96,640]{1,0:T(8,128)}, f32[96,640]{1,0:T(8,128)S(1)}, u32[]{:S(2)}, u32[]{:S(2)}) collective-permute-start(f32[96,640]{1,0:T(8,128)} %get-tuple-element.21), channel_id=1, source_target_pairs={{0,64},{64,128},{128,192},{192,256},{256,320},{320,384},{384,448},... | collective-permute-start | bytes 737288 | tf_op jit(solution)/shard_map/ppermute | solution.py:556
  28.3 1.9 %collective-permute-start.3 = (f32[96,640]{1,0:T(8,128)}, f32[96,640]{1,0:T(8,128)S(1)}, u32[]{:S(2)}, u32[]{:S(2)}) collective-permute-start(f32[96,640]{1,0:T(8,128)} %get-tuple-element.22), channel_id=1, source_target_pairs={{64,0},{128,64},{192,128},{256,192},{320,256},{384,320},{448,384},... | collective-permute-start | bytes 737288 | tf_op jit(solution)/shard_map/ppermute | solution.py:556
  30.3 3.2 %collective-permute-start = (f32[328,128]{1,0:T(8,128)}, f32[328,128]{1,0:T(8,128)S(1)}, u32[]{:S(2)}, u32[]{:S(2)}) collective-permute-start(f32[328,128]{1,0:T(8,128)} %get-tuple-element.19), channel_id=1, source_target_pairs={{0,1},{1,2},{2,3},{3,4},{4,5},{5,6},{6,7},{7,8},{8,9},{9,10},{10,1... | collective-permute-start | bytes 503816 | tf_op jit(solution)/shard_map/ppermute | solution.py:556
  33.5 1.3 %collective-permute-start.1 = (f32[328,128]{1,0:T(8,128)}, f32[328,128]{1,0:T(8,128)S(1)}, u32[]{:S(2)}, u32[]{:S(2)}) collective-permute-start(f32[328,128]{1,0:T(8,128)} %get-tuple-element.20), channel_id=1, source_target_pairs={{1,0},{2,1},{3,2},{4,3},{5,4},{6,5},{7,6},{8,7},{9,8},{10,9},{11,1... | collective-permute-start | bytes 503816 | tf_op jit(solution)/shard_map/ppermute | solution.py:556
  34.8 5.2 %values.1 = (f32[320,640]{1,0:T(8,128)}, f32[320,640]{1,0:T(8,128)}, f32[320,640]{1,0:T(8,128)}, f32[24,128]{1,0:T(8,128)}) custom-call(s32[320,640]{1,0:T(8,128)} %fuel.3, f32[8,128]{1,0:T(8,128)} %get-tuple-element.23.after, f32[13]{0:T(128)} %fuel_rate.1, f32[13]{0:T(128)} %fuel_wind.1, f32[13]{0:T(128)} %fuel_heat.1), custom_call_target="tpu_custom_call" | custom-call | tf_op jit(solution)/shard_map/values/pallas_call | solution.py:215
  39.9 0.0 copy-start.3
  39.9 0.0 copy-start.4
  39.9 0.0 collective-permute-done.from_left
  40.0 0.4 collective-permute-done.1.from_right
  40.4 0.0 all-to-all-done.blocks
  40.4 0.2 copy-done.3
  40.6 0.0 copy-done.4
  40.6 0.0 copy-start.2
  40.6 0.0 copy-start
  40.6 0.6 corners.1
  41.2 5.7 %collective-permute-start.4 = (f32[120,128]{1,0:T(8,128)S(1)}, f32[120,128]{1,0:T(8,128)S(1)}, u32[]{:S(2)}, u32[]{:S(2)}) collective-permute-start(f32[120,128]{1,0:T(8,128)S(1)} %get-tuple-element.25), channel_id=1, source_target_pairs={{0,64},{64,128},{128,192},{192,256},{256,320},{320,384},{384,448},... | collective-permute-start | bytes 184328 | tf_op jit(solution)/shard_map/ppermute | solution.py:556
  47.0 1.9 %collective-permute-start.5 = (f32[120,128]{1,0:T(8,128)S(1)}, f32[120,128]{1,0:T(8,128)S(1)}, u32[]{:S(2)}, u32[]{:S(2)}) collective-permute-start(f32[120,128]{1,0:T(8,128)S(1)} %get-tuple-element.26), channel_id=1, source_target_pairs={{64,0},{128,64},{192,128},{256,192},{320,256},{384,320},{448,384},... | collective-permute-start | bytes 184328 | tf_op jit(solution)/shard_map/ppermute | solution.py:556
  48.9 0.0 copy-done.2
  48.9 0.9 %sides.1 = (f32[320,128]{1,0:T(8,128)S(1)}, f32[320,128]{1,0:T(8,128)S(1)}, f32[320,128]{1,0:T(8,128)S(1)}) custom-call(f32[328,128]{1,0:T(8,128)S(1)} %collective-permute-done.from_left, f32[328,128]{1,0:T(8,128)S(1)} %collective-permute-done.1.from_right, f32[24,128]{1,0:T(8,128)S(1)} %copy-done.2, f32[40,128]{1,0:T(8,128)S(1)} %get-tuple-element.27.after.held), custom_call_target="tpu_custom_call" | custom-call | tf_op jit(solution)/shard_map/sides/pallas_call | solution.py:241
  49.8 0.0 collective-permute-done.2.from_up
  49.9 0.0 collective-permute-done.3.from_down
  49.9 0.0 collective-permute-done.4.corner_up
  49.9 2.6 %collective-permute-done.5.corner_down = f32[120,128]{1,0:T(8,128)S(1)} collective-permute-done((f32[120,128]{1,0:T(8,128)S(1)}, f32[120,128]{1,0:T(8,128)S(1)}, u32[]{:S(2)}, u32[]{:S(2)}) %collective-permute-start.5) | collective-permute-done | bytes 61472 | tf_op jit(solution)/shard_map/ppermute | solution.py:556
  52.5 0.0 copy-done
  52.5 9.5 %slab.1 = (f32[320,640]{1,0:T(8,128)}, f32[64,4,128]{2,1,0:T(4,128)S(1)}) custom-call(f32[320,640]{1,0:T(8,128)S(1)} %copy-done, f32[328,128]{1,0:T(8,128)S(1)} %collective-permute-done.from_left, f32[328,128]{1,0:T(8,128)S(1)} %collective-permute-done.1.from_right, f32[96,640]{1,0:T(8,128)S(1)} %collective-permute-done.2.from_up, ...), custom_call_target="tpu_custom_call" | custom-call | tf_op jit(solution)/shard_map/slab/pallas_call | solution.py:504
  62.0 0.0 copy-start.1
  62.0 29.8 %all_to_all.10.received = f32[64,4,128]{2,1,0:T(4,128)S(1)} all-to-all(f32[64,4,128]{2,1,0:T(4,128)S(1)} %get-tuple-element.35), channel_id=1, replica_groups=mesh['grp'=8,'tile'=64] {'tile'}, dimensions={0} | all-to-all | bytes 262144 | tf_op jit(solution)/shard_map/all_to_all | solution.py:577
  91.8 0.0 copy-done.1
  91.8 1.3 %final.1 = f32[2,16,32]{2,1,0:T(8,128)} custom-call(s32[1,64]{1,0:T(1,128)S(1)} %copy-done.4, f32[64,4,128]{2,1,0:T(4,128)S(1)} %all_to_all.10.received, f32[2,16,32]{2,1,0:T(8,128)S(1)} %copy-done.1), custom_call_target="tpu_custom_call" | custom-call | tf_op jit(solution)/shard_map/final/pallas_call | solution.py:547
Async XLA Ops:
  2.1 38.2 %all-to-all-start = ((f32[64,8,128]{2,1,0:T(8,128)}), f32[64,8,128]{2,1,0:T(8,128)S(1)}, u32[]{:S(2)}, u32[]{:S(2)}) async-start(f32[64,8,128]{2,1,0:T(8,128)} %blocks.1.after), calls=%async_computation | async-start | bytes 524288 | tf_op jit(solution)/shard_map/all_to_all | solution.py:562
  24.3 25.6 %collective-permute-start.2 = (f32[96,640]{1,0:T(8,128)}, f32[96,640]{1,0:T(8,128)S(1)}, u32[]{:S(2)}, u32[]{:S(2)}) collective-permute-start(f32[96,640]{1,0:T(8,128)} %get-tuple-element.21), channel_id=1, source_target_pairs={{0,64},{64,128},{128,192},{192,256},{256,320},{320,384},{384,448},... | collective-permute-start | bytes 737288 | tf_op jit(solution)/shard_map/ppermute | solution.py:556
  28.3 21.5 %collective-permute-start.3 = (f32[96,640]{1,0:T(8,128)}, f32[96,640]{1,0:T(8,128)S(1)}, u32[]{:S(2)}, u32[]{:S(2)}) collective-permute-start(f32[96,640]{1,0:T(8,128)} %get-tuple-element.22), channel_id=1, source_target_pairs={{64,0},{128,64},{192,128},{256,192},{320,256},{384,320},{448,384},... | collective-permute-start | bytes 737288 | tf_op jit(solution)/shard_map/ppermute | solution.py:556
  30.3 9.7 %collective-permute-start = (f32[328,128]{1,0:T(8,128)}, f32[328,128]{1,0:T(8,128)S(1)}, u32[]{:S(2)}, u32[]{:S(2)}) collective-permute-start(f32[328,128]{1,0:T(8,128)} %get-tuple-element.19), channel_id=1, source_target_pairs={{0,1},{1,2},{2,3},{3,4},{4,5},{5,6},{6,7},{7,8},{8,9},{9,10},{10,1... | collective-permute-start | bytes 503816 | tf_op jit(solution)/shard_map/ppermute | solution.py:556
  33.5 6.9 %collective-permute-start.1 = (f32[328,128]{1,0:T(8,128)}, f32[328,128]{1,0:T(8,128)S(1)}, u32[]{:S(2)}, u32[]{:S(2)}) collective-permute-start(f32[328,128]{1,0:T(8,128)} %get-tuple-element.20), channel_id=1, source_target_pairs={{1,0},{2,1},{3,2},{4,3},{5,4},{6,5},{7,6},{8,7},{9,8},{10,9},{11,1... | collective-permute-start | bytes 503816 | tf_op jit(solution)/shard_map/ppermute | solution.py:556
  39.9 0.7 copy-start.3
  39.9 0.7 copy-start.4
  40.6 8.3 %copy-start.2 = (f32[24,128]{1,0:T(8,128)S(1)}, f32[24,128]{1,0:T(8,128)}, u32[]{:S(2)}) copy-start(f32[24,128]{1,0:T(8,128)} %get-tuple-element.28.three) | copy-start | bytes 36868
  40.6 11.9 %copy-start = (f32[320,640]{1,0:T(8,128)S(1)}, f32[320,640]{1,0:T(8,128)}, u32[]{:S(2)}) copy-start(f32[320,640]{1,0:T(8,128)} %level.3) | copy-start | bytes 2457604
  41.2 8.6 %collective-permute-start.4 = (f32[120,128]{1,0:T(8,128)S(1)}, f32[120,128]{1,0:T(8,128)S(1)}, u32[]{:S(2)}, u32[]{:S(2)}) collective-permute-start(f32[120,128]{1,0:T(8,128)S(1)} %get-tuple-element.25), channel_id=1, source_target_pairs={{0,64},{64,128},{128,192},{192,256},{256,320},{320,384},{384,448},... | collective-permute-start | bytes 184328 | tf_op jit(solution)/shard_map/ppermute | solution.py:556
  47.0 5.5 %collective-permute-start.5 = (f32[120,128]{1,0:T(8,128)S(1)}, f32[120,128]{1,0:T(8,128)S(1)}, u32[]{:S(2)}, u32[]{:S(2)}) collective-permute-start(f32[120,128]{1,0:T(8,128)S(1)} %get-tuple-element.26), channel_id=1, source_target_pairs={{64,0},{128,64},{192,128},{256,192},{320,256},{384,320},{448,384},... | collective-permute-start | bytes 184328 | tf_op jit(solution)/shard_map/ppermute | solution.py:556
  62.0 29.8 %copy-start.1 = (f32[2,16,32]{2,1,0:T(8,128)S(1)}, f32[2,16,32]{2,1,0:T(8,128)}, u32[]{:S(2)}) copy-start(f32[2,16,32]{2,1,0:T(8,128)} %wind.3) | copy-start | bytes 12292

commit v8 on v6

--- a/solution.py
+++ b/solution.py
@@ -110,14 +110,40 @@
 def blocks_kernel(wind, slots):
     parts = [wind[0, 0:8, :], wind[0, 8:16, :], wind[1, 0:8, :], wind[1, 8:16, :]]
     block = jnp.concatenate(parts, axis=1)
-    for k in range(NX * NZ):
+    for k in range(NX):
         slots[k] = block
 
 
 def blocks_of(wind):
     return pl.pallas_call(
-        blocks_kernel, in_specs=[VM], out_specs=VM, out_shape=f32(NX * NZ, 8, 128), name="blocks"
+        blocks_kernel, in_specs=[VM], out_specs=VM, out_shape=f32(NX, 8, 128), name="blocks"
     )(wind)
+
+
+def route_kernel(owner, blocks, slots):
+    tile = lax.axis_index("tile")
+    first = (tile // NZ) * NZ
+    inside = lanes((8, 128)) % AX
+    for k in range(NZ):
+        reader = first + k
+        main = blocks[owner[0, reader] // NZ]
+        left = blocks[owner[0, jnp.maximum(reader - 1, 0)] // NZ]
+        right = blocks[owner[0, jnp.minimum(reader + 1, NX * NZ - 1)] // NZ]
+        edges = jnp.where(inside >= AX - 3, left, jnp.where(inside < 3, right, 0.0))
+        edges = pltpu.roll(edges, 3, 1)
+        small = edges[0:2]
+        for b in range(1, 4):
+            small = small + pltpu.roll(edges[2 * b : 2 * b + 2], 8 * b, 1)
+        for b in range(4):
+            slots[5 * k + b] = main[2 * b : 2 * b + 2]
+        slots[5 * k + 4] = small
+
+
+def route(owner, blocks):
+    return pl.pallas_call(
+        route_kernel, in_specs=[SM, VM], out_specs=VM, out_shape=f32(5 * NZ, 2, 128),
+        compiler_params=SMALL, name="route"
+    )(owner, blocks)
 
 
 def rows_kernel(
@@ -126,15 +152,20 @@
     tile = lax.axis_index("tile")
     lane = lanes((HALO, 128))
     lane8 = lanes((8, 128))
-    main = blocks[owner[0, tile]]
-    left = blocks[owner[0, jnp.maximum(tile - 1, 0)]]
-    right = blocks[owner[0, jnp.minimum(tile + 1, NX * NZ - 1)]]
+    main_at = 5 * (owner[0, tile] % NZ)
+    left_at = 5 * (owner[0, jnp.maximum(tile - 1, 0)] % NZ) + 4
+    right_at = 5 * (owner[0, jnp.minimum(tile + 1, NX * NZ - 1)] % NZ) + 4
+    main = jnp.concatenate([blocks[main_at + b] for b in range(4)], axis=0)
+    left, right = (
+        jnp.concatenate([pltpu.roll(small, (128 - 8 * b) % 128, 1) for b in range(4)], axis=0)
+        for small in (blocks[left_at], blocks[right_at])
+    )
     is_left = jnp.logical_and(lane8 >= LEFT - 2, lane8 <= LEFT)
     is_right = jnp.logical_and(lane8 >= RIGHT, lane8 <= RIGHT + 2)
     for q in range(4):
         own = pltpu.roll(main, (128 - 32 * q) % 128, 1)
-        one = pltpu.roll(left, (LEFT - 31 - 32 * q) % 128, 1)
-        two = pltpu.roll(right, (RIGHT - 32 * q) % 128, 1)
+        one = pltpu.roll(left, (LEFT - 2 - 32 * (q + 1)) % 128, 1)
+        two = pltpu.roll(right, (RIGHT - 3 - 32 * q) % 128, 1)
         held[8 * q : 8 * q + 8, :] = jnp.where(
             lane8 < AX, own, jnp.where(is_left, one, jnp.where(is_right, two, 0.0))
         )
@@ -320,14 +351,16 @@
     upper_edge = (edge_rate, edge_drift, edge_heat, TOP - HALO)
     lower_edge = (edge_rate, edge_drift, edge_heat, TOP + FY - HALO)
 
-    def update(phi, at, e, n, gate, fuels):
+    def update(phi, at, e, n, gate, fuels, cols=COLS):
         before = phi[pl.ds(pl.multiple_of(at - 8, 8), 8), :]
         now = phi[pl.ds(at, 8), :]
         after = phi[pl.ds(pl.multiple_of(at + 8, 8), 8), :]
-        south = jnp.where(sub8 == 0, pltpu.roll(before, 1, 0), pltpu.roll(now, 1, 0))
-        above = jnp.where(sub8 == 7, pltpu.roll(after, 7, 0), pltpu.roll(now, 7, 0))
-        west = pltpu.roll(now, 1, 1)
-        east_cell = pltpu.roll(now, COLS - 1, 1)
+        west = pltpu.roll(now, 1, 1)[:, 0:cols]
+        east_cell = pltpu.roll(now, COLS - 1, 1)[:, 0:cols]
+        before, now, after = before[:, 0:cols], now[:, 0:cols], after[:, 0:cols]
+        e, n, gate, sub = e[:, 0:cols], n[:, 0:cols], gate[:, 0:cols], sub8[:, 0:cols]
+        south = jnp.where(sub == 0, pltpu.roll(before, 1, 0), pltpu.roll(now, 1, 0))
+        above = jnp.where(sub == 7, pltpu.roll(after, 7, 0), pltpu.roll(now, 7, 0))
         back_x = now - west
         ahead_x = east_cell - now
         back_y = now - south
@@ -340,7 +373,7 @@
         slope = square * lax.rsqrt(square)
         carry = e * jnp.where(e > 0.0, back_x, ahead_x) + n * jnp.where(n > 0.0, back_y, ahead_y)
         there = pl.multiple_of(at - fuels[3], 8)
-        change = fuels[0][pl.ds(there, 8), :] * slope + fuels[1][pl.ds(there, 8), :] * carry
+        change = fuels[0][pl.ds(there, 8), 0:cols] * slope + fuels[1][pl.ds(there, 8), 0:cols] * carry
         return now - gate * change
 
     def wind_row(ref, row):
@@ -349,7 +382,7 @@
     def mix(a, b):
         return jnp.where(sub8 < 4, a, b)
 
-    def band(phi, m, k, region, fuels, finish):
+    def band(phi, m, k, region, fuels, finish, cols=COLS):
         at = pl.multiple_of(2 * PAD + 40 * m, 8)
         gate = jnp.broadcast_to(gates[region * 8 + k : region * 8 + k + 1, :], (8, COLS))
         row = 2 * m + 1
@@ -360,7 +393,7 @@
             else:
                 e, n = (wind_row(ref, row + t // 3) for ref in (east, north))
             here = pl.multiple_of(at + 8 * t, 8)
-            finish(here, update(phi, here, e, n, gate, fuels), fuels)
+            finish(here, update(phi, here, e, n, gate, fuels, cols), fuels)
 
     def tile_rows(phi, at, row, region, k, fuels):
         gate = jnp.broadcast_to(gates[region * 8 + k : region * 8 + k + 1, :], (8, COLS))
@@ -380,6 +413,8 @@
         return finish
 
     def flux_band(before, phi, out, k):
+        cols = COLS if out is not None else FX
+
         def body(m, region, fuels):
             parts = []
 
@@ -387,16 +422,16 @@
                 if out is not None:
                     out[pl.ds(here, 8), :] = new
                 else:
-                    level_out[pl.ds(pl.multiple_of(here - TOP, 8), 8), :] = new[:, 0:FX]
-                old = before[pl.ds(here, 8), :]
+                    level_out[pl.ds(pl.multiple_of(here - TOP, 8), 8), :] = new
+                old = before[pl.ds(here, 8), 0:cols]
                 there = pl.multiple_of(here - fuels[3], 8)
-                parts.append(fuels[2][pl.ds(there, 8), :] * (jnp.tanh(old) - jnp.tanh(new)))
-
-            band(phi, m, k, region, fuels, finish)
-            low = parts[0] + parts[1] + jnp.where(sub8 < 4, parts[2], 0.0)
-            high = parts[3] + parts[4] + jnp.where(sub8 >= 4, parts[2], 0.0)
-            sums[pl.ds(2 * m + 1, 1), :] = jnp.sum(low, axis=0, keepdims=True)
-            sums[pl.ds(2 * m + 2, 1), :] = jnp.sum(high, axis=0, keepdims=True)
+                parts.append(fuels[2][pl.ds(there, 8), 0:cols] * (jnp.tanh(old) - jnp.tanh(new)))
+
+            band(phi, m, k, region, fuels, finish, cols)
+            low = parts[0] + parts[1] + jnp.where(sub8[:, 0:cols] < 4, parts[2], 0.0)
+            high = parts[3] + parts[4] + jnp.where(sub8[:, 0:cols] >= 4, parts[2], 0.0)
+            sums[pl.ds(2 * m + 1, 1), 0:cols] = jnp.sum(low, axis=0, keepdims=True)
+            sums[pl.ds(2 * m + 2, 1), 0:cols] = jnp.sum(high, axis=0, keepdims=True)
 
         return body
 
@@ -506,11 +541,15 @@
 
 def shards(level, fuel, wind, owner, active, fuel_rate, fuel_wind, fuel_heat):
     active = jnp.transpose(active, (1, 2, 0))
+    along_x = [[x * NZ + z for x in range(NX)] for z in range(NZ)]
+    along_z = [[x * NZ + z for z in range(NZ)] for x in range(NX)]
     mine = blocks_of(wind)
-    blocks = lax.all_to_all(mine, "tile", 0, 0, tiled=True)
+    blocks = lax.all_to_all(mine, "tile", 0, 0, tiled=True, axis_index_groups=along_x)
     to_left, to_right = strips(level, fuel, active, mine)
     from_right = shift(to_left, "tile", -1)
     from_left = shift(to_right, "tile", 1)
+    blocks = route(owner, blocks)
+    blocks = lax.all_to_all(blocks, "tile", 0, 0, tiled=True, axis_index_groups=along_z)
     held, to_up, to_down = rows(level, fuel, from_left, from_right, blocks, owner, active)
     from_down = shift(to_up, "grp", -1)
     from_up = shift(to_down, "grp", 1)

time: 89.7 us -> 94.5 us (1.054)
  blocking collectives: 22.1 us -> 35.7 us
  waiting for transfers between devices: 15.5 us -> 8.95 us
  starting transfers between devices: 31.9 us -> 28.3 us
  Pallas kernels: 18.4 us -> 19.7 us
    all_to_all x0 -> x1, blocking collectives: none -> 9.19 us  [shards(): lax.all_to_all(mine, 'tile', 0, 0, tiled=True, axis_index_groups=along_x)]
    all_to_all x1, blocking collectives: 22.1 us -> 26.5 us  [shards(): flux = lax.all_to_all(flux, 'tile', 0, 0, tiled=True)]
    all_to_all x1, starting transfers between devices: 19.1 us -> 14.9 us  [shards(): lax.all_to_all(blocks, 'tile', 0, 0, tiled=True, axis_index_groups=along_z)]
    ppermute x4, waiting for transfers between devices: 12.9 us -> 8.95 us  [shift(): return lax.ppermute(value, axis, pairs)]
    all_to_all x1, waiting for transfers between devices: 2.54 us -> 0.01 us  [shards(): lax.all_to_all(blocks, 'tile', 0, 0, tiled=True, axis_index_groups=along_z)]
    pallas_call x0 -> x1, Pallas kernels: none -> 1.62 us  [route(): pl.pallas_call(route_kernel, in_specs=[SM, VM], out_specs=VM, out_shape=f...]
  transfers between devices with their start and end apart: 5 -> 5, of which waited for: 4 -> 3; matrix products, arithmetic and copies ran while one was open for 0% -> 0% of each run, Pallas kernels for 6% -> 6%
where the time goes in v8:
time: 94.5 us; the launch traced here: 93.4 us
  blocking collectives  35.7 us (38%)
  starting transfers between devices  28.3 us (30%)
  Pallas kernels  19.7 us (21%)
  waiting for transfers between devices  8.95 us (9%)
    all_to_all x1, blocking collectives, shards(): flux = lax.all_to_all(flux, 'tile', 0, 0, tiled=True)  26.5 us
    all_to_all x1, starting transfers between devices, shards(): lax.all_to_all(blocks, 'tile', 0, 0, tiled=True, axis_index_groups=along_z)  14.9 us
    ppermute x4, starting transfers between devices, shift(): return lax.ppermute(value, axis, pairs)  13.3 us
    all_to_all x1, blocking collectives, shards(): lax.all_to_all(mine, 'tile', 0, 0, tiled=True, axis_index_groups=along_x)  9.19 us
    pallas_call x1, Pallas kernels, slab(): pl.pallas_call(slab_kernel, in_specs=[VM] * 10, out_specs=[VM, VM], out_s...  8.96 us
    ppermute x4, waiting for transfers between devices, shift(): return lax.ppermute(value, axis, pairs)  8.95 us
    pallas_call x1, Pallas kernels, values(): pl.pallas_call(values_kernel, in_specs=[VM, VM, VM, ANY, SM, SM, SM], out...  2.87 us
    pallas_call x1, Pallas kernels, strips(): pl.pallas_call(strips_kernel, in_specs=[ANY, ANY, SM, ANY], out_specs=[VM...  2.76 us
  transfers between devices with their start and end apart: 5, of which 3 were waited for; matrix products, arithmetic and copies ran while one was open for 0% of the time, Pallas kernels for 6%

profile of v8, /device:TPU:1, one launch (start us, length us, event | category | flops | bytes accessed | tf_op | source)
XLA Modules:
  0.0 93.4 jit_solution(8400396061996956560)
XLA Ops:
  0.6 1.4 %blocks.1.after = f32[4,8,128]{2,1,0:T(8,128)} custom-call(f32[2,16,32]{2,1,0:T(8,128)} %wind.3), custom_call_target="tpu_custom_call" | custom-call | tf_op jit(solution)/shard_map/blocks/pallas_call | solution.py:118
  2.0 0.0 copy-start.3
  2.0 9.2 %all_to_all.15.blocks = f32[4,8,128]{2,1,0:T(8,128)S(1)} all-to-all(f32[4,8,128]{2,1,0:T(8,128)} %blocks.1.after), channel_id=1, replica_groups={{0,16,32,48},{1,17,33,49},{2,18,34,50},{3,19,35,51},{4,20,36,52},{5,21,..., dimensions={0} | all-to-all | bytes 32768 | tf_op jit(solution)/shard_map/all_to_all | solution.py:547
  11.2 0.0 copy-done.3
  11.2 1.6 %route.1 = f32[80,2,128]{2,1,0:T(2,128)} custom-call(s32[1,64]{1,0:T(1,128)S(1)} %copy-done.3, f32[4,8,128]{2,1,0:T(8,128)S(1)} %all_to_all.15.blocks), custom_call_target="tpu_custom_call" | custom-call | tf_op jit(solution)/shard_map/route/pallas_call | solution.py:143
  12.8 14.9 %all-to-all-start.1 = ((f32[80,2,128]{2,1,0:T(2,128)}), f32[80,2,128]{2,1,0:T(2,128)S(1)}, u32[]{:S(2)}, u32[]{:S(2)}) async-start(f32[80,2,128]{2,1,0:T(2,128)} %route.1), calls=%async_computation.1 | async-start | bytes 163840 | tf_op jit(solution)/shard_map/all_to_all | solution.py:552
  27.8 0.0 copy-start
  27.8 0.0 copy-start.1
  27.8 2.8 %strips.1 = (f32[328,128]{1,0:T(8,128)}, f32[328,128]{1,0:T(8,128)}) custom-call(f32[320,640]{1,0:T(8,128)} %level.5, s32[320,640]{1,0:T(8,128)} %fuel.5, s32[1,1,4]{2,1,0:T(1,128)} %bitcast.1, f32[4,8,128]{2,1,0:T(8,128)} %blocks.1.after), custom_call_target="tpu_custom_call" | custom-call | tf_op jit(solution)/shard_map/strips/pallas_call | solution.py:96
  30.5 0.0 copy-start.4
  30.6 3.3 %collective-permute-start = (f32[328,128]{1,0:T(8,128)}, f32[328,128]{1,0:T(8,128)S(1)}, u32[]{:S(2)}, u32[]{:S(2)}) collective-permute-start(f32[328,128]{1,0:T(8,128)} %get-tuple-element.13), channel_id=1, source_target_pairs={{0,1},{1,2},{2,3},{3,4},{4,5},{5,6},{6,7},{7,8},{8,9},{9,10},{10,1... | collective-permute-start | bytes 503816 | tf_op jit(solution)/shard_map/ppermute | solution.py:539
  33.8 1.3 %collective-permute-start.1 = (f32[328,128]{1,0:T(8,128)}, f32[328,128]{1,0:T(8,128)S(1)}, u32[]{:S(2)}, u32[]{:S(2)}) collective-permute-start(f32[328,128]{1,0:T(8,128)} %get-tuple-element.14), channel_id=1, source_target_pairs={{1,0},{2,1},{3,2},{4,3},{5,4},{6,5},{7,6},{8,7},{9,8},{10,9},{11,1... | collective-permute-start | bytes 503816 | tf_op jit(solution)/shard_map/ppermute | solution.py:539
  35.1 2.3 %collective-permute-done.from_left = f32[328,128]{1,0:T(8,128)S(1)} collective-permute-done((f32[328,128]{1,0:T(8,128)}, f32[328,128]{1,0:T(8,128)S(1)}, u32[]{:S(2)}, u32[]{:S(2)}) %collective-permute-start) | collective-permute-done | bytes 167968 | tf_op jit(solution)/shard_map/ppermute | solution.py:539
  37.4 3.2 %collective-permute-done.1.from_right = f32[328,128]{1,0:T(8,128)S(1)} collective-permute-done((f32[328,128]{1,0:T(8,128)}, f32[328,128]{1,0:T(8,128)S(1)}, u32[]{:S(2)}, u32[]{:S(2)}) %collective-permute-start.1) | collective-permute-done | bytes 167968 | tf_op jit(solution)/shard_map/ppermute | solution.py:539
  40.6 0.0 all-to-all-done.1.blocks
  40.6 0.0 copy-done
  40.6 0.0 copy-done.1
  40.6 0.0 copy-done.4
  40.6 0.7 rows.1
  41.4 6.7 %collective-permute-start.2 = (f32[104,768]{1,0:T(8,128)S(1)}, f32[104,768]{1,0:T(8,128)S(1)}, u32[]{:S(2)}, u32[]{:S(2)}) collective-permute-start(f32[104,768]{1,0:T(8,128)S(1)} %get-tuple-element.15), channel_id=1, source_target_pairs={{0,64},{64,128},{128,192},{192,256},{256,320},{320,384},{384,448},... | collective-permute-start | bytes 958472 | tf_op jit(solution)/shard_map/ppermute | solution.py:539
  48.1 0.0 copy-start.5
  48.1 0.0 copy-start.6
  48.1 0.0 copy-start.7
  48.1 2.1 %collective-permute-start.3 = (f32[104,768]{1,0:T(8,128)S(1)}, f32[104,768]{1,0:T(8,128)S(1)}, u32[]{:S(2)}, u32[]{:S(2)}) collective-permute-start(f32[104,768]{1,0:T(8,128)S(1)} %get-tuple-element.16), channel_id=1, source_target_pairs={{64,0},{128,64},{192,128},{256,192},{320,256},{384,320},{448,384},... | collective-permute-start | bytes 958472 | tf_op jit(solution)/shard_map/ppermute | solution.py:539
  50.2 0.0 copy-done.5
  50.2 0.0 copy-done.6
  50.2 0.0 copy-done.7
  50.2 2.9 %values.1 = (f32[320,768]{1,0:T(8,128)S(1)}, f32[320,768]{1,0:T(8,128)S(1)}, f32[320,768]{1,0:T(8,128)S(1)}, f32[24,128]{1,0:T(8,128)S(1)}) custom-call(s32[320,640]{1,0:T(8,128)S(1)} %copy-done.1, f32[328,128]{1,0:T(8,128)S(1)} %collective-permute-done.from_left, f32[328,128]{1,0:T(8,128)S(1)} %collective-permute-done.1.from_right, ...), custom_call_target="tpu_custom_call" | custom-call | tf_op jit(solution)/shard_map/values/pallas_call | solution.py:241
  53.1 0.0 collective-permute-done.2.from_up
  53.1 3.5 %collective-permute-done.3.from_down = f32[104,768]{1,0:T(8,128)S(1)} collective-permute-done((f32[104,768]{1,0:T(8,128)S(1)}, f32[104,768]{1,0:T(8,128)S(1)}, u32[]{:S(2)}, u32[]{:S(2)}) %collective-permute-start.3) | collective-permute-done | bytes 319520 | tf_op jit(solution)/shard_map/ppermute | solution.py:539
  56.6 9.0 %slab.1 = (f32[320,640]{1,0:T(8,128)}, f32[64,4,128]{2,1,0:T(4,128)S(1)}) custom-call(f32[320,640]{1,0:T(8,128)S(1)} %copy-done, f32[328,128]{1,0:T(8,128)S(1)} %collective-permute-done.from_left, f32[328,128]{1,0:T(8,128)S(1)} %collective-permute-done.1.from_right, f32[104,768]{1,0:T(8,128)S(1)} %collective-permute-done.2.from_up, ...), custom_call_target="tpu_custom_call" | custom-call | tf_op jit(solution)/shard_map/slab/pallas_call | solution.py:491
  65.5 0.0 copy-start.2
  65.5 26.5 %all_to_all.16.received = f32[64,4,128]{2,1,0:T(4,128)S(1)} all-to-all(f32[64,4,128]{2,1,0:T(4,128)S(1)} %get-tuple-element.23), channel_id=1, replica_groups=mesh['grp'=8,'tile'=64] {'tile'}, dimensions={0} | all-to-all | bytes 262144 | tf_op jit(solution)/shard_map/all_to_all | solution.py:558
  92.0 0.0 copy-done.2
  92.0 1.3 %final.1 = f32[2,16,32]{2,1,0:T(8,128)} custom-call(s32[1,64]{1,0:T(1,128)S(1)} %copy-done.3, f32[64,4,128]{2,1,0:T(4,128)S(1)} %all_to_all.16.received, f32[2,16,32]{2,1,0:T(8,128)S(1)} %copy-done.2), custom_call_target="tpu_custom_call" | custom-call | tf_op jit(solution)/shard_map/final/pallas_call | solution.py:530
Async XLA Ops:
  2.0 9.2 %copy-start.3 = (s32[1,64]{1,0:T(1,128)S(1)}, s32[1,64]{1,0:T(1,128)}, u32[]{:S(2)}) copy-start(s32[1,64]{1,0:T(1,128)} %owner.5) | copy-start | bytes 772
  12.8 27.8 %all-to-all-start.1 = ((f32[80,2,128]{2,1,0:T(2,128)}), f32[80,2,128]{2,1,0:T(2,128)S(1)}, u32[]{:S(2)}, u32[]{:S(2)}) async-start(f32[80,2,128]{2,1,0:T(2,128)} %route.1), calls=%async_computation.1 | async-start | bytes 163840 | tf_op jit(solution)/shard_map/all_to_all | solution.py:552
  27.8 12.9 %copy-start = (f32[320,640]{1,0:T(8,128)S(1)}, f32[320,640]{1,0:T(8,128)}, u32[]{:S(2)}) copy-start(f32[320,640]{1,0:T(8,128)} %level.5) | copy-start | bytes 2457604
  27.8 12.9 %copy-start.1 = (s32[320,640]{1,0:T(8,128)S(1)}, s32[320,640]{1,0:T(8,128)}, u32[]{:S(2)}) copy-start(s32[320,640]{1,0:T(8,128)} %fuel.5) | copy-start | bytes 2457604
  30.5 10.1 %copy-start.4 = (s32[4,1,1]{0,2,1:T(1,128)S(1)}, s32[4,1,1]{0,2,1:T(1,128)}, u32[]{:S(2)}) copy-start(s32[4,1,1]{0,2,1:T(1,128)} %param.12) | copy-start | bytes 52
  30.6 6.9 %collective-permute-start = (f32[328,128]{1,0:T(8,128)}, f32[328,128]{1,0:T(8,128)S(1)}, u32[]{:S(2)}, u32[]{:S(2)}) collective-permute-start(f32[328,128]{1,0:T(8,128)} %get-tuple-element.13), channel_id=1, source_target_pairs={{0,1},{1,2},{2,3},{3,4},{4,5},{5,6},{6,7},{7,8},{8,9},{9,10},{10,1... | collective-permute-start | bytes 503816 | tf_op jit(solution)/shard_map/ppermute | solution.py:539
  33.8 6.8 %collective-permute-start.1 = (f32[328,128]{1,0:T(8,128)}, f32[328,128]{1,0:T(8,128)S(1)}, u32[]{:S(2)}, u32[]{:S(2)}) collective-permute-start(f32[328,128]{1,0:T(8,128)} %get-tuple-element.14), channel_id=1, source_target_pairs={{1,0},{2,1},{3,2},{4,3},{5,4},{6,5},{7,6},{8,7},{9,8},{10,9},{11,1... | collective-permute-start | bytes 503816 | tf_op jit(solution)/shard_map/ppermute | solution.py:539
  41.4 11.7 %collective-permute-start.2 = (f32[104,768]{1,0:T(8,128)S(1)}, f32[104,768]{1,0:T(8,128)S(1)}, u32[]{:S(2)}, u32[]{:S(2)}) collective-permute-start(f32[104,768]{1,0:T(8,128)S(1)} %get-tuple-element.15), channel_id=1, source_target_pairs={{0,64},{64,128},{128,192},{192,256},{256,320},{320,384},{384,448},... | collective-permute-start | bytes 958472 | tf_op jit(solution)/shard_map/ppermute | solution.py:539
  48.1 2.1 %copy-start.5 = (f32[13]{0:T(128)S(1)}, f32[13]{0:T(128)}, u32[]{:S(2)}) copy-start(f32[13]{0:T(128)} %fuel_rate.1) | copy-start | bytes 160
  48.1 2.1 %copy-start.6 = (f32[13]{0:T(128)S(1)}, f32[13]{0:T(128)}, u32[]{:S(2)}) copy-start(f32[13]{0:T(128)} %fuel_wind.1) | copy-start | bytes 160
  48.1 2.1 %copy-start.7 = (f32[13]{0:T(128)S(1)}, f32[13]{0:T(128)}, u32[]{:S(2)}) copy-start(f32[13]{0:T(128)} %fuel_heat.1) | copy-start | bytes 160
  48.1 8.4 %collective-permute-start.3 = (f32[104,768]{1,0:T(8,128)S(1)}, f32[104,768]{1,0:T(8,128)S(1)}, u32[]{:S(2)}, u32[]{:S(2)}) collective-permute-start(f32[104,768]{1,0:T(8,128)S(1)} %get-tuple-element.16), channel_id=1, source_target_pairs={{64,0},{128,64},{192,128},{256,192},{320,256},{384,320},{448,384},... | collective-permute-start | bytes 958472 | tf_op jit(solution)/shard_map/ppermute | solution.py:539
  65.5 26.5 %copy-start.2 = (f32[2,16,32]{2,1,0:T(8,128)S(1)}, f32[2,16,32]{2,1,0:T(8,128)}, u32[]{:S(2)}) copy-start(f32[2,16,32]{2,1,0:T(8,128)} %wind.3) | copy-start | bytes 12292

commit v9 on v6

--- a/solution.py
+++ b/solution.py
@@ -99,6 +99,7 @@
         out_specs=[VM, VM],
         out_shape=[f32(FY + 8, 128), f32(FY + 8, 128)],
         scratch_shapes=[strip, strip, kinds, kinds, pltpu.SemaphoreType.DMA((4,))],
+        compiler_params=SMALL,
         name="strips",
     )(level, fuel, active, after)
 
@@ -320,14 +321,16 @@
     upper_edge = (edge_rate, edge_drift, edge_heat, TOP - HALO)
     lower_edge = (edge_rate, edge_drift, edge_heat, TOP + FY - HALO)
 
-    def update(phi, at, e, n, gate, fuels):
+    def update(phi, at, e, n, gate, fuels, cols=COLS):
         before = phi[pl.ds(pl.multiple_of(at - 8, 8), 8), :]
         now = phi[pl.ds(at, 8), :]
         after = phi[pl.ds(pl.multiple_of(at + 8, 8), 8), :]
-        south = jnp.where(sub8 == 0, pltpu.roll(before, 1, 0), pltpu.roll(now, 1, 0))
-        above = jnp.where(sub8 == 7, pltpu.roll(after, 7, 0), pltpu.roll(now, 7, 0))
-        west = pltpu.roll(now, 1, 1)
-        east_cell = pltpu.roll(now, COLS - 1, 1)
+        west = pltpu.roll(now, 1, 1)[:, 0:cols]
+        east_cell = pltpu.roll(now, COLS - 1, 1)[:, 0:cols]
+        before, now, after = before[:, 0:cols], now[:, 0:cols], after[:, 0:cols]
+        e, n, gate, sub = e[:, 0:cols], n[:, 0:cols], gate[:, 0:cols], sub8[:, 0:cols]
+        south = jnp.where(sub == 0, pltpu.roll(before, 1, 0), pltpu.roll(now, 1, 0))
+        above = jnp.where(sub == 7, pltpu.roll(after, 7, 0), pltpu.roll(now, 7, 0))
         back_x = now - west
         ahead_x = east_cell - now
         back_y = now - south
@@ -340,7 +343,7 @@
         slope = square * lax.rsqrt(square)
         carry = e * jnp.where(e > 0.0, back_x, ahead_x) + n * jnp.where(n > 0.0, back_y, ahead_y)
         there = pl.multiple_of(at - fuels[3], 8)
-        change = fuels[0][pl.ds(there, 8), :] * slope + fuels[1][pl.ds(there, 8), :] * carry
+        change = fuels[0][pl.ds(there, 8), 0:cols] * slope + fuels[1][pl.ds(there, 8), 0:cols] * carry
         return now - gate * change
 
     def wind_row(ref, row):
@@ -349,7 +352,7 @@
     def mix(a, b):
         return jnp.where(sub8 < 4, a, b)
 
-    def band(phi, m, k, region, fuels, finish):
+    def band(phi, m, k, region, fuels, finish, cols=COLS):
         at = pl.multiple_of(2 * PAD + 40 * m, 8)
         gate = jnp.broadcast_to(gates[region * 8 + k : region * 8 + k + 1, :], (8, COLS))
         row = 2 * m + 1
@@ -360,7 +363,7 @@
             else:
                 e, n = (wind_row(ref, row + t // 3) for ref in (east, north))
             here = pl.multiple_of(at + 8 * t, 8)
-            finish(here, update(phi, here, e, n, gate, fuels), fuels)
+            finish(here, update(phi, here, e, n, gate, fuels, cols), fuels)
 
     def tile_rows(phi, at, row, region, k, fuels):
         gate = jnp.broadcast_to(gates[region * 8 + k : region * 8 + k + 1, :], (8, COLS))
@@ -380,6 +383,8 @@
         return finish
 
     def flux_band(before, phi, out, k):
+        cols = COLS if out is not None else FX
+
         def body(m, region, fuels):
             parts = []
 
@@ -387,16 +392,16 @@
                 if out is not None:
                     out[pl.ds(here, 8), :] = new
                 else:
-                    level_out[pl.ds(pl.multiple_of(here - TOP, 8), 8), :] = new[:, 0:FX]
-                old = before[pl.ds(here, 8), :]
+                    level_out[pl.ds(pl.multiple_of(here - TOP, 8), 8), :] = new
+                old = before[pl.ds(here, 8), 0:cols]
                 there = pl.multiple_of(here - fuels[3], 8)
-                parts.append(fuels[2][pl.ds(there, 8), :] * (jnp.tanh(old) - jnp.tanh(new)))
-
-            band(phi, m, k, region, fuels, finish)
-            low = parts[0] + parts[1] + jnp.where(sub8 < 4, parts[2], 0.0)
-            high = parts[3] + parts[4] + jnp.where(sub8 >= 4, parts[2], 0.0)
-            sums[pl.ds(2 * m + 1, 1), :] = jnp.sum(low, axis=0, keepdims=True)
-            sums[pl.ds(2 * m + 2, 1), :] = jnp.sum(high, axis=0, keepdims=True)
+                parts.append(fuels[2][pl.ds(there, 8), 0:cols] * (jnp.tanh(old) - jnp.tanh(new)))
+
+            band(phi, m, k, region, fuels, finish, cols)
+            low = parts[0] + parts[1] + jnp.where(sub8[:, 0:cols] < 4, parts[2], 0.0)
+            high = parts[3] + parts[4] + jnp.where(sub8[:, 0:cols] >= 4, parts[2], 0.0)
+            sums[pl.ds(2 * m + 1, 1), 0:cols] = jnp.sum(low, axis=0, keepdims=True)
+            sums[pl.ds(2 * m + 2, 1), 0:cols] = jnp.sum(high, axis=0, keepdims=True)
 
         return body
 
@@ -508,7 +513,8 @@
     active = jnp.transpose(active, (1, 2, 0))
     mine = blocks_of(wind)
     blocks = lax.all_to_all(mine, "tile", 0, 0, tiled=True)
-    to_left, to_right = strips(level, fuel, active, mine)
+    stay = [pltpu.with_memory_space_constraint(value, pltpu.HBM) for value in (level, fuel, active, mine)]
+    to_left, to_right = strips(*stay)
     from_right = shift(to_left, "tile", -1)
     from_left = shift(to_right, "tile", 1)
     held, to_up, to_down = rows(level, fuel, from_left, from_right, blocks, owner, active)

time: 89.7 us -> 89.4 us (level)
  Pallas kernels: 18.4 us -> 17.4 us
where the time goes in v9:
time: 89.4 us; the launch traced here: 88.4 us
  starting transfers between devices  32 us (36%)
  blocking collectives  22 us (25%)
  Pallas kernels  17.4 us (19%)
  waiting for transfers between devices  16.1 us (18%)
    all_to_all x1, blocking collectives, shards(): flux = lax.all_to_all(flux, 'tile', 0, 0, tiled=True)  22 us
    all_to_all x1, starting transfers between devices, shards(): blocks = lax.all_to_all(mine, 'tile', 0, 0, tiled=True)  19.1 us
    ppermute x4, waiting for transfers between devices, shift(): return lax.ppermute(value, axis, pairs)  13.4 us
    ppermute x4, starting transfers between devices, shift(): return lax.ppermute(value, axis, pairs)  12.9 us
    pallas_call x1, Pallas kernels, slab(): pl.pallas_call(slab_kernel, in_specs=[VM] * 10, out_specs=[VM, VM], out_s...  8.96 us
    pallas_call x1, Pallas kernels, values(): pl.pallas_call(values_kernel, in_specs=[VM, VM, VM, ANY, SM, SM, SM], out...  2.87 us
    all_to_all x1, waiting for transfers between devices, shards(): blocks = lax.all_to_all(mine, 'tile', 0, 0, tiled=True)  2.76 us
    pallas_call x1, Pallas kernels, strips(): pl.pallas_call(strips_kernel, in_specs=[ANY, ANY, SM, ANY], out_specs=[VM...  2.1 us
  transfers between devices with their start and end apart: 5, of which 4 were waited for; matrix products, arithmetic and copies ran while one was open for 0% of the time, Pallas kernels for 6%

profile of v9, /device:TPU:1, one launch (start us, length us, event | category | flops | bytes accessed | tf_op | source)
XLA Modules:
  0.0 88.4 jit_solution(13244922182732302248)
XLA Ops:
  0.6 1.5 %blocks.1.after = f32[64,8,128]{2,1,0:T(8,128)} custom-call(f32[2,16,32]{2,1,0:T(8,128)} %wind.3), custom_call_target="tpu_custom_call" | custom-call | tf_op jit(solution)/shard_map/blocks/pallas_call | solution.py:119
  2.1 19.1 %all-to-all-start = ((f32[64,8,128]{2,1,0:T(8,128)}), f32[64,8,128]{2,1,0:T(8,128)S(1)}, u32[]{:S(2)}, u32[]{:S(2)}) async-start(f32[64,8,128]{2,1,0:T(8,128)} %blocks.1.after), calls=%async_computation | async-start | bytes 524288 | tf_op jit(solution)/shard_map/all_to_all | solution.py:515
  21.3 0.0 copy-start
  21.3 0.0 copy-start.1
  21.3 2.1 %strips.1 = (f32[328,128]{1,0:T(8,128)S(1)}, f32[328,128]{1,0:T(8,128)S(1)}) custom-call(f32[320,640]{1,0:T(8,128)} %level.5, s32[320,640]{1,0:T(8,128)} %fuel.5, s32[1,1,4]{2,1,0:T(1,128)} %bitcast.1, f32[64,8,128]{2,1,0:T(8,128)} %blocks.1.after), custom_call_target="tpu_custom_call" | custom-call | tf_op jit(solution)/shard_map/strips/pallas_call | solution.py:96
  23.4 0.0 copy-start.3
  23.4 0.0 copy-start.4
  23.4 2.9 %collective-permute-start = (f32[328,128]{1,0:T(8,128)S(1)}, f32[328,128]{1,0:T(8,128)S(1)}, u32[]{:S(2)}, u32[]{:S(2)}) collective-permute-start(f32[328,128]{1,0:T(8,128)S(1)} %get-tuple-element.13), channel_id=1, source_target_pairs={{0,1},{1,2},{2,3},{3,4},{4,5},{5,6},{6,7},{7,8},{8,9},{9,10},{10,1... | collective-permute-start | bytes 503816 | tf_op jit(solution)/shard_map/ppermute | solution.py:509
  26.3 1.3 %collective-permute-start.1 = (f32[328,128]{1,0:T(8,128)S(1)}, f32[328,128]{1,0:T(8,128)S(1)}, u32[]{:S(2)}, u32[]{:S(2)}) collective-permute-start(f32[328,128]{1,0:T(8,128)S(1)} %get-tuple-element.14), channel_id=1, source_target_pairs={{1,0},{2,1},{3,2},{4,3},{5,4},{6,5},{7,6},{8,7},{9,8},{10,9},{11,1... | collective-permute-start | bytes 503816 | tf_op jit(solution)/shard_map/ppermute | solution.py:509
  27.6 8.1 %collective-permute-done.from_left = f32[328,128]{1,0:T(8,128)S(1)} collective-permute-done((f32[328,128]{1,0:T(8,128)S(1)}, f32[328,128]{1,0:T(8,128)S(1)}, u32[]{:S(2)}, u32[]{:S(2)}) %collective-permute-start) | collective-permute-done | bytes 167968 | tf_op jit(solution)/shard_map/ppermute | solution.py:509
  35.7 1.8 %collective-permute-done.1.from_right = f32[328,128]{1,0:T(8,128)S(1)} collective-permute-done((f32[328,128]{1,0:T(8,128)S(1)}, f32[328,128]{1,0:T(8,128)S(1)}, u32[]{:S(2)}, u32[]{:S(2)}) %collective-permute-start.1) | collective-permute-done | bytes 167968 | tf_op jit(solution)/shard_map/ppermute | solution.py:509
  37.5 2.8 %all-to-all-done.blocks = f32[64,8,128]{2,1,0:T(8,128)S(1)} async-done(((f32[64,8,128]{2,1,0:T(8,128)}), f32[64,8,128]{2,1,0:T(8,128)S(1)}, u32[]{:S(2)}, u32[]{:S(2)}) %all-to-all-start) | async-done | bytes 262176 | tf_op jit(solution)/shard_map/all_to_all | solution.py:515
  40.3 0.0 copy-done
  40.3 0.0 copy-done.1
  40.3 0.0 copy-done.3
  40.3 0.0 copy-done.4
  40.3 0.6 rows.1
  41.0 6.6 %collective-permute-start.2 = (f32[104,768]{1,0:T(8,128)S(1)}, f32[104,768]{1,0:T(8,128)S(1)}, u32[]{:S(2)}, u32[]{:S(2)}) collective-permute-start(f32[104,768]{1,0:T(8,128)S(1)} %get-tuple-element.15), channel_id=1, source_target_pairs={{0,64},{64,128},{128,192},{192,256},{256,320},{320,384},{384,448},... | collective-permute-start | bytes 958472 | tf_op jit(solution)/shard_map/ppermute | solution.py:509
  47.6 0.0 copy-start.5
  47.6 0.0 copy-start.6
  47.6 0.0 copy-start.7
  47.7 2.1 %collective-permute-start.3 = (f32[104,768]{1,0:T(8,128)S(1)}, f32[104,768]{1,0:T(8,128)S(1)}, u32[]{:S(2)}, u32[]{:S(2)}) collective-permute-start(f32[104,768]{1,0:T(8,128)S(1)} %get-tuple-element.16), channel_id=1, source_target_pairs={{64,0},{128,64},{192,128},{256,192},{320,256},{384,320},{448,384},... | collective-permute-start | bytes 958472 | tf_op jit(solution)/shard_map/ppermute | solution.py:509
  49.7 0.0 copy-done.5
  49.7 0.0 copy-done.6
  49.7 0.0 copy-done.7
  49.7 2.9 %values.1 = (f32[320,768]{1,0:T(8,128)S(1)}, f32[320,768]{1,0:T(8,128)S(1)}, f32[320,768]{1,0:T(8,128)S(1)}, f32[24,128]{1,0:T(8,128)S(1)}) custom-call(s32[320,640]{1,0:T(8,128)S(1)} %copy-done.1, f32[328,128]{1,0:T(8,128)S(1)} %collective-permute-done.from_left, f32[328,128]{1,0:T(8,128)S(1)} %collective-permute-done.1.from_right, ...), custom_call_target="tpu_custom_call" | custom-call | tf_op jit(solution)/shard_map/values/pallas_call | solution.py:211
  52.6 0.0 collective-permute-done.2.from_up
  52.6 3.5 %collective-permute-done.3.from_down = f32[104,768]{1,0:T(8,128)S(1)} collective-permute-done((f32[104,768]{1,0:T(8,128)S(1)}, f32[104,768]{1,0:T(8,128)S(1)}, u32[]{:S(2)}, u32[]{:S(2)}) %collective-permute-start.3) | collective-permute-done | bytes 319520 | tf_op jit(solution)/shard_map/ppermute | solution.py:509
  56.1 9.0 %slab.1 = (f32[320,640]{1,0:T(8,128)}, f32[64,4,128]{2,1,0:T(4,128)S(1)}) custom-call(f32[320,640]{1,0:T(8,128)S(1)} %copy-done, f32[328,128]{1,0:T(8,128)S(1)} %collective-permute-done.from_left, f32[328,128]{1,0:T(8,128)S(1)} %collective-permute-done.1.from_right, f32[104,768]{1,0:T(8,128)S(1)} %collective-permute-done.2.from_up, ...), custom_call_target="tpu_custom_call" | custom-call | tf_op jit(solution)/shard_map/slab/pallas_call | solution.py:461
  65.1 0.0 copy-start.2
  65.1 22.0 %all_to_all.10.received = f32[64,4,128]{2,1,0:T(4,128)S(1)} all-to-all(f32[64,4,128]{2,1,0:T(4,128)S(1)} %get-tuple-element.23), channel_id=1, replica_groups=mesh['grp'=8,'tile'=64] {'tile'}, dimensions={0} | all-to-all | bytes 262144 | tf_op jit(solution)/shard_map/all_to_all | solution.py:525
  87.1 0.0 copy-done.2
  87.1 1.3 %final.1 = f32[2,16,32]{2,1,0:T(8,128)} custom-call(s32[1,64]{1,0:T(1,128)S(1)} %copy-done.4, f32[64,4,128]{2,1,0:T(4,128)S(1)} %all_to_all.10.received, f32[2,16,32]{2,1,0:T(8,128)S(1)} %copy-done.2), custom_call_target="tpu_custom_call" | custom-call | tf_op jit(solution)/shard_map/final/pallas_call | solution.py:500
Async XLA Ops:
  2.1 38.1 %all-to-all-start = ((f32[64,8,128]{2,1,0:T(8,128)}), f32[64,8,128]{2,1,0:T(8,128)S(1)}, u32[]{:S(2)}, u32[]{:S(2)}) async-start(f32[64,8,128]{2,1,0:T(8,128)} %blocks.1.after), calls=%async_computation | async-start | bytes 524288 | tf_op jit(solution)/shard_map/all_to_all | solution.py:515
  21.3 19.0 %copy-start = (f32[320,640]{1,0:T(8,128)S(1)}, f32[320,640]{1,0:T(8,128)}, u32[]{:S(2)}) copy-start(f32[320,640]{1,0:T(8,128)} %level.5) | copy-start | bytes 2457604
  21.3 19.0 %copy-start.1 = (s32[320,640]{1,0:T(8,128)S(1)}, s32[320,640]{1,0:T(8,128)}, u32[]{:S(2)}) copy-start(s32[320,640]{1,0:T(8,128)} %fuel.5) | copy-start | bytes 2457604
  23.4 16.9 %copy-start.3 = (s32[4,1,1]{0,2,1:T(1,128)S(1)}, s32[4,1,1]{0,2,1:T(1,128)}, u32[]{:S(2)}) copy-start(s32[4,1,1]{0,2,1:T(1,128)} %param.12) | copy-start | bytes 52
  23.4 16.9 %copy-start.4 = (s32[1,64]{1,0:T(1,128)S(1)}, s32[1,64]{1,0:T(1,128)}, u32[]{:S(2)}) copy-start(s32[1,64]{1,0:T(1,128)} %owner.3) | copy-start | bytes 772
  23.4 12.3 %collective-permute-start = (f32[328,128]{1,0:T(8,128)S(1)}, f32[328,128]{1,0:T(8,128)S(1)}, u32[]{:S(2)}, u32[]{:S(2)}) collective-permute-start(f32[328,128]{1,0:T(8,128)S(1)} %get-tuple-element.13), channel_id=1, source_target_pairs={{0,1},{1,2},{2,3},{3,4},{4,5},{5,6},{6,7},{7,8},{8,9},{9,10},{10,1... | collective-permute-start | bytes 503816 | tf_op jit(solution)/shard_map/ppermute | solution.py:509
  26.3 11.2 %collective-permute-start.1 = (f32[328,128]{1,0:T(8,128)S(1)}, f32[328,128]{1,0:T(8,128)S(1)}, u32[]{:S(2)}, u32[]{:S(2)}) collective-permute-start(f32[328,128]{1,0:T(8,128)S(1)} %get-tuple-element.14), channel_id=1, source_target_pairs={{1,0},{2,1},{3,2},{4,3},{5,4},{6,5},{7,6},{8,7},{9,8},{10,9},{11,1... | collective-permute-start | bytes 503816 | tf_op jit(solution)/shard_map/ppermute | solution.py:509
  41.0 11.7 %collective-permute-start.2 = (f32[104,768]{1,0:T(8,128)S(1)}, f32[104,768]{1,0:T(8,128)S(1)}, u32[]{:S(2)}, u32[]{:S(2)}) collective-permute-start(f32[104,768]{1,0:T(8,128)S(1)} %get-tuple-element.15), channel_id=1, source_target_pairs={{0,64},{64,128},{128,192},{192,256},{256,320},{320,384},{384,448},... | collective-permute-start | bytes 958472 | tf_op jit(solution)/shard_map/ppermute | solution.py:509
  47.6 2.1 %copy-start.5 = (f32[13]{0:T(128)S(1)}, f32[13]{0:T(128)}, u32[]{:S(2)}) copy-start(f32[13]{0:T(128)} %fuel_rate.1) | copy-start | bytes 160
  47.6 2.1 %copy-start.6 = (f32[13]{0:T(128)S(1)}, f32[13]{0:T(128)}, u32[]{:S(2)}) copy-start(f32[13]{0:T(128)} %fuel_wind.1) | copy-start | bytes 160
  47.6 2.1 %copy-start.7 = (f32[13]{0:T(128)S(1)}, f32[13]{0:T(128)}, u32[]{:S(2)}) copy-start(f32[13]{0:T(128)} %fuel_heat.1) | copy-start | bytes 160
  47.7 8.4 %collective-permute-start.3 = (f32[104,768]{1,0:T(8,128)S(1)}, f32[104,768]{1,0:T(8,128)S(1)}, u32[]{:S(2)}, u32[]{:S(2)}) collective-permute-start(f32[104,768]{1,0:T(8,128)S(1)} %get-tuple-element.16), channel_id=1, source_target_pairs={{64,0},{128,64},{192,128},{256,192},{320,256},{384,320},{448,384},... | collective-permute-start | bytes 958472 | tf_op jit(solution)/shard_map/ppermute | solution.py:509
  65.1 22.0 %copy-start.2 = (f32[2,16,32]{2,1,0:T(8,128)S(1)}, f32[2,16,32]{2,1,0:T(8,128)}, u32[]{:S(2)}) copy-start(f32[2,16,32]{2,1,0:T(8,128)} %wind.3) | copy-start | bytes 12292

commit v10 on v9

--- a/solution.py
+++ b/solution.py
@@ -24,6 +24,8 @@
 RIGHT = 40
 LEFT = 51
 CR = 24
+UP_ROWS = (42, 43, 44)
+DOWN_ROWS = (5, 4, 0)
 
 VM = pl.BlockSpec(memory_space=pltpu.VMEM)
 SM = pl.BlockSpec(memory_space=pltpu.SMEM)
@@ -141,28 +143,33 @@
         )
     for k in range(8):
         held[2 * AY + k : 2 * AY + k + 1, :] = jnp.full((1, 128), flag_of(active, k), jnp.float32)
-    for out, start, coarse in ((to_up, 0, 0), (to_down, FY - HALO, AY - 3)):
-        out[0:HALO, 0:FX] = level[start : start + HALO, :]
-        out[HALO : 2 * HALO, 0:FX] = fuel[start : start + HALO, :].astype(jnp.float32)
+    for out, start, near, more, coarse, (fuel_at, wind_at, flags_at) in (
+        (to_up, 0, 0, 40, 0, UP_ROWS),
+        (to_down, FY - HALO, 8, 7, AY - 3, DOWN_ROWS),
+    ):
         one = from_left[start : start + HALO, :]
         two = from_right[start : start + HALO, :]
+        side = pltpu.roll(jnp.where(lane < HALF, one, two), HALF, 1)
+        kinds = fuel[start : start + HALO, :].astype(jnp.float32)
+        out[0:HALO, 0:FX] = level[start : start + HALO, :]
         out[0:HALO, FX:COLS] = jnp.where(lane < HALF, two, one)
-        out[HALO : 2 * HALO, FX:COLS] = pltpu.roll(jnp.where(lane < HALF, one, two), HALF, 1)
+        out[HALO : HALO + 40, 0:FX] = kinds[near : near + 40]
+        out[HALO : HALO + 40, FX:COLS] = side[near : near + 40]
+        out[fuel_at : fuel_at + 1, 0:FX] = kinds[more : more + 1]
+        out[fuel_at : fuel_at + 1, FX:COLS] = side[more : more + 1]
         for k in range(4):
-            row = 2 * HALO + k
+            row = flags_at + k
             out[row : row + 1, 0:FX] = jnp.full((1, FX), flag_of(active, k), jnp.float32)
             out[row : row + 1, FX:COLS] = jnp.where(
                 lane[0:1] < HALF, from_right[FY + k : FY + k + 1, :], from_left[FY + k : FY + k + 1, :]
             )
-        row = 2 * HALO + 4
         for c in range(6):
             at = (c // 3) * AY + coarse + c % 3
-            out[row : row + 1, 128 * c : 128 * c + 128] = held[at : at + 1, :]
-        out[row + 1 : row + 4, :] = jnp.zeros((3, COLS), jnp.float32)
+            out[wind_at : wind_at + 1, 128 * c : 128 * c + 128] = held[at : at + 1, :]
 
 
 def rows(level, fuel, from_left, from_right, blocks, owner, active):
-    shape = (2 * HALO + 8, COLS)
+    shape = (HALO + 40, COLS)
     return pl.pallas_call(
         rows_kernel,
         in_specs=[VM] * 5 + [SM, SM],
@@ -252,35 +259,38 @@
         (three[8 * i : 8 * i + 8, :], out) for i, out in enumerate((edge_rate, edge_drift, edge_heat))
     ]
 
+    def look_rows(source, to):
+        for c in range(NL):
+            kinds = source(128 * c).astype(jnp.int32)
+            for row, out in tables:
+                out[pl.ds(to, 8), 128 * c : 128 * c + 128] = look(row, kinds)
+
     def halo_rows(i, _):
-        at = pl.multiple_of(i * 8, 8)
-        for source, start in ((from_up, 0), (from_down, HALO)):
-            to = pl.multiple_of(at + start, 8)
-            for c in range(NL):
-                kinds = source[pl.ds(pl.multiple_of(at + HALO, 8), 8), 128 * c : 128 * c + 128]
-                kinds = kinds.astype(jnp.int32)
-                for row, out in tables:
-                    out[pl.ds(to, 8), 128 * c : 128 * c + 128] = look(row, kinds)
+        at = pl.multiple_of(i * 8 + HALO, 8)
+        look_rows(lambda c: from_up[pl.ds(at, 8), c : c + 128], pl.multiple_of(i * 8 + 8, 8))
+        look_rows(lambda c: from_down[pl.ds(at, 8), c : c + 128], at)
         return 0
 
-    lax.fori_loop(0, HALO // 8, halo_rows, 0, unroll=6)
-
-    gates[0:8, :] = from_up[2 * HALO : 2 * HALO + 8, :]
-    gates[16:24, :] = from_down[2 * HALO : 2 * HALO + 8, :]
+    lax.fori_loop(0, 5, halo_rows, 0, unroll=5)
+    for source, row, to in ((from_up, DOWN_ROWS[0], 0), (from_down, UP_ROWS[0], 2 * HALO - 8)):
+        look_rows(lambda c: jnp.broadcast_to(source[row : row + 1, c : c + 128], (8, 128)), to)
+
+    gates[0:4, :] = from_up[DOWN_ROWS[2] : DOWN_ROWS[2] + 4, :]
+    gates[16:20, :] = from_down[UP_ROWS[2] : UP_ROWS[2] + 4, :]
     for c in range(FX // 128):
         gates[8:16, 128 * c : 128 * c + 128] = held[2 * AY : 2 * AY + 8, :]
     gates[8:16, FX:COLS] = jnp.where(
         lane8 < HALF, from_right[FY : FY + 8, :], from_left[FY : FY + 8, :]
     )
 
-    row = 2 * HALO + 4
+    above, under = DOWN_ROWS[1], UP_ROWS[1]
     for comp in range(2):
         base = comp * CR
         for c in range(3):
             at = 128 * (3 * comp + c)
-            winds[base + c : base + c + 1, :] = from_up[row : row + 1, at : at + 128]
+            winds[base + c : base + c + 1, :] = from_up[above : above + 1, at : at + 128]
             below = base + 3 + AY + c
-            winds[below : below + 1, :] = from_down[row : row + 1, at : at + 128]
+            winds[below : below + 1, :] = from_down[under : under + 1, at : at + 128]
         winds[base + 3 : base + 3 + AY, :] = held[AY * comp : AY * comp + AY, :]
         winds[base + 6 + AY : base + CR, :] = jnp.zeros((CR - 6 - AY, 128), jnp.float32)
 

time: 89.4 us -> 88.9 us (level)
  no operation moved by 1% of the time
where the time goes in v10:
time: 88.9 us; the launch traced here: 88 us
  starting transfers between devices  32 us (36%)
  blocking collectives  22.1 us (25%)
  Pallas kernels  17.4 us (20%)
  waiting for transfers between devices  15.6 us (18%)
    all_to_all x1, blocking collectives, shards(): flux = lax.all_to_all(flux, 'tile', 0, 0, tiled=True)  22.1 us
    all_to_all x1, starting transfers between devices, shards(): blocks = lax.all_to_all(mine, 'tile', 0, 0, tiled=True)  19.1 us
    ppermute x4, starting transfers between devices, shift(): return lax.ppermute(value, axis, pairs)  12.9 us
    ppermute x4, waiting for transfers between devices, shift(): return lax.ppermute(value, axis, pairs)  12.8 us
    pallas_call x1, Pallas kernels, slab(): pl.pallas_call(slab_kernel, in_specs=[VM] * 10, out_specs=[VM, VM], out_s...  8.97 us
    pallas_call x1, Pallas kernels, values(): pl.pallas_call(values_kernel, in_specs=[VM, VM, VM, ANY, SM, SM, SM], out...  2.87 us
    all_to_all x1, waiting for transfers between devices, shards(): blocks = lax.all_to_all(mine, 'tile', 0, 0, tiled=True)  2.76 us
    pallas_call x1, Pallas kernels, strips(): pl.pallas_call(strips_kernel, in_specs=[ANY, ANY, SM, ANY], out_specs=[VM...  2.1 us
  transfers between devices with their start and end apart: 5, of which 4 were waited for; matrix products, arithmetic and copies ran while one was open for 0% of the time, Pallas kernels for 6%

profile of v10, /device:TPU:1, one launch (start us, length us, event | category | flops | bytes accessed | tf_op | source)
XLA Modules:
  0.0 88.0 jit_solution(15453359644747724234)
XLA Ops:
  0.6 1.5 %blocks.1.after = f32[64,8,128]{2,1,0:T(8,128)} custom-call(f32[2,16,32]{2,1,0:T(8,128)} %wind.3), custom_call_target="tpu_custom_call" | custom-call | tf_op jit(solution)/shard_map/blocks/pallas_call | solution.py:121
  2.1 19.1 %all-to-all-start = ((f32[64,8,128]{2,1,0:T(8,128)}), f32[64,8,128]{2,1,0:T(8,128)S(1)}, u32[]{:S(2)}, u32[]{:S(2)}) async-start(f32[64,8,128]{2,1,0:T(8,128)} %blocks.1.after), calls=%async_computation | async-start | bytes 524288 | tf_op jit(solution)/shard_map/all_to_all | solution.py:525
  21.3 0.0 copy-start
  21.3 0.0 copy-start.1
  21.3 2.1 %strips.1 = (f32[328,128]{1,0:T(8,128)S(1)}, f32[328,128]{1,0:T(8,128)S(1)}) custom-call(f32[320,640]{1,0:T(8,128)} %level.5, s32[320,640]{1,0:T(8,128)} %fuel.5, s32[1,1,4]{2,1,0:T(1,128)} %bitcast.1, f32[64,8,128]{2,1,0:T(8,128)} %blocks.1.after), custom_call_target="tpu_custom_call" | custom-call | tf_op jit(solution)/shard_map/strips/pallas_call | solution.py:98
  23.4 0.0 copy-start.3
  23.4 0.0 copy-start.4
  23.4 2.9 %collective-permute-start = (f32[328,128]{1,0:T(8,128)S(1)}, f32[328,128]{1,0:T(8,128)S(1)}, u32[]{:S(2)}, u32[]{:S(2)}) collective-permute-start(f32[328,128]{1,0:T(8,128)S(1)} %get-tuple-element.13), channel_id=1, source_target_pairs={{0,1},{1,2},{2,3},{3,4},{4,5},{5,6},{6,7},{7,8},{8,9},{9,10},{10,1... | collective-permute-start | bytes 503816 | tf_op jit(solution)/shard_map/ppermute | solution.py:519
  26.3 1.3 %collective-permute-start.1 = (f32[328,128]{1,0:T(8,128)S(1)}, f32[328,128]{1,0:T(8,128)S(1)}, u32[]{:S(2)}, u32[]{:S(2)}) collective-permute-start(f32[328,128]{1,0:T(8,128)S(1)} %get-tuple-element.14), channel_id=1, source_target_pairs={{1,0},{2,1},{3,2},{4,3},{5,4},{6,5},{7,6},{8,7},{9,8},{10,9},{11,1... | collective-permute-start | bytes 503816 | tf_op jit(solution)/shard_map/ppermute | solution.py:519
  27.6 8.1 %collective-permute-done.from_left = f32[328,128]{1,0:T(8,128)S(1)} collective-permute-done((f32[328,128]{1,0:T(8,128)S(1)}, f32[328,128]{1,0:T(8,128)S(1)}, u32[]{:S(2)}, u32[]{:S(2)}) %collective-permute-start) | collective-permute-done | bytes 167968 | tf_op jit(solution)/shard_map/ppermute | solution.py:519
  35.7 1.8 %collective-permute-done.1.from_right = f32[328,128]{1,0:T(8,128)S(1)} collective-permute-done((f32[328,128]{1,0:T(8,128)S(1)}, f32[328,128]{1,0:T(8,128)S(1)}, u32[]{:S(2)}, u32[]{:S(2)}) %collective-permute-start.1) | collective-permute-done | bytes 167968 | tf_op jit(solution)/shard_map/ppermute | solution.py:519
  37.5 2.8 %all-to-all-done.blocks = f32[64,8,128]{2,1,0:T(8,128)S(1)} async-done(((f32[64,8,128]{2,1,0:T(8,128)}), f32[64,8,128]{2,1,0:T(8,128)S(1)}, u32[]{:S(2)}, u32[]{:S(2)}) %all-to-all-start) | async-done | bytes 262176 | tf_op jit(solution)/shard_map/all_to_all | solution.py:525
  40.3 0.0 copy-done
  40.3 0.0 copy-done.1
  40.3 0.0 copy-done.3
  40.3 0.0 copy-done.4
  40.3 0.6 rows.1
  41.0 6.7 %collective-permute-start.2 = (f32[88,768]{1,0:T(8,128)S(1)}, f32[88,768]{1,0:T(8,128)S(1)}, u32[]{:S(2)}, u32[]{:S(2)}) collective-permute-start(f32[88,768]{1,0:T(8,128)S(1)} %get-tuple-element.15), channel_id=1, source_target_pairs={{0,64},{64,128},{128,192},{192,256},{256,320},{320,384},{384,448},... | collective-permute-start | bytes 811016 | tf_op jit(solution)/shard_map/ppermute | solution.py:519
  47.6 0.0 copy-start.5
  47.6 0.0 copy-start.6
  47.6 0.0 copy-start.7
  47.7 2.1 %collective-permute-start.3 = (f32[88,768]{1,0:T(8,128)S(1)}, f32[88,768]{1,0:T(8,128)S(1)}, u32[]{:S(2)}, u32[]{:S(2)}) collective-permute-start(f32[88,768]{1,0:T(8,128)S(1)} %get-tuple-element.16), channel_id=1, source_target_pairs={{64,0},{128,64},{192,128},{256,192},{320,256},{384,320},{448,384},... | collective-permute-start | bytes 811016 | tf_op jit(solution)/shard_map/ppermute | solution.py:519
  49.7 0.0 copy-done.5
  49.7 0.0 copy-done.6
  49.7 0.0 copy-done.7
  49.7 2.9 %values.1 = (f32[320,768]{1,0:T(8,128)S(1)}, f32[320,768]{1,0:T(8,128)S(1)}, f32[320,768]{1,0:T(8,128)S(1)}, f32[24,128]{1,0:T(8,128)S(1)}) custom-call(s32[320,640]{1,0:T(8,128)S(1)} %copy-done.1, f32[328,128]{1,0:T(8,128)S(1)} %collective-permute-done.from_left, f32[328,128]{1,0:T(8,128)S(1)} %collective-permute-done.1.from_right, ...), custom_call_target="tpu_custom_call" | custom-call | tf_op jit(solution)/shard_map/values/pallas_call | solution.py:218
  52.6 0.0 collective-permute-done.2.from_up
  52.6 2.9 %collective-permute-done.3.from_down = f32[88,768]{1,0:T(8,128)S(1)} collective-permute-done((f32[88,768]{1,0:T(8,128)S(1)}, f32[88,768]{1,0:T(8,128)S(1)}, u32[]{:S(2)}, u32[]{:S(2)}) %collective-permute-start.3) | collective-permute-done | bytes 270368 | tf_op jit(solution)/shard_map/ppermute | solution.py:519
  55.6 9.0 %slab.1 = (f32[320,640]{1,0:T(8,128)}, f32[64,4,128]{2,1,0:T(4,128)S(1)}) custom-call(f32[320,640]{1,0:T(8,128)S(1)} %copy-done, f32[328,128]{1,0:T(8,128)S(1)} %collective-permute-done.from_left, f32[328,128]{1,0:T(8,128)S(1)} %collective-permute-done.1.from_right, f32[88,768]{1,0:T(8,128)S(1)} %collective-permute-done.2.from_up, ...), custom_call_target="tpu_custom_call" | custom-call | tf_op jit(solution)/shard_map/slab/pallas_call | solution.py:471
  64.5 0.0 copy-start.2
  64.5 22.1 %all_to_all.10.received = f32[64,4,128]{2,1,0:T(4,128)S(1)} all-to-all(f32[64,4,128]{2,1,0:T(4,128)S(1)} %get-tuple-element.23), channel_id=1, replica_groups=mesh['grp'=8,'tile'=64] {'tile'}, dimensions={0} | all-to-all | bytes 262144 | tf_op jit(solution)/shard_map/all_to_all | solution.py:535
  86.6 0.0 copy-done.2
  86.6 1.3 %final.1 = f32[2,16,32]{2,1,0:T(8,128)} custom-call(s32[1,64]{1,0:T(1,128)S(1)} %copy-done.4, f32[64,4,128]{2,1,0:T(4,128)S(1)} %all_to_all.10.received, f32[2,16,32]{2,1,0:T(8,128)S(1)} %copy-done.2), custom_call_target="tpu_custom_call" | custom-call | tf_op jit(solution)/shard_map/final/pallas_call | solution.py:510
Async XLA Ops:
  2.1 38.1 %all-to-all-start = ((f32[64,8,128]{2,1,0:T(8,128)}), f32[64,8,128]{2,1,0:T(8,128)S(1)}, u32[]{:S(2)}, u32[]{:S(2)}) async-start(f32[64,8,128]{2,1,0:T(8,128)} %blocks.1.after), calls=%async_computation | async-start | bytes 524288 | tf_op jit(solution)/shard_map/all_to_all | solution.py:525
  21.3 19.0 %copy-start = (f32[320,640]{1,0:T(8,128)S(1)}, f32[320,640]{1,0:T(8,128)}, u32[]{:S(2)}) copy-start(f32[320,640]{1,0:T(8,128)} %level.5) | copy-start | bytes 2457604
  21.3 19.0 %copy-start.1 = (s32[320,640]{1,0:T(8,128)S(1)}, s32[320,640]{1,0:T(8,128)}, u32[]{:S(2)}) copy-start(s32[320,640]{1,0:T(8,128)} %fuel.5) | copy-start | bytes 2457604
  23.4 16.9 %copy-start.3 = (s32[4,1,1]{0,2,1:T(1,128)S(1)}, s32[4,1,1]{0,2,1:T(1,128)}, u32[]{:S(2)}) copy-start(s32[4,1,1]{0,2,1:T(1,128)} %param.12) | copy-start | bytes 52
  23.4 16.9 %copy-start.4 = (s32[1,64]{1,0:T(1,128)S(1)}, s32[1,64]{1,0:T(1,128)}, u32[]{:S(2)}) copy-start(s32[1,64]{1,0:T(1,128)} %owner.3) | copy-start | bytes 772
  23.4 12.3 %collective-permute-start = (f32[328,128]{1,0:T(8,128)S(1)}, f32[328,128]{1,0:T(8,128)S(1)}, u32[]{:S(2)}, u32[]{:S(2)}) collective-permute-start(f32[328,128]{1,0:T(8,128)S(1)} %get-tuple-element.13), channel_id=1, source_target_pairs={{0,1},{1,2},{2,3},{3,4},{4,5},{5,6},{6,7},{7,8},{8,9},{9,10},{10,1... | collective-permute-start | bytes 503816 | tf_op jit(solution)/shard_map/ppermute | solution.py:519
  26.3 11.2 %collective-permute-start.1 = (f32[328,128]{1,0:T(8,128)S(1)}, f32[328,128]{1,0:T(8,128)S(1)}, u32[]{:S(2)}, u32[]{:S(2)}) collective-permute-start(f32[328,128]{1,0:T(8,128)S(1)} %get-tuple-element.14), channel_id=1, source_target_pairs={{1,0},{2,1},{3,2},{4,3},{5,4},{6,5},{7,6},{8,7},{9,8},{10,9},{11,1... | collective-permute-start | bytes 503816 | tf_op jit(solution)/shard_map/ppermute | solution.py:519
  41.0 11.7 %collective-permute-start.2 = (f32[88,768]{1,0:T(8,128)S(1)}, f32[88,768]{1,0:T(8,128)S(1)}, u32[]{:S(2)}, u32[]{:S(2)}) collective-permute-start(f32[88,768]{1,0:T(8,128)S(1)} %get-tuple-element.15), channel_id=1, source_target_pairs={{0,64},{64,128},{128,192},{192,256},{256,320},{320,384},{384,448},... | collective-permute-start | bytes 811016 | tf_op jit(solution)/shard_map/ppermute | solution.py:519
  47.6 2.1 %copy-start.5 = (f32[13]{0:T(128)S(1)}, f32[13]{0:T(128)}, u32[]{:S(2)}) copy-start(f32[13]{0:T(128)} %fuel_rate.1) | copy-start | bytes 160
  47.6 2.1 %copy-start.6 = (f32[13]{0:T(128)S(1)}, f32[13]{0:T(128)}, u32[]{:S(2)}) copy-start(f32[13]{0:T(128)} %fuel_wind.1) | copy-start | bytes 160
  47.6 2.1 %copy-start.7 = (f32[13]{0:T(128)S(1)}, f32[13]{0:T(128)}, u32[]{:S(2)}) copy-start(f32[13]{0:T(128)} %fuel_heat.1) | copy-start | bytes 160
  47.7 7.9 %collective-permute-start.3 = (f32[88,768]{1,0:T(8,128)S(1)}, f32[88,768]{1,0:T(8,128)S(1)}, u32[]{:S(2)}, u32[]{:S(2)}) collective-permute-start(f32[88,768]{1,0:T(8,128)S(1)} %get-tuple-element.16), channel_id=1, source_target_pairs={{64,0},{128,64},{192,128},{256,192},{320,256},{384,320},{448,384},... | collective-permute-start | bytes 811016 | tf_op jit(solution)/shard_map/ppermute | solution.py:519
  64.5 22.1 %copy-start.2 = (f32[2,16,32]{2,1,0:T(8,128)S(1)}, f32[2,16,32]{2,1,0:T(8,128)}, u32[]{:S(2)}) copy-start(f32[2,16,32]{2,1,0:T(8,128)} %wind.3) | copy-start | bytes 12292

commit v11 on v10

--- a/solution.py
+++ b/solution.py
@@ -211,7 +211,7 @@
                 out[pl.ds(at, 8), 128 * c : 128 * c + 128] = look(row, kinds)
         return 0
 
-    lax.fori_loop(0, FY // 8, own_rows, 0, unroll=4)
+    lax.fori_loop(0, FY // 8, own_rows, 0, unroll=8)
 
 
 def values(fuel, from_left, from_right, after, *names):
@@ -254,7 +254,7 @@
         phi_a[pl.ds(to, 8), FX:COLS] = jnp.where(lane8 < HALF, two, one)
         return 0
 
-    lax.fori_loop(0, FY // 8, own_rows, 0, unroll=4)
+    lax.fori_loop(0, FY // 8, own_rows, 0, unroll=8)
     tables = [
         (three[8 * i : 8 * i + 8, :], out) for i, out in enumerate((edge_rate, edge_drift, edge_heat))
     ]

time: 88.9 us -> 88.9 us (level)
  no operation moved by 1% of the time
where the time goes in v11:
time: 88.9 us; the launch traced here: 87.9 us
  starting transfers between devices  32 us (36%)
  blocking collectives  22.1 us (25%)
  Pallas kernels  17.8 us (20%)
  waiting for transfers between devices  15.2 us (17%)
    all_to_all x1, blocking collectives, shards(): flux = lax.all_to_all(flux, 'tile', 0, 0, tiled=True)  22.1 us
    all_to_all x1, starting transfers between devices, shards(): blocks = lax.all_to_all(mine, 'tile', 0, 0, tiled=True)  19.1 us
    ppermute x4, starting transfers between devices, shift(): return lax.ppermute(value, axis, pairs)  12.9 us
    ppermute x4, waiting for transfers between devices, shift(): return lax.ppermute(value, axis, pairs)  12.4 us
    pallas_call x1, Pallas kernels, slab(): pl.pallas_call(slab_kernel, in_specs=[VM] * 10, out_specs=[VM, VM], out_s...  8.95 us
    pallas_call x1, Pallas kernels, values(): pl.pallas_call(values_kernel, in_specs=[VM, VM, VM, ANY, SM, SM, SM], out...  3.27 us
    all_to_all x1, waiting for transfers between devices, shards(): blocks = lax.all_to_all(mine, 'tile', 0, 0, tiled=True)  2.76 us
    pallas_call x1, Pallas kernels, strips(): pl.pallas_call(strips_kernel, in_specs=[ANY, ANY, SM, ANY], out_specs=[VM...  2.1 us
  transfers between devices with their start and end apart: 5, of which 4 were waited for; matrix products, arithmetic and copies ran while one was open for 0% of the time, Pallas kernels for 6%

profile of v11, /device:TPU:1, one launch (start us, length us, event | category | flops | bytes accessed | tf_op | source)
XLA Modules:
  0.0 87.9 jit_solution(8963777007511985470)
XLA Ops:
  0.6 1.5 %blocks.1.after = f32[64,8,128]{2,1,0:T(8,128)} custom-call(f32[2,16,32]{2,1,0:T(8,128)} %wind.3), custom_call_target="tpu_custom_call" | custom-call | tf_op jit(solution)/shard_map/blocks/pallas_call | solution.py:121
  2.1 19.1 %all-to-all-start = ((f32[64,8,128]{2,1,0:T(8,128)}), f32[64,8,128]{2,1,0:T(8,128)S(1)}, u32[]{:S(2)}, u32[]{:S(2)}) async-start(f32[64,8,128]{2,1,0:T(8,128)} %blocks.1.after), calls=%async_computation | async-start | bytes 524288 | tf_op jit(solution)/shard_map/all_to_all | solution.py:525
  21.3 0.0 copy-start
  21.3 0.0 copy-start.1
  21.3 2.1 %strips.1 = (f32[328,128]{1,0:T(8,128)S(1)}, f32[328,128]{1,0:T(8,128)S(1)}) custom-call(f32[320,640]{1,0:T(8,128)} %level.5, s32[320,640]{1,0:T(8,128)} %fuel.5, s32[1,1,4]{2,1,0:T(1,128)} %bitcast.1, f32[64,8,128]{2,1,0:T(8,128)} %blocks.1.after), custom_call_target="tpu_custom_call" | custom-call | tf_op jit(solution)/shard_map/strips/pallas_call | solution.py:98
  23.4 0.0 copy-start.3
  23.4 0.0 copy-start.4
  23.4 2.9 %collective-permute-start = (f32[328,128]{1,0:T(8,128)S(1)}, f32[328,128]{1,0:T(8,128)S(1)}, u32[]{:S(2)}, u32[]{:S(2)}) collective-permute-start(f32[328,128]{1,0:T(8,128)S(1)} %get-tuple-element.13), channel_id=1, source_target_pairs={{0,1},{1,2},{2,3},{3,4},{4,5},{5,6},{6,7},{7,8},{8,9},{9,10},{10,1... | collective-permute-start | bytes 503816 | tf_op jit(solution)/shard_map/ppermute | solution.py:519
  26.3 1.3 %collective-permute-start.1 = (f32[328,128]{1,0:T(8,128)S(1)}, f32[328,128]{1,0:T(8,128)S(1)}, u32[]{:S(2)}, u32[]{:S(2)}) collective-permute-start(f32[328,128]{1,0:T(8,128)S(1)} %get-tuple-element.14), channel_id=1, source_target_pairs={{1,0},{2,1},{3,2},{4,3},{5,4},{6,5},{7,6},{8,7},{9,8},{10,9},{11,1... | collective-permute-start | bytes 503816 | tf_op jit(solution)/shard_map/ppermute | solution.py:519
  27.6 8.1 %collective-permute-done.from_left = f32[328,128]{1,0:T(8,128)S(1)} collective-permute-done((f32[328,128]{1,0:T(8,128)S(1)}, f32[328,128]{1,0:T(8,128)S(1)}, u32[]{:S(2)}, u32[]{:S(2)}) %collective-permute-start) | collective-permute-done | bytes 167968 | tf_op jit(solution)/shard_map/ppermute | solution.py:519
  35.7 1.8 %collective-permute-done.1.from_right = f32[328,128]{1,0:T(8,128)S(1)} collective-permute-done((f32[328,128]{1,0:T(8,128)S(1)}, f32[328,128]{1,0:T(8,128)S(1)}, u32[]{:S(2)}, u32[]{:S(2)}) %collective-permute-start.1) | collective-permute-done | bytes 167968 | tf_op jit(solution)/shard_map/ppermute | solution.py:519
  37.5 2.8 %all-to-all-done.blocks = f32[64,8,128]{2,1,0:T(8,128)S(1)} async-done(((f32[64,8,128]{2,1,0:T(8,128)}), f32[64,8,128]{2,1,0:T(8,128)S(1)}, u32[]{:S(2)}, u32[]{:S(2)}) %all-to-all-start) | async-done | bytes 262176 | tf_op jit(solution)/shard_map/all_to_all | solution.py:525
  40.3 0.0 copy-done
  40.3 0.0 copy-done.1
  40.3 0.0 copy-done.3
  40.3 0.0 copy-done.4
  40.3 0.6 rows.1
  41.0 6.6 %collective-permute-start.2 = (f32[88,768]{1,0:T(8,128)S(1)}, f32[88,768]{1,0:T(8,128)S(1)}, u32[]{:S(2)}, u32[]{:S(2)}) collective-permute-start(f32[88,768]{1,0:T(8,128)S(1)} %get-tuple-element.15), channel_id=1, source_target_pairs={{0,64},{64,128},{128,192},{192,256},{256,320},{320,384},{384,448},... | collective-permute-start | bytes 811016 | tf_op jit(solution)/shard_map/ppermute | solution.py:519
  47.6 0.0 copy-start.5
  47.6 0.0 copy-start.6
  47.6 0.0 copy-start.7
  47.7 2.1 %collective-permute-start.3 = (f32[88,768]{1,0:T(8,128)S(1)}, f32[88,768]{1,0:T(8,128)S(1)}, u32[]{:S(2)}, u32[]{:S(2)}) collective-permute-start(f32[88,768]{1,0:T(8,128)S(1)} %get-tuple-element.16), channel_id=1, source_target_pairs={{64,0},{128,64},{192,128},{256,192},{320,256},{384,320},{448,384},... | collective-permute-start | bytes 811016 | tf_op jit(solution)/shard_map/ppermute | solution.py:519
  49.7 0.0 copy-done.5
  49.7 0.0 copy-done.6
  49.7 0.0 copy-done.7
  49.7 3.3 %values.1 = (f32[320,768]{1,0:T(8,128)S(1)}, f32[320,768]{1,0:T(8,128)S(1)}, f32[320,768]{1,0:T(8,128)S(1)}, f32[24,128]{1,0:T(8,128)S(1)}) custom-call(s32[320,640]{1,0:T(8,128)S(1)} %copy-done.1, f32[328,128]{1,0:T(8,128)S(1)} %collective-permute-done.from_left, f32[328,128]{1,0:T(8,128)S(1)} %collective-permute-done.1.from_right, ...), custom_call_target="tpu_custom_call" | custom-call | tf_op jit(solution)/shard_map/values/pallas_call | solution.py:218
  53.0 0.0 collective-permute-done.2.from_up
  53.0 2.5 %collective-permute-done.3.from_down = f32[88,768]{1,0:T(8,128)S(1)} collective-permute-done((f32[88,768]{1,0:T(8,128)S(1)}, f32[88,768]{1,0:T(8,128)S(1)}, u32[]{:S(2)}, u32[]{:S(2)}) %collective-permute-start.3) | collective-permute-done | bytes 270368 | tf_op jit(solution)/shard_map/ppermute | solution.py:519
  55.6 9.0 %slab.1 = (f32[320,640]{1,0:T(8,128)}, f32[64,4,128]{2,1,0:T(4,128)S(1)}) custom-call(f32[320,640]{1,0:T(8,128)S(1)} %copy-done, f32[328,128]{1,0:T(8,128)S(1)} %collective-permute-done.from_left, f32[328,128]{1,0:T(8,128)S(1)} %collective-permute-done.1.from_right, f32[88,768]{1,0:T(8,128)S(1)} %collective-permute-done.2.from_up, ...), custom_call_target="tpu_custom_call" | custom-call | tf_op jit(solution)/shard_map/slab/pallas_call | solution.py:471
  64.5 0.0 copy-start.2
  64.5 22.1 %all_to_all.10.received = f32[64,4,128]{2,1,0:T(4,128)S(1)} all-to-all(f32[64,4,128]{2,1,0:T(4,128)S(1)} %get-tuple-element.23), channel_id=1, replica_groups=mesh['grp'=8,'tile'=64] {'tile'}, dimensions={0} | all-to-all | bytes 262144 | tf_op jit(solution)/shard_map/all_to_all | solution.py:535
  86.6 0.0 copy-done.2
  86.6 1.3 %final.1 = f32[2,16,32]{2,1,0:T(8,128)} custom-call(s32[1,64]{1,0:T(1,128)S(1)} %copy-done.4, f32[64,4,128]{2,1,0:T(4,128)S(1)} %all_to_all.10.received, f32[2,16,32]{2,1,0:T(8,128)S(1)} %copy-done.2), custom_call_target="tpu_custom_call" | custom-call | tf_op jit(solution)/shard_map/final/pallas_call | solution.py:510
Async XLA Ops:
  2.1 38.1 %all-to-all-start = ((f32[64,8,128]{2,1,0:T(8,128)}), f32[64,8,128]{2,1,0:T(8,128)S(1)}, u32[]{:S(2)}, u32[]{:S(2)}) async-start(f32[64,8,128]{2,1,0:T(8,128)} %blocks.1.after), calls=%async_computation | async-start | bytes 524288 | tf_op jit(solution)/shard_map/all_to_all | solution.py:525
  21.3 19.0 %copy-start = (f32[320,640]{1,0:T(8,128)S(1)}, f32[320,640]{1,0:T(8,128)}, u32[]{:S(2)}) copy-start(f32[320,640]{1,0:T(8,128)} %level.5) | copy-start | bytes 2457604
  21.3 19.0 %copy-start.1 = (s32[320,640]{1,0:T(8,128)S(1)}, s32[320,640]{1,0:T(8,128)}, u32[]{:S(2)}) copy-start(s32[320,640]{1,0:T(8,128)} %fuel.5) | copy-start | bytes 2457604
  23.4 16.9 %copy-start.3 = (s32[4,1,1]{0,2,1:T(1,128)S(1)}, s32[4,1,1]{0,2,1:T(1,128)}, u32[]{:S(2)}) copy-start(s32[4,1,1]{0,2,1:T(1,128)} %param.12) | copy-start | bytes 52
  23.4 16.9 %copy-start.4 = (s32[1,64]{1,0:T(1,128)S(1)}, s32[1,64]{1,0:T(1,128)}, u32[]{:S(2)}) copy-start(s32[1,64]{1,0:T(1,128)} %owner.3) | copy-start | bytes 772
  23.4 12.3 %collective-permute-start = (f32[328,128]{1,0:T(8,128)S(1)}, f32[328,128]{1,0:T(8,128)S(1)}, u32[]{:S(2)}, u32[]{:S(2)}) collective-permute-start(f32[328,128]{1,0:T(8,128)S(1)} %get-tuple-element.13), channel_id=1, source_target_pairs={{0,1},{1,2},{2,3},{3,4},{4,5},{5,6},{6,7},{7,8},{8,9},{9,10},{10,1... | collective-permute-start | bytes 503816 | tf_op jit(solution)/shard_map/ppermute | solution.py:519
  26.3 11.2 %collective-permute-start.1 = (f32[328,128]{1,0:T(8,128)S(1)}, f32[328,128]{1,0:T(8,128)S(1)}, u32[]{:S(2)}, u32[]{:S(2)}) collective-permute-start(f32[328,128]{1,0:T(8,128)S(1)} %get-tuple-element.14), channel_id=1, source_target_pairs={{1,0},{2,1},{3,2},{4,3},{5,4},{6,5},{7,6},{8,7},{9,8},{10,9},{11,1... | collective-permute-start | bytes 503816 | tf_op jit(solution)/shard_map/ppermute | solution.py:519
  41.0 12.1 %collective-permute-start.2 = (f32[88,768]{1,0:T(8,128)S(1)}, f32[88,768]{1,0:T(8,128)S(1)}, u32[]{:S(2)}, u32[]{:S(2)}) collective-permute-start(f32[88,768]{1,0:T(8,128)S(1)} %get-tuple-element.15), channel_id=1, source_target_pairs={{0,64},{64,128},{128,192},{192,256},{256,320},{320,384},{384,448},... | collective-permute-start | bytes 811016 | tf_op jit(solution)/shard_map/ppermute | solution.py:519
  47.6 2.1 %copy-start.5 = (f32[13]{0:T(128)S(1)}, f32[13]{0:T(128)}, u32[]{:S(2)}) copy-start(f32[13]{0:T(128)} %fuel_rate.1) | copy-start | bytes 160
  47.6 2.1 %copy-start.6 = (f32[13]{0:T(128)S(1)}, f32[13]{0:T(128)}, u32[]{:S(2)}) copy-start(f32[13]{0:T(128)} %fuel_wind.1) | copy-start | bytes 160
  47.6 2.1 %copy-start.7 = (f32[13]{0:T(128)S(1)}, f32[13]{0:T(128)}, u32[]{:S(2)}) copy-start(f32[13]{0:T(128)} %fuel_heat.1) | copy-start | bytes 160
  47.7 7.9 %collective-permute-start.3 = (f32[88,768]{1,0:T(8,128)S(1)}, f32[88,768]{1,0:T(8,128)S(1)}, u32[]{:S(2)}, u32[]{:S(2)}) collective-permute-start(f32[88,768]{1,0:T(8,128)S(1)} %get-tuple-element.16), channel_id=1, source_target_pairs={{64,0},{128,64},{192,128},{256,192},{320,256},{384,320},{448,384},... | collective-permute-start | bytes 811016 | tf_op jit(solution)/shard_map/ppermute | solution.py:519
  64.5 22.1 %copy-start.2 = (f32[2,16,32]{2,1,0:T(8,128)S(1)}, f32[2,16,32]{2,1,0:T(8,128)}, u32[]{:S(2)}) copy-start(f32[2,16,32]{2,1,0:T(8,128)} %wind.3) | copy-start | bytes 12292
